TPU v7x, 256 devices: a whole 4x4x8 slice. The times are simulated.
256 devices in a mesh: dp: 4 (over y), graph: 64 (over z, x, core).
Axes of the slice: x: 4, y: 4, z: 8, core: 2. Of those that a mesh axis runs over, the one named last changes fastest.
Arguments:
- edge_state: bfloat16 [4, 131072, 512], P('dp', 'graph'), may hold values from -6 to 6
- cotangent: bfloat16 [4, 131072, 512], P('dp', 'graph'), may hold values from -6 to 6
- edge_count: int32 [4, 64], P('dp', 'graph'), may hold values from 1024 to 2048, as said below
- triplet_basis: bfloat16 [4, 16, 524288], P('dp', None, 'graph'), may hold values from -6 to 6
- triplet_in: int32 [4, 524288], P('dp', 'graph'), may hold values from 0 to 2047, as said below
- triplet_out: int32 [4, 524288], P('dp', 'graph'), may hold values from 0 to 2047, as said below
- down_weight: bfloat16 [512, 64], replicated, may hold values from -0.25 to 0.25
- basis_weight: bfloat16 [16, 64], replicated, may hold values from -1.5 to 1.5
- bilinear_weight: bfloat16 [64, 64], replicated, may hold values from -0.75 to 0.75
- up_weight: bfloat16 [64, 512], replicated, may hold values from -0.75 to 0.75
- first_weight: bfloat16 [512, 512], replicated, may hold values from -0.25 to 0.25
- second_weight: bfloat16 [512, 512], replicated, may hold values from -0.25 to 0.25
Outputs:
- edge_grad: bfloat16 [4, 131072, 512], P('dp', 'graph')
- down_grad: float32 [512, 64], replicated
- basis_grad: float32 [16, 64], replicated
- bilinear_grad: float32 [64, 64], replicated
- up_grad: float32 [64, 512], replicated
- first_grad: float32 [512, 512], replicated
- second_grad: float32 [512, 512], replicated
Inputs may be any that keep to these rules, and one draw needn't show every extreme that they name: `edge_count`: every entry is a multiple of 128; in every batch some shard holds all 2048 slots live. Slot s * 8192 + j * 128 + k (s and j below 64, k below 128) holds a triplet of shard s whose in-edge is row triplet_in of shard j, a live row: below edge_count[b, j]. Slot s * 8192 + t holds a triplet whose out-edge is row triplet_out of shard s, a live row: below edge_count[b, s].
All inputs are finite; a program needn't handle non-finite values.
Results may differ from a plain program's by a relative error of at most 0.0096.
Values may be sent and summed in bfloat16 or wider, within the bound.
A program may use at most 128 MiB of HBM per device.

v0:
```python
import math

import jax
import jax.numpy as jnp
from jax import lax
from jax.sharding import PartitionSpec as P

HALF = 0.7071067811865476


def silu_slope(argument):
    logistic = jax.nn.sigmoid(argument)
    return logistic * (1.0 + argument * (1.0 - logistic))


def contract(left, right, left_dim, right_dim):
    return lax.dot_general(
        left, right, (((left_dim,), (right_dim,)), ((), ())), preferred_element_type=jnp.float32
    )


def local(
    edge_state,
    cotangent,
    edge_count,
    triplet_basis,
    triplet_in,
    triplet_out,
    down_weight,
    basis_weight,
    bilinear_weight,
    up_weight,
    first_weight,
    second_weight,
):
    edge_rows = edge_state[0]
    row_count = edge_rows.shape[0]
    shards = lax.axis_size("graph")
    narrow = down_weight.shape[1]
    in_local = triplet_in[0]
    out_local = triplet_out[0]
    tri_rows = in_local.shape[0]
    slot_count = tri_rows // shards
    live_mask = (jnp.arange(row_count, dtype=jnp.int32) < edge_count[0, 0]).astype(jnp.float32)
    wanted = lax.all_to_all(
        in_local.reshape(shards, slot_count), "graph", split_axis=0, concat_axis=0, tiled=True
    ).reshape(tri_rows)
    pre_down = contract(down_weight, edge_rows, 0, 1)
    down_rows = jax.nn.silu(pre_down).astype(jnp.bfloat16)
    tri_coef = contract(basis_weight, triplet_basis[0], 0, 0)
    served = jnp.take(down_rows, wanted, axis=1).reshape(narrow, shards, slot_count)
    fetched = lax.all_to_all(served, "graph", split_axis=1, concat_axis=1, tiled=True).reshape(
        narrow, tri_rows
    )
    message = tri_coef * fetched.astype(jnp.float32)
    gathered = (
        jnp.zeros((narrow, row_count), jnp.float32)
        .at[:, out_local]
        .add(message)
        .astype(jnp.bfloat16)
    )
    mixed_rows = contract(bilinear_weight, gathered, 0, 0).astype(jnp.bfloat16)
    pre_up = contract(mixed_rows, up_weight, 0, 0)
    summed = edge_rows.astype(jnp.float32) + jax.nn.silu(pre_up)
    summed_half = summed.astype(jnp.bfloat16)
    pre_first = jnp.dot(summed_half, first_weight, preferred_element_type=jnp.float32)
    first_rows = jax.nn.silu(pre_first).astype(jnp.bfloat16)
    pre_second = jnp.dot(first_rows, second_weight, preferred_element_type=jnp.float32)
    back_top = cotangent[0].astype(jnp.float32) * live_mask[:, None] * HALF
    back_second = (back_top * silu_slope(pre_second)).astype(jnp.bfloat16)
    back_first = (contract(back_second, second_weight, 1, 1) * silu_slope(pre_first)).astype(
        jnp.bfloat16
    )
    first_grad = contract(summed_half, back_first, 0, 0)
    second_grad = contract(first_rows, back_second, 0, 0)
    back_summed = back_top + contract(back_first, first_weight, 1, 1)
    back_up = (back_summed * silu_slope(pre_up)).astype(jnp.bfloat16)
    back_mixed = contract(up_weight, back_up, 1, 1).astype(jnp.bfloat16)
    back_gathered = contract(bilinear_weight, back_mixed, 1, 0)
    back_message = jnp.take(back_gathered, out_local, axis=1)
    back_coef = (back_message * fetched.astype(jnp.float32)).astype(jnp.bfloat16)
    back_fetched = back_message * tri_coef
    returned = (
        lax.all_to_all(
            back_fetched.reshape(narrow, shards, slot_count).astype(jnp.bfloat16),
            "graph",
            split_axis=1,
            concat_axis=1,
            tiled=True,
        )
        .astype(jnp.float32)
        .reshape(narrow, tri_rows)
    )
    back_down = jnp.zeros((narrow, row_count), jnp.float32).at[:, wanted].add(returned)
    up_grad = contract(mixed_rows, back_up, 1, 0)
    bilinear_grad = contract(gathered, back_mixed, 1, 1)
    basis_grad = contract(triplet_basis[0], back_coef, 1, 1)
    back_pre = (back_down * silu_slope(pre_down)).astype(jnp.bfloat16)
    down_grad = contract(edge_rows, back_pre, 0, 1)
    edge_grad = (back_summed + contract(back_pre, down_weight, 0, 1)).astype(jnp.bfloat16)
    down_grad, basis_grad, bilinear_grad, up_grad, first_grad, second_grad = lax.psum(
        (down_grad, basis_grad, bilinear_grad, up_grad, first_grad, second_grad), ("dp", "graph")
    )
    grad_scale = 1.0 / math.sqrt(lax.axis_size("dp") * shards * row_count)
    return (
        edge_grad[None],
        down_grad * grad_scale,
        basis_grad * grad_scale,
        bilinear_grad * grad_scale,
        up_grad * grad_scale,
        first_grad * grad_scale,
        second_grad * grad_scale,
    )


def solution(mesh):
    in_specs = (
        P("dp", "graph", None),
        P("dp", "graph", None),
        P("dp", "graph"),
        P("dp", None, "graph"),
        P("dp", "graph"),
        P("dp", "graph"),
        P(),
        P(),
        P(),
        P(),
        P(),
        P(),
    )
    out_specs = (P("dp", "graph", None), P(), P(), P(), P(), P(), P())
    return jax.shard_map(local, mesh=mesh, in_specs=in_specs, out_specs=out_specs, check_vma=False)
```

profile of v0, /device:TPU:1, one launch (start us, length us, event | category | flops | bytes accessed | tf_op | source)
XLA Modules:
  0.0 557.8 jit_solution(4663164017009512426)
XLA Ops:
  7.2 0.0 copy-start
  7.2 13.1 %all-to-all-start = ((s32[64,1,128]{2,1,0:T(1,128)}), s32[64,1,128]{2,1,0:T(1,128)S(1)}, u32[]{:S(2)}, u32[]{:S(2)}) async-start(s32[64,1,128]{2,1,0:T(1,128)} %bitcast.127), calls=%async_computation | async-start | bytes 65536 | tf_op jit(solution)/shard_map/all_to_all | solution.py:45
  21.0 0.8 compare_and_fusion.1
  21.7 3.2 multiply_convert_fusion.4
  24.9 0.3 copy.35
  25.2 4.4 all-to-all-done
  29.7 24.0 %gather_fusion = bf16[8192,64]{1,0:T(8,128)(2,1)S(1)} fusion(bf16[64,2048]{0,1:T(8,128)(2,1)S(1)} %copy.35, s32[8192]{0:T(1024)S(1)} %broadcast_clamp_fusion.1), kind=kCustom, calls=%fused_computation | custom fusion | bytes 2129920 | tf_op jit(solution)/shard_map/jit(_take)/gather | solution.py:51
  53.8 1.6 copy.36
  55.4 2.4 broadcast_select_fusion
  57.7 6.1 %all-to-all-start.1 = ((bf16[64,64,128]{2,0,1:T(8,128)(2,1)}), bf16[64,64,128]{2,0,1:T(8,128)(2,1)}, u32[]{:S(2)}, u32[]{:S(2)}) async-start(bf16[64,64,128]{2,0,1:T(8,128)(2,1)} %broadcast_select_fusion), calls=%async_computation.1 | async-start | bytes 2097152 | tf_op jit(solution)/shard_map/all_to_all | solution.py:52
  63.9 0.4 fusion.25
  64.4 27.5 %all-to-all-done.1 = bf16[64,64,128]{2,0,1:T(8,128)(2,1)} async-done(((bf16[64,64,128]{2,0,1:T(8,128)(2,1)}), bf16[64,64,128]{2,0,1:T(8,128)(2,1)}, u32[]{:S(2)}, u32[]{:S(2)}) %all-to-all-start.1) | async-done | bytes 1048608 | tf_op jit(solution)/shard_map/all_to_all | solution.py:52
  91.9 2.7 fusion.6
  94.6 3.8 copy.38
  98.4 45.3 %scatter_custom_fusion = f32[64,2048]{0,1:T(8,128)} fusion(s32[8192]{0:T(1024)S(1)} %bitcast.126, f32[8192,64]{1,0:T(8,128)} %copy.38, f32[]{:T(128)} %constant.18.clone.1), kind=kCustom, calls=%fused_computation.50 | custom fusion | flops 524288 | bytes 524800 | tf_op jit(solution)/shard_map/scatter-add | solution.py:59
  143.7 0.0 copy-done.12
  143.7 1.6 convolution_convert_fusion.1
  145.3 2.9 add_convert_fusion.1
  148.2 0.0 copy-start.14
  148.2 0.0 copy-start.15
  148.2 1.9 multiply_convert_fusion.2
  150.1 0.4 copy-done.14
  150.6 0.1 copy-done.15
  150.6 2.6 fusion.3
  153.3 2.3 multiply_convert_fusion.1
  155.6 0.0 copy-done.22
  155.6 0.0 copy-start.18
  155.6 4.0 multiply_convert_fusion
  159.6 0.0 copy-done.18
  159.6 0.7 convolution_convert_fusion
  160.3 0.6 copy-done.4
  160.9 0.7 copy-done.6
  161.6 1.0 convolution_bitcast_fusion
  162.6 1.4 copy.39
  164.0 27.9 %gather_fusion.1 = f32[8192,64]{1,0:T(8,128)} fusion(f32[64,2048]{0,1:T(8,128)S(1)} %copy.39, s32[8192]{0:T(1024)S(1)} %broadcast_clamp_fusion), kind=kCustom, calls=%fused_computation.1 | custom fusion | bytes 4227072 | tf_op jit(solution)/shard_map/jit(_take)/gather | solution.py:80
  191.9 3.8 copy.40
  195.7 2.9 copy_bitcast_fusion
  198.6 6.4 %all-to-all-start.2 = ((bf16[64,64,128]{2,0,1:T(8,128)(2,1)}), bf16[64,64,128]{2,0,1:T(8,128)(2,1)S(1)}, u32[]{:S(2)}, u32[]{:S(2)}) async-start(bf16[64,64,128]{2,0,1:T(8,128)(2,1)} %copy_bitcast_fusion), calls=%async_computation.2 | async-start | bytes 2097152 | tf_op jit(solution)/shard_map/all_to_all | solution.py:84
  205.0 0.3 all-reduce.4.cloned.1.call-start
  205.3 0.0 copy-start.21
  205.3 1.1 fusion.31
  206.5 0.5 copy-done.21
  206.9 4.0 fusion.33
  210.9 2.3 fusion.32
  213.2 20.0 %all-to-all-done.2 = bf16[64,64,128]{2,0,1:T(8,128)(2,1)S(1)} async-done(((bf16[64,64,128]{2,0,1:T(8,128)(2,1)}), bf16[64,64,128]{2,0,1:T(8,128)(2,1)S(1)}, u32[]{:S(2)}, u32[]{:S(2)}) %all-to-all-start.2) | async-done | bytes 1048608 | tf_op jit(solution)/shard_map/all_to_all | solution.py:84
  233.2 0.1 bitcast_bitcast_fusion
  233.3 2.8 copy.43
  236.1 44.6 %scatter_custom_fusion.1 = f32[64,2048]{0,1:T(8,128)S(1)} fusion(s32[8192]{0:T(1024)S(1)} %bitcast.124, f32[8192,64]{1,0:T(8,128)} %copy.43, f32[]{:T(128)} %constant.18.clone.1), kind=kCustom, calls=%fused_computation.48 | custom fusion | flops 524288 | bytes 524800 | tf_op jit(solution)/shard_map/scatter-add | solution.py:94
  280.7 0.3 copy.44
  281.1 0.2 multiply_convert_fusion.3
  281.3 0.0 copy-start.2
  281.3 2.8 fusion.13
  284.1 0.0 all-reduce.4.cloned.1.call-update
  284.1 1.4 fusion.27
  285.5 0.2 copy-done.3
  285.8 1.7 convolution_bitcast_fusion.1
  287.5 77.2 %all-reduce = (f32[16,64]{1,0:T(8,128)S(1)}, f32[64,64]{1,0:T(8,128)S(1)}) all-reduce(f32[16,64]{1,0:T(8,128)S(1)} %convolution_bitcast_fusion.1, f32[64,64]{1,0:T(8,128)S(1)} %fusion.27), channel_id=1, replica_groups=mesh['dp'=4,'graph'=64] {'dp','graph'}, use_global_device_ids=true, to_apply=%region_3.4 | all-reduce | flops 5120 | bytes 40960 | tf_op jit(solution)/shard_map/psum | solution.py:101
  364.6 0.6 broadcast_multiply_fusion.5
  365.2 0.6 broadcast_multiply_fusion.4
  365.9 4.3 fusion.4
  370.1 174.6 %all-reduce.4.cloned.1.call-done = (f32[512,64]{0,1:T(8,128)}, f32[64,512]{1,0:T(8,128)}, f32[512,512]{1,0:T(8,128)}, f32[512,512]{1,0:T(8,128)}) async-done(((f32[512,64]{0,1:T(8,128)}, f32[64,512]{1,0:T(8,128)}, f32[512,512]{1,0:T(8,128)}, f32[512,512]{1,0:T(8,128)}), (f32[512,64]{0,1:T(8,128)}, f32[64,512]{1,0:T(8,128)}, f32[512,512]{1,0:T(8,128)}, f32[512,512]{1,0:T(8,128)})) %all-reduce.4.cloned.1.call-update) | async-done | bytes 2359312 | tf_op jit(solution)/shard_map/psum | solution.py:101
  544.7 1.6 broadcast_multiply_fusion.3
  546.3 1.6 broadcast_multiply_fusion.2
  547.8 3.2 broadcast_multiply_fusion
  (38 shorter events, 0.2 us)
Async XLA Ops:
  7.2 141.0 %copy-start = (bf16[512,512]{1,0:T(8,128)(2,1)S(1)}, bf16[512,512]{1,0:T(8,128)(2,1)}, u32[]{:S(2)}) copy-start(bf16[512,512]{1,0:T(8,128)(2,1)} %param.22) | copy-start | bytes 1572868
  7.2 22.5 %all-to-all-start = ((s32[64,1,128]{2,1,0:T(1,128)}), s32[64,1,128]{2,1,0:T(1,128)S(1)}, u32[]{:S(2)}, u32[]{:S(2)}) async-start(s32[64,1,128]{2,1,0:T(1,128)} %bitcast.127), calls=%async_computation | async-start | bytes 65536 | tf_op jit(solution)/shard_map/all_to_all | solution.py:45
  55.4 8.5 %copy-start.8 = (s32[1,8192]{1,0:T(1,128)S(1)}, s32[1,8192]{1,0:T(1,128)}, u32[]{:S(2)}) copy-start(s32[1,8192]{1,0:T(1,128)} %param.17) | copy-start | bytes 98308
  55.4 8.5 %copy-start.9 = (bf16[1,16,8192]{2,1,0:T(8,128)(2,1)S(1)}, bf16[1,16,8192]{2,1,0:T(8,128)(2,1)}, u32[]{:S(2)}) copy-start(bf16[1,16,8192]{2,1,0:T(8,128)(2,1)} %param.15) | copy-start | bytes 786436
  55.4 8.5 %copy-start.13 = (bf16[16,64]{1,0:T(8,128)(2,1)S(1)}, bf16[16,64]{1,0:T(8,128)(2,1)}, u32[]{:S(2)}) copy-start(bf16[16,64]{1,0:T(8,128)(2,1)} %param.19) | copy-start | bytes 6148
  57.7 34.2 %all-to-all-start.1 = ((bf16[64,64,128]{2,0,1:T(8,128)(2,1)}), bf16[64,64,128]{2,0,1:T(8,128)(2,1)}, u32[]{:S(2)}, u32[]{:S(2)}) async-start(bf16[64,64,128]{2,0,1:T(8,128)(2,1)} %broadcast_select_fusion), calls=%async_computation.1 | async-start | bytes 2097152 | tf_op jit(solution)/shard_map/all_to_all | solution.py:52
  94.6 49.1 %copy-start.12 = (bf16[64,64]{1,0:T(8,128)(2,1)S(1)}, bf16[64,64]{1,0:T(8,128)(2,1)}, u32[]{:S(2)}) copy-start(bf16[64,64]{1,0:T(8,128)(2,1)} %param.20) | copy-start | bytes 24580
  98.4 46.9 %copy-start.11 = (bf16[64,512]{1,0:T(8,128)(2,1)S(1)}, bf16[64,512]{1,0:T(8,128)(2,1)}, u32[]{:S(2)}) copy-start(bf16[64,512]{1,0:T(8,128)(2,1)} %param.21) | copy-start | bytes 196612
  148.2 1.9 copy-start.16
  148.2 2.3 copy-start.14
  148.2 2.4 copy-start.15
  150.1 3.2 copy-start.20
  153.3 2.3 copy-start.22
  155.6 4.0 copy-start.18
  159.6 1.3 copy-start.4
  160.9 0.7 copy-start.6
  198.6 6.7 %copy-start.5 = (bf16[2048,512]{1,0:T(8,128)(2,1)S(1)}, bf16[2048,512]{1,0:T(8,128)(2,1)}, u32[]{:S(2)}) copy-start(bf16[2048,512]{1,0:T(8,128)(2,1)} %copy-done.4) | copy-start | bytes 6291460
  198.6 34.6 %all-to-all-start.2 = ((bf16[64,64,128]{2,0,1:T(8,128)(2,1)}), bf16[64,64,128]{2,0,1:T(8,128)(2,1)S(1)}, u32[]{:S(2)}, u32[]{:S(2)}) async-start(bf16[64,64,128]{2,0,1:T(8,128)(2,1)} %copy_bitcast_fusion), calls=%async_computation.2 | async-start | bytes 2097152 | tf_op jit(solution)/shard_map/all_to_all | solution.py:84
  205.0 339.7 %all-reduce.4.cloned.1.call-start = ((), (), s32[]{:S(2)}) async-start(), calls=%async_computation.3 | async-start | bytes 4718592 | tf_op jit(solution)/shard_map/psum | solution.py:101
  205.3 1.6 copy-start.21
  206.9 4.0 copy-start.17
  206.9 4.0 copy-start.19
  236.1 44.9 %copy-start.7 = (f32[64,2048]{1,0:T(8,128)S(1)}, f32[64,2048]{1,0:T(8,128)}, u32[]{:S(2)}) copy-start(f32[64,2048]{1,0:T(8,128)} %get-tuple-element.14) | copy-start | bytes 1572868
  281.3 2.9 copy-start.2
  284.1 1.7 copy-start.3
  285.8 80.1 %copy-start.10 = (bf16[512,64]{0,1:T(8,128)(2,1)S(1)}, bf16[512,64]{0,1:T(8,128)(2,1)}, u32[]{:S(2)}) copy-start(bf16[512,64]{0,1:T(8,128)(2,1)} %param.18) | copy-start | bytes 196612
  547.8 3.2 copy-start.1
Sparse Core Ops, SparseCore 0:
  284.2 260.3 all-reduce.3
where the time goes:
time: 560 us; the launch traced here: 558 us
  waiting for transfers between devices  226 us (40%)
  other arithmetic  107 us (19%)
  blocking collectives  77.2 us (14%)
  local copies, waits for them, and re-layouts  68.5 us (12%)
  matrix products  38.2 us (7%)
  starting transfers between devices  25.9 us (5%)
  between operations  15 us (3%)
    psum x1, waiting for transfers between devices, local(): lax.psum((down_grad, basis_grad, bilinear_grad, up_grad, first_grad, seco...  175 us
    psum x1, blocking collectives, local(): lax.psum((down_grad, basis_grad, bilinear_grad, up_grad, first_grad, seco...  77.2 us
    scatter-add x1, other arithmetic, local(): gathered = jnp.zeros((narrow, row_count), jnp.float32).at[:, out_local].a...  45.3 us
    scatter-add x1, other arithmetic, local(): jnp.zeros((narrow, row_count), jnp.float32).at[:, wanted].add(returned)  44.6 us
    dot_general x15, matrix products, contract(): lax.dot_general(left, right, (((left_dim,), (right_dim,)), ((), ())), pre...  33.7 us
    gather x2, local copies, waits for them, and re-layouts, local(): back_message = jnp.take(back_gathered, out_local, axis=1)  31.7 us
    all_to_all x1, waiting for transfers between devices, local(): lax.all_to_all(served, 'graph', split_axis=1, concat_axis=1, tiled=True)  27.5 us
    gather x2, local copies, waits for them, and re-layouts, local(): jnp.take(down_rows, wanted, axis=1).reshape(narrow, shards, slot_count)  25.6 us
  transfers between devices with their start and end apart: 4, of which 4 were waited for; matrix products, arithmetic and copies ran while one was open for 4% of the time, Pallas kernels for 0%

commit v1 on v0

v1 whole, which is shorter than its diff:
```python
import functools
import math

import jax
import jax.numpy as jnp
from jax import lax
from jax.experimental import pallas as pl
from jax.experimental.pallas import tpu as pltpu
from jax.sharding import PartitionSpec as P

HALF = 0.7071067811865476
LOW = 256
MESH = pl.DeviceIdType.MESH
F32 = jnp.float32
BF16 = jnp.bfloat16
VMEM_LIMIT = 60 * 1024 * 1024


def silu_slope(argument):
    logistic = jax.nn.sigmoid(argument)
    return logistic * (1.0 + argument * (1.0 - logistic))


def contract(left, right, left_dim, right_dim):
    return lax.dot_general(
        left, right, (((left_dim,), (right_dim,)), ((), ())), preferred_element_type=jnp.float32
    )


def low_hot(low, width):
    rows = lax.broadcasted_iota(jnp.int32, (LOW, width), 0)
    return jnp.where(rows == low, 1.0, 0.0).astype(BF16)


def pick(table, index, narrow):
    width = index.shape[1]
    high = table.shape[0] // narrow
    hot = low_hot(index & (LOW - 1), width)
    upper = index >> 8
    wide = jnp.dot(table, hot, preferred_element_type=F32)
    out = wide[:narrow]
    for h in range(1, high):
        out = jnp.where(upper == h, wide[h * narrow : (h + 1) * narrow], out)
    return out


def spread(value, index, high):
    hot = low_hot(index & (LOW - 1), index.shape[1])
    upper = index >> 8
    parts = [jnp.where(upper == h, value, 0.0).astype(BF16) for h in range(high)]
    return contract(jnp.concatenate(parts, axis=0), hot, 1, 1)


def serve_kernel(table_ref, index_ref, out_ref):
    narrow = out_ref.shape[1]
    table = table_ref[...]

    @pl.loop(0, index_ref.shape[0])
    def _(i):
        got = pick(table, index_ref[i], narrow).astype(BF16)
        out_ref[2 * i] = got[:, :128]
        out_ref[2 * i + 1] = got[:, 128:]


def coef_of(weight, basis):
    return contract(weight, basis, 0, 0)


def pair_of(ref, i):
    return jnp.concatenate([ref[2 * i], ref[2 * i + 1]], axis=1).astype(F32)


def gather_kernel(fetched_ref, basis_ref, index_ref, weight_ref, out_ref, acc_ref):
    narrow = fetched_ref.shape[1]
    high = acc_ref.shape[0] // narrow
    acc_ref[...] = jnp.zeros_like(acc_ref)

    @pl.loop(0, index_ref.shape[0])
    def _(i):
        columns = pl.ds(pl.multiple_of(i * LOW, LOW), LOW)
        coef = coef_of(weight_ref[...], basis_ref[:, columns])
        message = coef * pair_of(fetched_ref, i)
        acc_ref[...] += spread(message, index_ref[i], high)

    for h in range(high):
        out_ref[:, h * LOW : (h + 1) * LOW] = acc_ref[h * narrow : (h + 1) * narrow].astype(BF16)


def back_kernel(table_ref, fetched_ref, basis_ref, index_ref, weight_ref, out_ref, grad_ref):
    narrow = fetched_ref.shape[1]
    table = table_ref[...]
    grad_ref[...] = jnp.zeros_like(grad_ref)

    @pl.loop(0, index_ref.shape[0])
    def _(i):
        columns = pl.ds(pl.multiple_of(i * LOW, LOW), LOW)
        basis = basis_ref[:, columns]
        got = pick(table, index_ref[i], narrow)
        back_coef = (got * pair_of(fetched_ref, i)).astype(BF16)
        grad_ref[...] += contract(basis, back_coef, 1, 1)
        back = (got * coef_of(weight_ref[...], basis)).astype(BF16)
        out_ref[2 * i] = back[:, :128]
        out_ref[2 * i + 1] = back[:, 128:]


def return_kernel(returned_ref, index_ref, pre_ref, out_ref, acc_ref):
    narrow = returned_ref.shape[1]
    high = acc_ref.shape[0] // narrow
    acc_ref[...] = jnp.zeros_like(acc_ref)

    @pl.loop(0, index_ref.shape[0])
    def _(i):
        acc_ref[...] += spread(pair_of(returned_ref, i), index_ref[i], high)

    for h in range(high):
        columns = slice(h * LOW, (h + 1) * LOW)
        back = acc_ref[h * narrow : (h + 1) * narrow]
        out_ref[:, columns] = (back * silu_slope(pre_ref[:, columns])).astype(BF16)


def local_call(kernel, out_shape, *args, scratch=()):
    vmem = pl.BlockSpec(memory_space=pltpu.VMEM)
    return pl.pallas_call(
        kernel,
        out_shape=out_shape,
        in_specs=[vmem] * len(args),
        out_specs=jax.tree.map(lambda _: vmem, out_shape),
        scratch_shapes=list(scratch),
        compiler_params=pltpu.CompilerParams(vmem_limit_bytes=VMEM_LIMIT),
    )(*args)


def reduce_kernel(scale, first_ref, second_ref, small_ref, first_out, second_out, small_out,
                  send, got_a, part, got_b, held, sem_a, sem_ar, sem_b, sem_br, sem_c, sem_cr):
    wide = first_ref.shape[1]
    rows = send.shape[1]
    group = send.shape[0]
    depth = got_b.shape[0]
    y = lax.axis_index("dp")
    g = lax.axis_index("graph")
    z, x, c = g // 8, (g // 2) % 4, g % 2
    mine = y * 8 + x * 2 + c

    def member(j):
        py = (y + j // 8) % 4
        px = (x + (j // 2) % 4) % 4
        pc = (c + j % 2) % 2
        return (py, z * 8 + px * 2 + pc), py * 8 + px * 2 + pc

    def along(j):
        pz = (z + j) % depth
        return (y, pz * 8 + x * 2 + c)

    barrier = pltpu.get_barrier_semaphore()

    @pl.loop(1, group)
    def _(j):
        pl.semaphore_signal(barrier, inc=1, device_id=member(j)[0], device_id_type=MESH)

    @pl.loop(1, depth)
    def _(j):
        pl.semaphore_signal(barrier, inc=1, device_id=along(j), device_id_type=MESH)

    @pl.loop(0, group)
    def _(m):
        at = pl.ds(pl.multiple_of(m * rows, rows), rows)
        send[m, :, :wide] = first_ref[at, :].astype(BF16)
        send[m, :, wide : 2 * wide] = second_ref[at, :].astype(BF16)
        send[m, :, 2 * wide :] = small_ref[at, :].astype(BF16)

    pl.semaphore_wait(barrier, group - 1 + depth - 1)

    def copy_a(j):
        device, index = member(j)
        return pltpu.make_async_remote_copy(
            src_ref=send.at[index], dst_ref=got_a.at[j], send_sem=sem_a.at[j],
            recv_sem=sem_ar.at[j], device_id=device, device_id_type=MESH)

    def copy_b(j):
        return pltpu.make_async_remote_copy(
            src_ref=part, dst_ref=got_b.at[z], send_sem=sem_b.at[j],
            recv_sem=sem_br.at[j], device_id=along(j), device_id_type=MESH)

    def copy_c(j):
        device, _ = member(j)
        return pltpu.make_async_remote_copy(
            src_ref=held.at[mine], dst_ref=held.at[mine], send_sem=sem_c.at[j],
            recv_sem=sem_cr.at[j], device_id=device, device_id_type=MESH)

    @pl.loop(1, group)
    def _(j):
        copy_a(j).start()

    got_a[0] = send[mine]

    @pl.loop(1, group)
    def _(j):
        copy_a(j).wait()

    total = got_a[0].astype(F32)
    for j in range(1, group):
        total = total + got_a[j].astype(F32)
    part[...] = total.astype(BF16)
    got_b[z] = total.astype(BF16)

    @pl.loop(1, depth)
    def _(j):
        copy_b(j).start()

    @pl.loop(1, depth)
    def _(j):
        copy_b(j).wait()

    total = got_b[0].astype(F32)
    for j in range(1, depth):
        total = total + got_b[j].astype(F32)
    held[mine] = (total * scale).astype(BF16)

    @pl.loop(1, group)
    def _(j):
        copy_c(j).start()

    @pl.loop(1, group)
    def _(j):
        copy_c(j).wait()

    @pl.loop(0, group)
    def _(m):
        at = pl.ds(pl.multiple_of(m * rows, rows), rows)
        first_out[at, :] = held[m, :, :wide].astype(F32)
        second_out[at, :] = held[m, :, wide : 2 * wide].astype(F32)
        small_out[at, :] = held[m, :, 2 * wide :].astype(F32)


def reduce_all(scale, first, second, small):
    group, depth = 32, 8
    rows = first.shape[0] // group
    width = 2 * first.shape[1] + small.shape[1]
    vmem = pl.BlockSpec(memory_space=pltpu.VMEM)
    dma = pltpu.SemaphoreType.DMA
    return pl.pallas_call(
        functools.partial(reduce_kernel, scale),
        out_shape=(
            jax.ShapeDtypeStruct(first.shape, F32),
            jax.ShapeDtypeStruct(second.shape, F32),
            jax.ShapeDtypeStruct(small.shape, F32),
        ),
        in_specs=[vmem] * 3,
        out_specs=(vmem,) * 3,
        scratch_shapes=[
            pltpu.VMEM((group, rows, width), BF16),
            pltpu.VMEM((group, rows, width), BF16),
            pltpu.VMEM((rows, width), BF16),
            pltpu.VMEM((depth, rows, width), BF16),
            pltpu.VMEM((group, rows, width), BF16),
            dma((group,)), dma((group,)), dma((depth,)), dma((depth,)), dma((group,)), dma((group,)),
        ],
        compiler_params=pltpu.CompilerParams(
            collective_id=0, has_side_effects=True, vmem_limit_bytes=VMEM_LIMIT),
    )(first, second, small)


def local(
    edge_state,
    cotangent,
    edge_count,
    triplet_basis,
    triplet_in,
    triplet_out,
    down_weight,
    basis_weight,
    bilinear_weight,
    up_weight,
    first_weight,
    second_weight,
):
    edge_rows = edge_state[0]
    row_count, wide = edge_rows.shape
    shards = lax.axis_size("graph")
    narrow = down_weight.shape[1]
    high = row_count // LOW
    in_local = triplet_in[0]
    tri_rows = in_local.shape[0]
    slot_count = tri_rows // shards
    steps = tri_rows // LOW
    basis = triplet_basis[0]
    out_index = triplet_out[0].reshape(steps, 1, LOW)
    live_mask = (jnp.arange(row_count, dtype=jnp.int32) < edge_count[0, 0]).astype(jnp.float32)
    wanted = lax.all_to_all(
        in_local.reshape(shards, slot_count), "graph", split_axis=0, concat_axis=0, tiled=True
    ).reshape(steps, 1, LOW)
    pre_down = contract(down_weight, edge_rows, 0, 1)
    down_rows = jax.nn.silu(pre_down).astype(jnp.bfloat16)
    block = jax.ShapeDtypeStruct((shards, narrow, slot_count), BF16)

    def to_table(rows):
        return rows.reshape(narrow, high, LOW).transpose(1, 0, 2).reshape(high * narrow, LOW)

    served = local_call(serve_kernel, block, to_table(down_rows), wanted)
    fetched = lax.all_to_all(served, "graph", split_axis=0, concat_axis=0, tiled=True)
    acc = pltpu.VMEM((high * narrow, LOW), F32)
    gathered = local_call(
        gather_kernel, jax.ShapeDtypeStruct((narrow, row_count), BF16),
        fetched, basis, out_index, basis_weight, scratch=(acc,))
    mixed_rows = contract(bilinear_weight, gathered, 0, 0).astype(jnp.bfloat16)
    pre_up = contract(mixed_rows, up_weight, 0, 0)
    summed = edge_rows.astype(jnp.float32) + jax.nn.silu(pre_up)
    summed_half = summed.astype(jnp.bfloat16)
    pre_first = jnp.dot(summed_half, first_weight, preferred_element_type=jnp.float32)
    first_rows = jax.nn.silu(pre_first).astype(jnp.bfloat16)
    pre_second = jnp.dot(first_rows, second_weight, preferred_element_type=jnp.float32)
    back_top = cotangent[0].astype(jnp.float32) * live_mask[:, None] * HALF
    back_second = (back_top * silu_slope(pre_second)).astype(jnp.bfloat16)
    back_first = (contract(back_second, second_weight, 1, 1) * silu_slope(pre_first)).astype(
        jnp.bfloat16
    )
    first_grad = contract(summed_half, back_first, 0, 0)
    second_grad = contract(first_rows, back_second, 0, 0)
    back_summed = back_top + contract(back_first, first_weight, 1, 1)
    back_up = (back_summed * silu_slope(pre_up)).astype(jnp.bfloat16)
    back_mixed = contract(up_weight, back_up, 1, 1).astype(jnp.bfloat16)
    back_gathered = contract(bilinear_weight, back_mixed, 1, 0)
    back_fetched, basis_grad = local_call(
        back_kernel, (block, jax.ShapeDtypeStruct(basis_weight.shape, F32)),
        to_table(back_gathered.astype(BF16)), fetched, basis, out_index, basis_weight)
    returned = lax.all_to_all(back_fetched, "graph", split_axis=0, concat_axis=0, tiled=True)
    back_pre = local_call(
        return_kernel, jax.ShapeDtypeStruct((narrow, row_count), BF16),
        returned, wanted, pre_down, scratch=(acc,))
    up_grad = contract(back_up, mixed_rows, 0, 1)
    bilinear_grad = contract(gathered, back_mixed, 1, 1)
    down_grad = contract(edge_rows, back_pre, 0, 1)
    edge_grad = (back_summed + contract(back_pre, down_weight, 0, 1)).astype(jnp.bfloat16)
    corner = jnp.concatenate([bilinear_grad, basis_grad], axis=0)
    corner = jnp.pad(corner, ((0, wide - corner.shape[0]), (0, 128 - narrow)))
    small = jnp.concatenate([down_grad, up_grad, corner], axis=1)
    grad_scale = 1.0 / math.sqrt(lax.axis_size("dp") * shards * row_count)
    first_grad, second_grad, small = reduce_all(grad_scale, first_grad, second_grad, small)
    return (
        edge_grad[None],
        small[:, :narrow],
        small[narrow : narrow + basis_weight.shape[0], 2 * narrow : 3 * narrow],
        small[:narrow, 2 * narrow : 3 * narrow],
        small[:, narrow : 2 * narrow].T,
        first_grad,
        second_grad,
    )


def solution(mesh):
    in_specs = (
        P("dp", "graph", None),
        P("dp", "graph", None),
        P("dp", "graph"),
        P("dp", None, "graph"),
        P("dp", "graph"),
        P("dp", "graph"),
        P(),
        P(),
        P(),
        P(),
        P(),
        P(),
    )
    out_specs = (P("dp", "graph", None), P(), P(), P(), P(), P(), P())
    return jax.shard_map(local, mesh=mesh, in_specs=in_specs, out_specs=out_specs, check_vma=False)
```

time: 560 us -> 235 us (0.42)
  waiting for transfers between devices: 226 us -> 54.2 us
  Pallas kernels: 0 us -> 109 us
  other arithmetic: 107 us -> 1.87 us
  blocking collectives: 77.2 us -> 0 us
  local copies, waits for them, and re-layouts: 68.5 us -> 11.4 us
  between operations: 15 us -> 1.57 us
  matrix products: 38.2 us -> 30.8 us
    psum x1 -> x0, waiting for transfers between devices: 175 us -> none  [local(): lax.psum((down_grad, basis_grad, bilinear_grad, up_grad, first_grad, seco...]
    pallas_call x0 -> x5, Pallas kernels: none -> 109 us  [the longest x1 59.3 us: reduce_all(): pl.pallas_call(functools.partial(reduce_kernel, scale), out_shape=(jax.Sh...]
    scatter-add x2 -> x0, other arithmetic: 89.9 us -> none  [the longest x1 45.3 us: local(): gathered = jnp.zeros((narrow, row_count), jnp.float32).at[:, out_local].a...]
    psum x1 -> x0, blocking collectives: 77.2 us -> none  [local(): lax.psum((down_grad, basis_grad, bilinear_grad, up_grad, first_grad, seco...]
    gather x4 -> x0, local copies, waits for them, and re-layouts: 57.3 us -> none  [the longest x2 31.7 us: local(): back_message = jnp.take(back_gathered, out_local, axis=1)]
    mul x6 -> x0, other arithmetic: 10.2 us -> none  [the longest x1 3.16 us: local(): second_grad * grad_scale]
    dot_general x15 -> x13, matrix products: 33.7 us -> 26.3 us  [contract(): lax.dot_general(left, right, (((left_dim,), (right_dim,)), ((), ())), pre...]
  transfers between devices with their start and end apart: 4 -> 3, of which waited for: 4 -> 3; matrix products, arithmetic and copies ran while one was open for 4% -> 4% of each run, Pallas kernels for 0% -> 0%
where the time goes in v1:
time: 235 us; the launch traced here: 233 us
  Pallas kernels  109 us (46%)
  waiting for transfers between devices  54.2 us (23%)
  matrix products  30.8 us (13%)
  starting transfers between devices  24.5 us (10%)
  local copies, waits for them, and re-layouts  11.4 us (5%)
    pallas_call x1, Pallas kernels, reduce_all(): pl.pallas_call(functools.partial(reduce_kernel, scale), out_shape=(jax.Sh...  59.3 us
    pallas_call x4, Pallas kernels, local_call(): pl.pallas_call(kernel, out_shape=out_shape, in_specs=[vmem] * len(args),...  49.7 us
    all_to_all x1, waiting for transfers between devices, local(): lax.all_to_all(served, 'graph', split_axis=0, concat_axis=0, tiled=True)  27.5 us
    dot_general x13, matrix products, contract(): lax.dot_general(left, right, (((left_dim,), (right_dim,)), ((), ())), pre...  26.3 us
    all_to_all x1, waiting for transfers between devices, local(): lax.all_to_all(back_fetched, 'graph', split_axis=0, concat_axis=0, tiled=...  21.3 us
    all_to_all x1, starting transfers between devices, local(): lax.all_to_all(in_local.reshape(shards, slot_count), 'graph', split_axis=...  13.1 us
    all_to_all x1, starting transfers between devices, local(): lax.all_to_all(back_fetched, 'graph', split_axis=0, concat_axis=0, tiled=...  6.45 us
    unnamed x46, local copies, waits for them, and re-layouts  6.04 us
  transfers between devices with their start and end apart: 3, of which 3 were waited for; matrix products, arithmetic and copies ran while one was open for 4% of the time, Pallas kernels for 0%

profile of v1, /device:TPU:1, one launch (start us, length us, event | category | flops | bytes accessed | tf_op | source)
XLA Modules:
  0.0 233.4 jit_solution(17737817729861124988)
XLA Ops:
  0.6 0.0 copy-start
  0.6 13.1 %all-to-all-start = ((s32[64,1,128]{2,1,0:T(1,128)}), s32[64,1,128]{2,1,0:T(1,128)S(1)}, u32[]{:S(2)}, u32[]{:S(2)}) async-start(s32[64,1,128]{2,1,0:T(1,128)} %bitcast.79), calls=%async_computation | async-start | bytes 65536 | tf_op jit(solution)/shard_map/all_to_all | solution.py:289
  13.8 0.0 copy-start.10
  13.8 0.0 copy-start.9
  13.8 3.2 %multiply_convert_fusion.3 = (bf16[64,2048]{1,0:T(8,128)(2,1)S(1)}, f32[64,2048]{1,0:T(8,128)}) fusion(bf16[512,64]{0,1:T(8,128)(2,1)} %param.18, bf16[1,2048,512]{2,1,0:T(8,128)(2,1)} %param.12), kind=kOutput, calls=%fused_computation.22 | convolution fusion | flops 134873088 | bytes 2949120 | tf_op jit(solution)/shard_map/dot_general | solution.py:25
  17.0 0.7 copy.41
  17.7 5.4 %all-to-all-done = s32[64,1,128]{2,1,0:T(1,128)S(1)} async-done(((s32[64,1,128]{2,1,0:T(1,128)}), s32[64,1,128]{2,1,0:T(1,128)S(1)}, u32[]{:S(2)}, u32[]{:S(2)}) %all-to-all-start) | async-done | bytes 32800 | tf_op jit(solution)/shard_map/all_to_all | solution.py:289
  23.1 0.6 copy-done.7
  23.7 9.9 %shard_map.171 = bf16[64,64,128]{2,1,0:T(8,128)(2,1)} custom-call(bf16[512,256]{1,0:T(8,128)(2,1)} %bitcast.73, s32[32,1,256]{2,1,0:T(1,128)} %bitcast.74), custom_call_target="tpu_custom_call" | custom-call | tf_op jit(solution)/shard_map/pallas_call | solution.py:123
  33.6 4.9 %all-to-all-start.1 = ((bf16[64,64,128]{2,1,0:T(8,128)(2,1)}), bf16[64,64,128]{2,1,0:T(8,128)(2,1)S(1)}, u32[]{:S(2)}, u32[]{:S(2)}) async-start(bf16[64,64,128]{2,1,0:T(8,128)(2,1)} %shard_map.171), calls=%async_computation.1 | async-start | bytes 2097152 | tf_op jit(solution)/shard_map/all_to_all | solution.py:300
  39.2 27.5 %all-to-all-done.1.fetched_ref = bf16[64,64,128]{2,1,0:T(8,128)(2,1)S(1)} async-done(((bf16[64,64,128]{2,1,0:T(8,128)(2,1)}), bf16[64,64,128]{2,1,0:T(8,128)(2,1)S(1)}, u32[]{:S(2)}, u32[]{:S(2)}) %all-to-all-start.1) | async-done | bytes 1048608 | tf_op jit(solution)/shard_map/all_to_all | solution.py:300
  66.7 1.0 copy-done.1
  67.7 13.9 %shard_map.172 = bf16[64,2048]{1,0:T(8,128)(2,1)} custom-call(bf16[64,64,128]{2,1,0:T(8,128)(2,1)} %copy-done.1, bf16[16,8192]{1,0:T(8,128)(2,1)} %bitcast.69, s32[32,1,256]{2,1,0:T(1,128)} %bitcast.77, bf16[16,64]{1,0:T(8,128)(2,1)} %weight_ref.3), custom_call_target="tpu_custom_call" | custom-call | tf_op jit(solution)/shard_map/pallas_call | solution.py:123
  81.6 0.0 copy-done.10
  81.6 1.2 convolution_convert_fusion.2
  82.9 0.0 copy-done.9
  82.9 2.9 %add_convert_fusion.1 = (bf16[2048,512]{1,0:T(8,128)(2,1)S(1)}, f32[2048,512]{1,0:T(8,128)S(1)}) fusion(bf16[1,2048,512]{2,1,0:T(8,128)(2,1)} %param.12, bf16[2048,64]{0,1:T(8,128)(2,1)S(1)} %convolution_convert_fusion.2, bf16[64,512]{1,0:T(8,128)(2,1)S(1)} %copy-done.9), kind=kOutput, calls=%fused_computation.10 | convolution fusion | flops 141557760 | bytes 8716288 | tf_op jit(solution)/shard_map/dot_general | solution.py:25
  85.8 0.0 copy-start.13
  85.8 0.0 copy-done
  85.8 0.0 copy-start.11
  85.8 0.0 copy-start.12
  85.8 1.9 multiply_convert_fusion.2
  87.7 0.0 copy-done.13
  87.7 0.0 copy-start.17
  87.7 0.4 copy-done.11
  88.1 0.1 copy-done.12
  88.2 2.6 %fusion.3 = bf16[2048,512]{1,0:T(8,128)(2,1)S(1)} fusion(bf16[1,2048,512]{2,1,0:T(8,128)(2,1)S(1)} %copy-done.11, f32[2048]{0:T(1024)S(1)} %fusion.12, bf16[2048,512]{1,0:T(8,128)(2,1)S(1)} %get-tuple-element.37, bf16[512,512]{1,0:T(8,128)(2,1)S(1)} %copy-done.12), kind=kOutput, calls=%fused_computation.4 | convolution fusion | flops 1086324736 | bytes 6823936 | tf_op jit(solution)/shard_map/dot_general | solution.py:311
  90.8 0.0 copy-done.17
  90.8 0.0 copy-start.19
  90.9 2.3 multiply_convert_fusion.1
  93.2 0.0 copy-done.19
  93.2 0.0 copy-start.15
  93.2 4.0 %multiply_convert_fusion = (bf16[2048,512]{1,0:T(8,128)(2,1)S(1)}, f32[2048,512]{1,0:T(8,128)}) fusion(f32[2048,512]{1,0:T(8,128)S(1)} %get-tuple-element.36, bf16[2048,512]{1,0:T(8,128)(2,1)S(1)} %multiply_convert_fusion.1, bf16[512,512]{1,0:T(8,128)(2,1)S(1)} %copy-done, f32[2048]{0:T(1024)S(1)} %fusion.12, bf16[1,2048,512]{2,1,0:T(8,128)(2,1)S(1)} %copy-done.11), kind=kOutput, calls=%fused_computation.6 | convolution fusion | flops 1087373312 | bytes 15212544 | tf_op jit(solution)/shard_map/dot_general | solution.py:25
  97.2 0.0 copy-done.15
  97.2 0.7 convolution_convert_fusion.1
  97.9 0.2 convolution_convert_fusion
  98.1 0.7 copy.40
  98.9 15.0 %shard_map.173 = (bf16[64,64,128]{2,1,0:T(8,128)(2,1)}, f32[16,64]{1,0:T(8,128)}) custom-call(bf16[512,256]{1,0:T(8,128)(2,1)} %bitcast.71, bf16[64,64,128]{2,1,0:T(8,128)(2,1)} %copy-done.1, bf16[16,8192]{1,0:T(8,128)(2,1)} %bitcast.70, s32[32,1,256]{2,1,0:T(1,128)} %bitcast.78, bf16[16,64]{1,0:T(8,128)(2,1)} %weight_ref.3), custom_call_target="tpu_custom_call" | custom-call | tf_op jit(solution)/shard_map/pallas_call | solution.py:123
  113.9 6.5 %all-to-all-start.2 = ((bf16[64,64,128]{2,1,0:T(8,128)(2,1)}), bf16[64,64,128]{2,1,0:T(8,128)(2,1)}, u32[]{:S(2)}, u32[]{:S(2)}) async-start(bf16[64,64,128]{2,1,0:T(8,128)(2,1)} %get-tuple-element.12), calls=%async_computation.2 | async-start | bytes 2097152 | tf_op jit(solution)/shard_map/all_to_all | solution.py:326
  120.4 0.0 copy-done.3
  120.4 0.0 copy-start.18
  120.4 0.0 copy-start.20
  120.4 0.2 fusion.16
  120.6 0.9 select_maximum_fusion
  121.5 0.7 fusion.15
  122.2 0.0 copy-done.18
  122.2 0.4 copy-done.20
  122.6 2.2 fusion.14.second_ref
  124.8 0.0 copy-done.14
  124.9 0.0 copy-done.16
  124.9 2.2 fusion.13.first_ref
  127.1 21.3 %all-to-all-done.2.returned_ref = bf16[64,64,128]{2,1,0:T(8,128)(2,1)} async-done(((bf16[64,64,128]{2,1,0:T(8,128)(2,1)}), bf16[64,64,128]{2,1,0:T(8,128)(2,1)}, u32[]{:S(2)}, u32[]{:S(2)}) %all-to-all-start.2) | async-done | bytes 1048608 | tf_op jit(solution)/shard_map/all_to_all | solution.py:326
  148.4 10.9 %shard_map.174 = bf16[64,2048]{1,0:T(8,128)(2,1)} custom-call(bf16[64,64,128]{2,1,0:T(8,128)(2,1)} %all-to-all-done.2.returned_ref, s32[32,1,256]{2,1,0:T(1,128)} %bitcast.75, f32[64,2048]{1,0:T(8,128)} %get-tuple-element.34.pre_ref), custom_call_target="tpu_custom_call" | custom-call | tf_op jit(solution)/shard_map/pallas_call | solution.py:123
  159.3 1.9 fusion.9
  161.3 1.0 pad_maximum_fusion.small_ref
  162.3 59.3 %shard_map.175 = (f32[512,512]{1,0:T(8,128)}, f32[512,512]{1,0:T(8,128)}, f32[512,256]{1,0:T(8,128)}) custom-call(f32[512,512]{1,0:T(8,128)} %fusion.13.first_ref, f32[512,512]{1,0:T(8,128)} %fusion.14.second_ref, f32[512,256]{1,0:T(8,128)} %pad_maximum_fusion.small_ref), custom_call_target="tpu_custom_call" | custom-call | tf_op jit(solution)/shard_map/pallas_call | solution.py:241
  221.6 1.3 slice.13
  222.9 1.4 slice.14
  224.3 1.2 slice_bitcast_fusion
  225.5 4.3 %fusion.4 = bf16[1,2048,512]{2,1,0:T(8,128)(2,1)} fusion(f32[2048,512]{1,0:T(8,128)} %get-tuple-element.40, bf16[64,2048]{1,0:T(8,128)(2,1)S(1)} %copy-done.2, bf16[512,64]{0,1:T(8,128)(2,1)S(1)} %copy-done.8), kind=kOutput, calls=%fused_computation.12 | convolution fusion | flops 136314880 | bytes 6619136 | tf_op jit(solution)/shard_map/dot_general | solution.py:25
  229.9 0.8 copy.32
  230.7 0.8 copy.31
  231.4 1.0 copy.45
  232.4 1.0 copy.46
  (16 shorter events, 0.0 us)
Async XLA Ops:
  0.6 85.2 %copy-start = (bf16[512,512]{1,0:T(8,128)(2,1)S(1)}, bf16[512,512]{1,0:T(8,128)(2,1)}, u32[]{:S(2)}) copy-start(bf16[512,512]{1,0:T(8,128)(2,1)} %param.22) | copy-start | bytes 1572868
  0.6 22.5 %all-to-all-start = ((s32[64,1,128]{2,1,0:T(1,128)}), s32[64,1,128]{2,1,0:T(1,128)S(1)}, u32[]{:S(2)}, u32[]{:S(2)}) async-start(s32[64,1,128]{2,1,0:T(1,128)} %bitcast.79), calls=%async_computation | async-start | bytes 65536 | tf_op jit(solution)/shard_map/all_to_all | solution.py:289
  13.8 67.9 %copy-start.10 = (bf16[64,64]{1,0:T(8,128)(2,1)S(1)}, bf16[64,64]{1,0:T(8,128)(2,1)}, u32[]{:S(2)}) copy-start(bf16[64,64]{1,0:T(8,128)(2,1)} %param.20) | copy-start | bytes 24580
  13.8 69.1 %copy-start.9 = (bf16[64,512]{1,0:T(8,128)(2,1)S(1)}, bf16[64,512]{1,0:T(8,128)(2,1)}, u32[]{:S(2)}) copy-start(bf16[64,512]{1,0:T(8,128)(2,1)} %param.21) | copy-start | bytes 196612
  23.1 0.6 copy-start.7
  33.6 33.1 %all-to-all-start.1 = ((bf16[64,64,128]{2,1,0:T(8,128)(2,1)}), bf16[64,64,128]{2,1,0:T(8,128)(2,1)S(1)}, u32[]{:S(2)}, u32[]{:S(2)}) async-start(bf16[64,64,128]{2,1,0:T(8,128)(2,1)} %shard_map.171), calls=%async_computation.1 | async-start | bytes 2097152 | tf_op jit(solution)/shard_map/all_to_all | solution.py:300
  66.7 1.0 copy-start.1
  85.8 1.9 copy-start.13
  85.8 2.3 %copy-start.11 = (bf16[1,2048,512]{2,1,0:T(8,128)(2,1)S(1)}, bf16[1,2048,512]{2,1,0:T(8,128)(2,1)}, u32[]{:S(2)}) copy-start(bf16[1,2048,512]{2,1,0:T(8,128)(2,1)} %param.13) | copy-start | bytes 6291460
  85.8 2.4 %copy-start.12 = (bf16[512,512]{1,0:T(8,128)(2,1)S(1)}, bf16[512,512]{1,0:T(8,128)(2,1)}, u32[]{:S(2)}) copy-start(bf16[512,512]{1,0:T(8,128)(2,1)} %param.23) | copy-start | bytes 1572868
  87.7 3.1 %copy-start.17 = (bf16[2048,512]{1,0:T(8,128)(2,1)}, bf16[2048,512]{1,0:T(8,128)(2,1)S(1)}, u32[]{:S(2)}) copy-start(bf16[2048,512]{1,0:T(8,128)(2,1)S(1)} %get-tuple-element.37) | copy-start | bytes 6291460
  90.8 2.3 copy-start.19
  93.2 4.0 %copy-start.15 = (bf16[2048,512]{1,0:T(8,128)(2,1)}, bf16[2048,512]{1,0:T(8,128)(2,1)S(1)}, u32[]{:S(2)}) copy-start(bf16[2048,512]{1,0:T(8,128)(2,1)S(1)} %multiply_convert_fusion.1) | copy-start | bytes 6291460
  97.2 23.2 %copy-start.3 = (bf16[64,2048]{1,0:T(8,128)(2,1)S(1)}, bf16[64,2048]{1,0:T(8,128)(2,1)}, u32[]{:S(2)}) copy-start(bf16[64,2048]{1,0:T(8,128)(2,1)} %shard_map.172) | copy-start | bytes 786436
  113.9 34.5 %all-to-all-start.2 = ((bf16[64,64,128]{2,1,0:T(8,128)(2,1)}), bf16[64,64,128]{2,1,0:T(8,128)(2,1)}, u32[]{:S(2)}, u32[]{:S(2)}) async-start(bf16[64,64,128]{2,1,0:T(8,128)(2,1)} %get-tuple-element.12), calls=%async_computation.2 | async-start | bytes 2097152 | tf_op jit(solution)/shard_map/all_to_all | solution.py:326
  120.4 1.9 copy-start.18
  120.4 2.2 copy-start.20
  122.6 2.2 copy-start.14
  122.6 2.2 copy-start.16
  124.9 34.5 %copy-start.4 = (bf16[1,2048,512]{2,1,0:T(8,128)(2,1)S(1)}, bf16[1,2048,512]{2,1,0:T(8,128)(2,1)}, u32[]{:S(2)}) copy-start(bf16[1,2048,512]{2,1,0:T(8,128)(2,1)} %param.12) | copy-start | bytes 6291460
  159.3 66.2 %copy-start.2 = (bf16[64,2048]{1,0:T(8,128)(2,1)S(1)}, bf16[64,2048]{1,0:T(8,128)(2,1)}, u32[]{:S(2)}) copy-start(bf16[64,2048]{1,0:T(8,128)(2,1)} %shard_map.174) | copy-start | bytes 786436
  159.3 66.2 %copy-start.8 = (bf16[512,64]{0,1:T(8,128)(2,1)S(1)}, bf16[512,64]{0,1:T(8,128)(2,1)}, u32[]{:S(2)}) copy-start(bf16[512,64]{0,1:T(8,128)(2,1)} %param.18) | copy-start | bytes 196612
  224.3 7.2 %copy-start.6 = (f32[512,512]{1,0:T(8,128)S(1)}, f32[512,512]{1,0:T(8,128)}, u32[]{:S(2)}) copy-start(f32[512,512]{1,0:T(8,128)} %get-tuple-element.53) | copy-start | bytes 3145732
  225.5 6.9 %copy-start.5 = (f32[512,512]{1,0:T(8,128)S(1)}, f32[512,512]{1,0:T(8,128)}, u32[]{:S(2)}) copy-start(f32[512,512]{1,0:T(8,128)} %get-tuple-element.54) | copy-start | bytes 3145732

commit v2 on v1

--- a/solution.py
+++ b/solution.py
@@ -51,56 +51,256 @@
     return contract(jnp.concatenate(parts, axis=0), hot, 1, 1)
 
 
-def serve_kernel(table_ref, index_ref, out_ref):
-    narrow = out_ref.shape[1]
-    table = table_ref[...]
-
-    @pl.loop(0, index_ref.shape[0])
-    def _(i):
-        got = pick(table, index_ref[i], narrow).astype(BF16)
-        out_ref[2 * i] = got[:, :128]
-        out_ref[2 * i + 1] = got[:, 128:]
-
-
 def coef_of(weight, basis):
     return contract(weight, basis, 0, 0)
 
 
+def place():
+    g = lax.axis_index("graph")
+    return lax.axis_index("dp"), g // 8, (g // 2) % 4, g % 2
+
+
+def chip_at(k, a, sign):
+    _, z, x, _ = place()
+    dz, dx = (k + 2 * a) % 8, a
+    if sign < 0:
+        dz, dx = 8 - dz, 4 - dx
+    return (z + dz) % 8 * 4 + (x + dx) % 4
+
+
+def for_peers(k, a, sign, fn):
+    q = chip_at(k, a, sign)
+    if a:
+        fn(2 * q)
+        fn(2 * q + 1)
+        return
+
+    @pl.when(k > 0)
+    def _():
+        fn(2 * q)
+        fn(2 * q + 1)
+
+    @pl.when(k == 0)
+    def _():
+        g = lax.axis_index("graph")
+        fn(g + 1 - 2 * (g % 2))
+
+
+def row_of(ref, k, sign):
+    return jnp.concatenate([ref[chip_at(k, a, sign)] for a in range(4)], axis=1)
+
+
+def pairs_of(ref, k, sign):
+    chips = [chip_at(k, a, sign) for a in range(4)]
+    return jnp.concatenate([ref[2 * q + c] for q in chips for c in range(2)], axis=1)
+
+
+def columns_of(ref, k, sign):
+    chips = [chip_at(k, a, sign) for a in range(4)]
+    return jnp.concatenate(
+        [ref[:, pl.ds(pl.multiple_of(q * LOW, LOW), LOW)] for q in chips], axis=1)
+
+
+def put_pairs(ref, k, sign, value):
+    for a in range(4):
+        q = chip_at(k, a, sign)
+        for c in range(2):
+            at = (2 * a + c) * 128
+            ref[2 * q + c] = value[:, at : at + 128]
+
+
+def exchange(src, dst, send_sem, recv_sem):
+    y = lax.axis_index("dp")
+    g = lax.axis_index("graph")
+
+    def out(p):
+        return pltpu.make_async_remote_copy(
+            src_ref=src.at[p], dst_ref=dst.at[g], send_sem=send_sem.at[p],
+            recv_sem=recv_sem.at[g], device_id=(y, p), device_id_type=MESH)
+
+    def back(p):
+        return pltpu.make_async_remote_copy(
+            src_ref=src.at[p], dst_ref=dst.at[p], send_sem=send_sem.at[p],
+            recv_sem=recv_sem.at[p], device_id=(y, p), device_id_type=MESH)
+
+    return out, back
+
+
+def forward_kernel(edge_ref, in_ref, out_ref, basis_ref, down_ref, weight_ref,
+                   fetched, wanted, pre_ref, gathered_ref,
+                   table, outbox, acc, is_sem, ir_sem, rs_sem, rr_sem):
+    shards, narrow = fetched.shape[:2]
+    high = table.shape[0] // narrow
+    y = lax.axis_index("dp")
+    g = lax.axis_index("graph")
+    barrier = pltpu.get_barrier_semaphore()
+
+    @pl.loop(1, shards)
+    def _(j):
+        pl.semaphore_signal(barrier, inc=1, device_id=(y, (g + j) % shards), device_id_type=MESH)
+
+    wanted[g] = in_ref[g]
+    for h in range(high):
+        pre = jnp.dot(edge_ref[h * LOW : (h + 1) * LOW], down_ref[...], preferred_element_type=F32)
+        pre = pre.T
+        pre_ref[:, h * LOW : (h + 1) * LOW] = pre
+        table[h * narrow : (h + 1) * narrow] = (pre * jax.nn.sigmoid(pre)).astype(BF16)
+    acc[...] = jnp.zeros_like(acc)
+    pl.semaphore_wait(barrier, shards - 1)
+    ask, asked = exchange(in_ref, wanted, is_sem, ir_sem)
+    give, given = exchange(outbox, fetched, rs_sem, rr_sem)
+
+    @pl.loop(0, 8)
+    def _(k):
+        for a in range(4):
+            for_peers(k, a, -1, lambda p: ask(p).start())
+
+    @pl.loop(0, 8)
+    def _(k):
+        for a in range(4):
+            for_peers(k, a, 1, lambda p: asked(p).wait_recv())
+        index = pairs_of(wanted, k, 1)
+        put_pairs(outbox, k, 1, pick(table[...], index, narrow).astype(BF16))
+        for a in range(4):
+            for_peers(k, a, 1, lambda p: give(p).start())
+
+    fetched[g] = outbox[g]
+
+    @pl.loop(0, 8)
+    def _(k):
+        for a in range(4):
+            for_peers(k, a, -1, lambda p: given(p).wait_recv())
+        coef = coef_of(weight_ref[...], columns_of(basis_ref, k, -1))
+        message = coef * pairs_of(fetched, k, -1).astype(F32)
+        acc[...] += spread(message, row_of(out_ref, k, -1), high)
+
+    for h in range(high):
+        gathered_ref[:, h * LOW : (h + 1) * LOW] = acc[h * narrow : (h + 1) * narrow].astype(BF16)
+
+    @pl.loop(1, shards)
+    def _(j):
+        p = (g + j) % shards
+        ask(p).wait_send()
+        give(p).wait_send()
+
+
+VM = pl.BlockSpec(memory_space=pltpu.VMEM)
+
+
+def forward(edge_rows, in_index, out_index, basis, down_weight, basis_weight):
+    shards, _, slots = in_index.shape
+    rows = edge_rows.shape[0]
+    narrow = down_weight.shape[1]
+    high = rows // LOW
+    dma = pltpu.SemaphoreType.DMA
+    return pl.pallas_call(
+        forward_kernel,
+        out_shape=(
+            jax.ShapeDtypeStruct((shards, narrow, slots), BF16),
+            jax.ShapeDtypeStruct(in_index.shape, jnp.int32),
+            jax.ShapeDtypeStruct((narrow, rows), F32),
+            jax.ShapeDtypeStruct((narrow, rows), BF16),
+        ),
+        in_specs=[VM] * 6,
+        out_specs=(VM,) * 4,
+        scratch_shapes=[
+            pltpu.VMEM((high * narrow, LOW), BF16),
+            pltpu.VMEM((shards, narrow, slots), BF16),
+            pltpu.VMEM((high * narrow, LOW), F32),
+            dma((shards,)), dma((shards,)), dma((shards,)), dma((shards,)),
+        ],
+        compiler_params=pltpu.CompilerParams(
+            collective_id=1, has_side_effects=True, vmem_limit_bytes=VMEM_LIMIT),
+        name="forward_exchange",
+    )(edge_rows, in_index, out_index, basis, down_weight, basis_weight)
+
+
+def slope_from(value, logistic):
+    return logistic * (1.0 + value * (1.0 - logistic))
+
+
+def dense_kernel(edge_ref, cot_ref, count_ref, gathered_ref, bil_ref, up_ref, w1_ref, w2_ref,
+                 summed_ref, table_ref, first_ref, second_ref, upg_ref, bilg_ref):
+    narrow = gathered_ref.shape[0]
+    block = LOW
+    steps = edge_ref.shape[0] // block
+    first_ref[...] = jnp.zeros_like(first_ref)
+    second_ref[...] = jnp.zeros_like(second_ref)
+    upg_ref[...] = jnp.zeros_like(upg_ref)
+    bilg_ref[...] = jnp.zeros_like(bilg_ref)
+    count = count_ref[0, 0]
+
+    @pl.loop(0, steps)
+    def _(i):
+        at = pl.ds(pl.multiple_of(i * block, block), block)
+        gat = gathered_ref[:, at]
+        mixed = contract(bil_ref[...], gat, 0, 0).astype(BF16)
+        pre_up = contract(mixed, up_ref[...], 0, 0)
+        s_up = jax.nn.sigmoid(pre_up)
+        half = (edge_ref[at, :].astype(F32) + pre_up * s_up).astype(BF16)
+        pre_first = jnp.dot(half, w1_ref[...], preferred_element_type=F32)
+        s_first = jax.nn.sigmoid(pre_first)
+        rows1 = (pre_first * s_first).astype(BF16)
+        pre_second = jnp.dot(rows1, w2_ref[...], preferred_element_type=F32)
+        live = lax.broadcasted_iota(jnp.int32, (block, 1), 0) + i * block < count
+        top = cot_ref[at, :].astype(F32) * jnp.where(live, HALF, 0.0)
+        back2 = (top * slope_from(pre_second, jax.nn.sigmoid(pre_second))).astype(BF16)
+        back1 = contract(back2, w2_ref[...], 1, 1) * slope_from(pre_first, s_first)
+        back1 = back1.astype(BF16)
+        total = top + contract(back1, w1_ref[...], 1, 1)
+        summed_ref[at, :] = total
+        back_up = (total * slope_from(pre_up, s_up)).astype(BF16)
+        back_mixed = contract(up_ref[...], back_up, 1, 1).astype(BF16)
+        where = pl.ds(pl.multiple_of(i * narrow, narrow), narrow)
+        table_ref[where, :] = jnp.dot(
+            bil_ref[...], back_mixed, preferred_element_type=F32).astype(BF16)
+        first_ref[...] += contract(half, back1, 0, 0)
+        second_ref[...] += contract(rows1, back2, 0, 0)
+        upg_ref[...] += jnp.dot(mixed, back_up, preferred_element_type=F32)
+        bilg_ref[...] += contract(gat, back_mixed, 1, 1)
+
+
+def dense(edge_rows, cotangent, count, gathered, bilinear, up, first, second):
+    rows, wide = edge_rows.shape
+    narrow = gathered.shape[0]
+    shape = jax.ShapeDtypeStruct
+    return pl.pallas_call(
+        dense_kernel,
+        out_shape=(
+            shape((rows, wide), F32),
+            shape((rows // LOW * narrow, LOW), BF16),
+            shape((wide, wide), F32),
+            shape((wide, wide), F32),
+            shape((narrow, wide), F32),
+            shape((narrow, narrow), F32),
+        ),
+        in_specs=[VM, VM, pl.BlockSpec(memory_space=pltpu.SMEM)] + [VM] * 5,
+        out_specs=(VM,) * 6,
+        compiler_params=pltpu.CompilerParams(vmem_limit_bytes=VMEM_LIMIT),
+        name="dense",
+    )(edge_rows, cotangent, count, gathered, bilinear, up, first, second)
+
+
 def pair_of(ref, i):
-    return jnp.concatenate([ref[2 * i], ref[2 * i + 1]], axis=1).astype(F32)
-
-
-def gather_kernel(fetched_ref, basis_ref, index_ref, weight_ref, out_ref, acc_ref):
-    narrow = fetched_ref.shape[1]
-    high = acc_ref.shape[0] // narrow
-    acc_ref[...] = jnp.zeros_like(acc_ref)
-
-    @pl.loop(0, index_ref.shape[0])
-    def _(i):
-        columns = pl.ds(pl.multiple_of(i * LOW, LOW), LOW)
-        coef = coef_of(weight_ref[...], basis_ref[:, columns])
-        message = coef * pair_of(fetched_ref, i)
-        acc_ref[...] += spread(message, index_ref[i], high)
-
-    for h in range(high):
-        out_ref[:, h * LOW : (h + 1) * LOW] = acc_ref[h * narrow : (h + 1) * narrow].astype(BF16)
+    return jnp.concatenate([ref[8 * i + a] for a in range(8)], axis=1).astype(F32)
 
 
 def back_kernel(table_ref, fetched_ref, basis_ref, index_ref, weight_ref, out_ref, grad_ref):
     narrow = fetched_ref.shape[1]
     table = table_ref[...]
+    width = index_ref.shape[2]
     grad_ref[...] = jnp.zeros_like(grad_ref)
 
     @pl.loop(0, index_ref.shape[0])
     def _(i):
-        columns = pl.ds(pl.multiple_of(i * LOW, LOW), LOW)
+        columns = pl.ds(pl.multiple_of(i * width, width), width)
         basis = basis_ref[:, columns]
         got = pick(table, index_ref[i], narrow)
         back_coef = (got * pair_of(fetched_ref, i)).astype(BF16)
         grad_ref[...] += contract(basis, back_coef, 1, 1)
         back = (got * coef_of(weight_ref[...], basis)).astype(BF16)
-        out_ref[2 * i] = back[:, :128]
-        out_ref[2 * i + 1] = back[:, 128:]
+        for a in range(8):
+            out_ref[8 * i + a] = back[:, a * 128 : (a + 1) * 128]
 
 
 def return_kernel(returned_ref, index_ref, pre_ref, out_ref, acc_ref):
@@ -119,12 +319,11 @@
 
 
 def local_call(kernel, out_shape, *args, scratch=()):
-    vmem = pl.BlockSpec(memory_space=pltpu.VMEM)
     return pl.pallas_call(
         kernel,
         out_shape=out_shape,
-        in_specs=[vmem] * len(args),
-        out_specs=jax.tree.map(lambda _: vmem, out_shape),
+        in_specs=[VM] * len(args),
+        out_specs=jax.tree.map(lambda _: VM, out_shape),
         scratch_shapes=list(scratch),
         compiler_params=pltpu.CompilerParams(vmem_limit_bytes=VMEM_LIMIT),
     )(*args)
@@ -279,61 +478,30 @@
     shards = lax.axis_size("graph")
     narrow = down_weight.shape[1]
     high = row_count // LOW
-    in_local = triplet_in[0]
-    tri_rows = in_local.shape[0]
+    tri_rows = triplet_in.shape[1]
     slot_count = tri_rows // shards
-    steps = tri_rows // LOW
     basis = triplet_basis[0]
-    out_index = triplet_out[0].reshape(steps, 1, LOW)
-    live_mask = (jnp.arange(row_count, dtype=jnp.int32) < edge_count[0, 0]).astype(jnp.float32)
-    wanted = lax.all_to_all(
-        in_local.reshape(shards, slot_count), "graph", split_axis=0, concat_axis=0, tiled=True
-    ).reshape(steps, 1, LOW)
-    pre_down = contract(down_weight, edge_rows, 0, 1)
-    down_rows = jax.nn.silu(pre_down).astype(jnp.bfloat16)
+    out_index = triplet_out[0].reshape(tri_rows // LOW, 1, LOW)
+    in_index = triplet_in[0].reshape(shards, 1, slot_count)
+    fetched, wanted, pre_down, gathered = forward(
+        edge_rows, in_index, out_index, basis, down_weight, basis_weight)
+    back_summed, table, first_grad, second_grad, up_grad, bilinear_grad = dense(
+        edge_rows, cotangent[0], edge_count, gathered, bilinear_weight, up_weight,
+        first_weight, second_weight)
     block = jax.ShapeDtypeStruct((shards, narrow, slot_count), BF16)
-
-    def to_table(rows):
-        return rows.reshape(narrow, high, LOW).transpose(1, 0, 2).reshape(high * narrow, LOW)
-
-    served = local_call(serve_kernel, block, to_table(down_rows), wanted)
-    fetched = lax.all_to_all(served, "graph", split_axis=0, concat_axis=0, tiled=True)
-    acc = pltpu.VMEM((high * narrow, LOW), F32)
-    gathered = local_call(
-        gather_kernel, jax.ShapeDtypeStruct((narrow, row_count), BF16),
-        fetched, basis, out_index, basis_weight, scratch=(acc,))
-    mixed_rows = contract(bilinear_weight, gathered, 0, 0).astype(jnp.bfloat16)
-    pre_up = contract(mixed_rows, up_weight, 0, 0)
-    summed = edge_rows.astype(jnp.float32) + jax.nn.silu(pre_up)
-    summed_half = summed.astype(jnp.bfloat16)
-    pre_first = jnp.dot(summed_half, first_weight, preferred_element_type=jnp.float32)
-    first_rows = jax.nn.silu(pre_first).astype(jnp.bfloat16)
-    pre_second = jnp.dot(first_rows, second_weight, preferred_element_type=jnp.float32)
-    back_top = cotangent[0].astype(jnp.float32) * live_mask[:, None] * HALF
-    back_second = (back_top * silu_slope(pre_second)).astype(jnp.bfloat16)
-    back_first = (contract(back_second, second_weight, 1, 1) * silu_slope(pre_first)).astype(
-        jnp.bfloat16
-    )
-    first_grad = contract(summed_half, back_first, 0, 0)
-    second_grad = contract(first_rows, back_second, 0, 0)
-    back_summed = back_top + contract(back_first, first_weight, 1, 1)
-    back_up = (back_summed * silu_slope(pre_up)).astype(jnp.bfloat16)
-    back_mixed = contract(up_weight, back_up, 1, 1).astype(jnp.bfloat16)
-    back_gathered = contract(bilinear_weight, back_mixed, 1, 0)
     back_fetched, basis_grad = local_call(
         back_kernel, (block, jax.ShapeDtypeStruct(basis_weight.shape, F32)),
-        to_table(back_gathered.astype(BF16)), fetched, basis, out_index, basis_weight)
+        table, fetched, basis, out_index.reshape(8, 1, 1024), basis_weight)
     returned = lax.all_to_all(back_fetched, "graph", split_axis=0, concat_axis=0, tiled=True)
     back_pre = local_call(
         return_kernel, jax.ShapeDtypeStruct((narrow, row_count), BF16),
-        returned, wanted, pre_down, scratch=(acc,))
-    up_grad = contract(back_up, mixed_rows, 0, 1)
-    bilinear_grad = contract(gathered, back_mixed, 1, 1)
+        returned, wanted.reshape(8, 1, 1024), pre_down,
+        scratch=(pltpu.VMEM((high * narrow, LOW), F32),))
     down_grad = contract(edge_rows, back_pre, 0, 1)
     edge_grad = (back_summed + contract(back_pre, down_weight, 0, 1)).astype(jnp.bfloat16)
     corner = jnp.concatenate([bilinear_grad, basis_grad], axis=0)
     corner = jnp.pad(corner, ((0, wide - corner.shape[0]), (0, 128 - narrow)))
-    small = jnp.concatenate([down_grad, up_grad, corner], axis=1)
+    small = jnp.concatenate([down_grad, up_grad.T, corner], axis=1)
     grad_scale = 1.0 / math.sqrt(lax.axis_size("dp") * shards * row_count)
     first_grad, second_grad, small = reduce_all(grad_scale, first_grad, second_grad, small)
     return (

time: 235 us -> 198 us (0.84)
  Pallas kernels: 109 us -> 145 us
  waiting for transfers between devices: 54.2 us -> 26.5 us
  matrix products: 30.8 us -> 6.2 us
  starting transfers between devices: 24.5 us -> 5.36 us
    pallas_call x4, Pallas kernels: 49.7 us -> 86.1 us  [the longest x1 50.4 us: forward(): pl.pallas_call(forward_kernel, out_shape=(jax.ShapeDtypeStruct((shards, n...]
    all_to_all x2 -> x0, waiting for transfers between devices: 32.9 us -> none  [the longest x1 27.5 us: local(): lax.all_to_all(served, 'graph', split_axis=0, concat_axis=0, tiled=True)]
    dot_general x13 -> x2, matrix products: 26.3 us -> 6.2 us  [contract(): lax.dot_general(left, right, (((left_dim,), (right_dim,)), ((), ())), pre...]
    all_to_all x2 -> x0, starting transfers between devices: 18.1 us -> none  [the longest x1 13.1 us: local(): lax.all_to_all(in_local.reshape(shards, slot_count), 'graph', split_axis=...]
    all_to_all x1, waiting for transfers between devices: 21.3 us -> 26.5 us  [local(): lax.all_to_all(back_fetched, 'graph', split_axis=0, concat_axis=0, tiled=...]
    dot_general x2 -> x0, matrix products: 4.47 us -> none  [the longest x1 2.6 us: local(): jnp.dot(first_rows, second_weight, preferred_element_type=jnp.float32)]
    unnamed x46 -> x23, local copies, waits for them, and re-layouts: 6.04 us -> 6.08 us
  transfers between devices with their start and end apart: 3 -> 1, of which waited for: 3 -> 1; matrix products, arithmetic and copies ran while one was open for 4% -> 1% of each run, Pallas kernels for 0% -> 0%
where the time goes in v2:
time: 198 us; the launch traced here: 197 us
  Pallas kernels  145 us (73%)
  waiting for transfers between devices  26.5 us (13%)
  local copies, waits for them, and re-layouts  10.1 us (5%)
  matrix products  6.2 us (3%)
  starting transfers between devices  5.36 us (3%)
  other arithmetic  2.48 us (1%)
    pallas_call x1, Pallas kernels, reduce_all(): pl.pallas_call(functools.partial(reduce_kernel, scale), out_shape=(jax.Sh...  59.3 us
    pallas_call x1, Pallas kernels, forward(): pl.pallas_call(forward_kernel, out_shape=(jax.ShapeDtypeStruct((shards, n...  50.4 us
    all_to_all x1, waiting for transfers between devices, local(): lax.all_to_all(back_fetched, 'graph', split_axis=0, concat_axis=0, tiled=...  26.5 us
    pallas_call x1, Pallas kernels, dense(): pl.pallas_call(dense_kernel, out_shape=(shape((rows, wide), F32), shape((...  22.1 us
    pallas_call x2, Pallas kernels, local_call(): pl.pallas_call(kernel, out_shape=out_shape, in_specs=[VM] * len(args), ou...  13.6 us
    dot_general x2, matrix products, contract(): lax.dot_general(left, right, (((left_dim,), (right_dim,)), ((), ())), pre...  6.2 us
    unnamed x23, local copies, waits for them, and re-layouts  6.08 us
    all_to_all x1, starting transfers between devices, local(): lax.all_to_all(back_fetched, 'graph', split_axis=0, concat_axis=0, tiled=...  5.36 us
  transfers between devices with their start and end apart: 1, of which 1 were waited for; matrix products, arithmetic and copies ran while one was open for 1% of the time, Pallas kernels for 0%

profile of v2, /device:TPU:1, one launch (start us, length us, event | category | flops | bytes accessed | tf_op | source)
XLA Modules:
  0.0 197.4 jit_solution(18310194706343026913)
XLA Ops:
  1.3 1.6 copy.19.down_ref
  2.9 50.4 %forward_exchange.1 = (bf16[64,64,128]{2,1,0:T(8,128)(2,1)}, s32[64,1,128]{2,1,0:T(1,128)}, f32[64,2048]{1,0:T(8,128)}, bf16[64,2048]{1,0:T(8,128)(2,1)}) custom-call(bf16[2048,512]{1,0:T(8,128)(2,1)} %bitcast.19, s32[64,1,128]{2,1,0:T(1,128)} %bitcast.27, s32[32,1,256]{2,1,0:T(1,128)} %bitcast.25, bf16[16,8192]{1,0:T(8,128)(2,1)} %bitcast.22, ...), custom_call_target="tpu_custom_call" | custom-call | tf_op jit(solution)/shard_map/forward_exchange/pallas_call | solution.py:196
  53.3 22.1 %dense.1 = (f32[2048,512]{1,0:T(8,128)}, bf16[512,256]{1,0:T(8,128)(2,1)}, f32[512,512]{1,0:T(8,128)}, f32[512,512]{1,0:T(8,128)}, f32[64,512]{1,0:T(8,128)}, /*index=5*/f32[64,64]{1,0:T(8,128)}) custom-call(bf16[2048,512]{1,0:T(8,128)(2,1)} %bitcast.20, bf16[2048,512]{1,0:T(8,128)(2,1)} %bitcast.21, s32[1,1]{1,0:T(1,128)S(6)} %copy.27.count_ref, ...), custom_call_target="tpu_custom_call" | custom-call | tf_op jit(solution)/shard_map/dense/pallas_call | solution.py:267
  75.4 0.0 copy-start.7
  75.4 7.4 %shard_map.171 = (bf16[64,64,128]{2,1,0:T(8,128)(2,1)}, f32[16,64]{1,0:T(8,128)}) custom-call(bf16[512,256]{1,0:T(8,128)(2,1)} %get-tuple-element.24.table_ref, bf16[64,64,128]{2,1,0:T(8,128)(2,1)} %get-tuple-element.25.fetched_ref, bf16[16,8192]{1,0:T(8,128)(2,1)} %bitcast.23, s32[8,1,1024]{2,1,0:T(1,128)} %bitcast.26, bf16[16,64]{1,0:T(8,128)(2,1)} %weight_ref.3), custom_call_target="tpu_custom_call" | custom-call | tf_op jit(solution)/shard_map/pallas_call | solution.py:322
  82.7 0.0 copy-start.8
  82.7 0.0 copy-start
  82.8 5.4 %all-to-all-start = ((bf16[64,64,128]{2,1,0:T(8,128)(2,1)}), bf16[64,64,128]{2,1,0:T(8,128)(2,1)S(1)}, u32[]{:S(2)}, u32[]{:S(2)}) async-start(bf16[64,64,128]{2,1,0:T(8,128)(2,1)} %get-tuple-element.26), calls=%async_computation | async-start | bytes 2097152 | tf_op jit(solution)/shard_map/all_to_all | solution.py:495
  88.1 0.0 copy-done.7
  88.1 0.1 copy.21
  88.3 0.0 copy-done.8
  88.3 1.5 select_maximum_fusion
  89.7 26.5 %all-to-all-done.returned_ref = bf16[64,64,128]{2,1,0:T(8,128)(2,1)S(1)} async-done(((bf16[64,64,128]{2,1,0:T(8,128)(2,1)}), bf16[64,64,128]{2,1,0:T(8,128)(2,1)S(1)}, u32[]{:S(2)}, u32[]{:S(2)}) %all-to-all-start) | async-done | bytes 1048608 | tf_op jit(solution)/shard_map/all_to_all | solution.py:495
  116.3 0.0 copy-start.1
  116.3 1.0 copy-done.1
  117.3 0.0 copy-start.3
  117.3 6.2 %shard_map.172 = bf16[64,2048]{1,0:T(8,128)(2,1)} custom-call(bf16[64,64,128]{2,1,0:T(8,128)(2,1)} %copy-done.1, s32[8,1,1024]{2,1,0:T(1,128)} %bitcast.28, f32[64,2048]{1,0:T(8,128)} %get-tuple-element.28.pre_ref), custom_call_target="tpu_custom_call" | custom-call | tf_op jit(solution)/shard_map/pallas_call | solution.py:322
  123.5 0.0 copy-done
  123.5 1.9 convolution_bitcast_fusion
  125.4 0.0 copy-done.3
  125.4 1.0 pad_maximum_fusion.small_ref
  126.4 0.0 copy-start.2
  126.4 0.0 copy-start.6
  126.4 59.3 %shard_map.173 = (f32[512,512]{1,0:T(8,128)}, f32[512,512]{1,0:T(8,128)}, f32[512,256]{1,0:T(8,128)}) custom-call(f32[512,512]{1,0:T(8,128)} %get-tuple-element.29.first_ref, f32[512,512]{1,0:T(8,128)} %get-tuple-element.30.second_ref, f32[512,256]{1,0:T(8,128)} %pad_maximum_fusion.small_ref), custom_call_target="tpu_custom_call" | custom-call | tf_op jit(solution)/shard_map/pallas_call | solution.py:440
  185.7 1.3 slice.13
  187.0 1.4 slice.14
  188.4 1.2 slice_bitcast_fusion
  189.6 0.0 copy-done.2
  189.6 0.0 copy-done.6
  189.6 0.0 copy-start.5
  189.6 4.3 %fusion = bf16[1,2048,512]{2,1,0:T(8,128)(2,1)} fusion(f32[2048,512]{1,0:T(8,128)} %get-tuple-element.23, bf16[64,2048]{1,0:T(8,128)(2,1)S(1)} %copy-done.2, bf16[512,64]{0,1:T(8,128)(2,1)S(1)} %copy-done.6), kind=kOutput, calls=%fused_computation.1 | convolution fusion | flops 136314880 | bytes 6619136 | tf_op jit(solution)/shard_map/dot_general | solution.py:25
  193.9 0.0 copy-start.4
  193.9 0.8 copy.23
  194.7 0.8 copy.22
  195.5 0.0 copy-done.5
  195.5 1.0 copy.28
  196.4 0.0 copy-done.4
  196.4 1.0 copy.29
Async XLA Ops:
  75.4 12.8 %copy-start.7 = (f32[64,512]{1,0:T(8,128)S(1)}, f32[64,512]{1,0:T(8,128)}, u32[]{:S(2)}) copy-start(f32[64,512]{1,0:T(8,128)} %get-tuple-element.31) | copy-start | bytes 393220
  82.7 5.5 %copy-start.8 = (f32[16,64]{1,0:T(8,128)S(1)}, f32[16,64]{1,0:T(8,128)}, u32[]{:S(2)}) copy-start(f32[16,64]{1,0:T(8,128)} %get-tuple-element.33) | copy-start | bytes 12292
  82.7 40.7 %copy-start = (bf16[1,2048,512]{2,1,0:T(8,128)(2,1)S(1)}, bf16[1,2048,512]{2,1,0:T(8,128)(2,1)}, u32[]{:S(2)}) copy-start(bf16[1,2048,512]{2,1,0:T(8,128)(2,1)} %param.12) | copy-start | bytes 6291460
  82.8 33.5 %all-to-all-start = ((bf16[64,64,128]{2,1,0:T(8,128)(2,1)}), bf16[64,64,128]{2,1,0:T(8,128)(2,1)S(1)}, u32[]{:S(2)}, u32[]{:S(2)}) async-start(bf16[64,64,128]{2,1,0:T(8,128)(2,1)} %get-tuple-element.26), calls=%async_computation | async-start | bytes 2097152 | tf_op jit(solution)/shard_map/all_to_all | solution.py:495
  116.3 1.0 copy-start.1
  117.3 8.1 %copy-start.3 = (f32[512,128]{1,0:T(8,128)S(1)}, f32[512,128]{1,0:T(8,128)}, u32[]{:S(2)}) copy-start(f32[512,128]{1,0:T(8,128)} %select_maximum_fusion) | copy-start | bytes 786436
  126.4 63.2 %copy-start.2 = (bf16[64,2048]{1,0:T(8,128)(2,1)S(1)}, bf16[64,2048]{1,0:T(8,128)(2,1)}, u32[]{:S(2)}) copy-start(bf16[64,2048]{1,0:T(8,128)(2,1)} %shard_map.172) | copy-start | bytes 786436
  126.4 63.2 %copy-start.6 = (bf16[512,64]{0,1:T(8,128)(2,1)S(1)}, bf16[512,64]{0,1:T(8,128)(2,1)}, u32[]{:S(2)}) copy-start(bf16[512,64]{0,1:T(8,128)(2,1)} %param.18) | copy-start | bytes 196612
  189.6 5.9 %copy-start.5 = (f32[512,512]{1,0:T(8,128)S(1)}, f32[512,512]{1,0:T(8,128)}, u32[]{:S(2)}) copy-start(f32[512,512]{1,0:T(8,128)} %get-tuple-element.58) | copy-start | bytes 3145732
  193.9 2.5 %copy-start.4 = (f32[512,512]{1,0:T(8,128)S(1)}, f32[512,512]{1,0:T(8,128)}, u32[]{:S(2)}) copy-start(f32[512,512]{1,0:T(8,128)} %get-tuple-element.59) | copy-start | bytes 3145732

commit v3 on v2

--- a/solution.py
+++ b/solution.py
@@ -281,182 +281,265 @@
     )(edge_rows, cotangent, count, gathered, bilinear, up, first, second)
 
 
-def pair_of(ref, i):
-    return jnp.concatenate([ref[8 * i + a] for a in range(8)], axis=1).astype(F32)
-
-
-def back_kernel(table_ref, fetched_ref, basis_ref, index_ref, weight_ref, out_ref, grad_ref):
-    narrow = fetched_ref.shape[1]
-    table = table_ref[...]
-    width = index_ref.shape[2]
-    grad_ref[...] = jnp.zeros_like(grad_ref)
-
-    @pl.loop(0, index_ref.shape[0])
-    def _(i):
-        columns = pl.ds(pl.multiple_of(i * width, width), width)
-        basis = basis_ref[:, columns]
-        got = pick(table, index_ref[i], narrow)
-        back_coef = (got * pair_of(fetched_ref, i)).astype(BF16)
-        grad_ref[...] += contract(basis, back_coef, 1, 1)
-        back = (got * coef_of(weight_ref[...], basis)).astype(BF16)
-        for a in range(8):
-            out_ref[8 * i + a] = back[:, a * 128 : (a + 1) * 128]
-
-
-def return_kernel(returned_ref, index_ref, pre_ref, out_ref, acc_ref):
-    narrow = returned_ref.shape[1]
-    high = acc_ref.shape[0] // narrow
-    acc_ref[...] = jnp.zeros_like(acc_ref)
-
-    @pl.loop(0, index_ref.shape[0])
-    def _(i):
-        acc_ref[...] += spread(pair_of(returned_ref, i), index_ref[i], high)
+def backward_kernel(scale, table_ref, fetched_ref, basis_ref, index_ref, weight_ref, wanted_ref,
+                    pre_ref, edge_ref, summed_ref, down_ref, first_ref, second_ref, up_ref, bil_ref,
+                    edge_out, first_out, second_out, tail_out, corner_out,
+                    outbox, returned, acc, grad, back_pre,
+                    send_a, got_a, part_b, got_b, full_b, held,
+                    send_t, got_t, part_z, got_z, held_t,
+                    rs_sem, rr_sem, as_sem, ar_sem, bs_sem, br_sem, cs_sem, cr_sem, ds_sem, dr_sem,
+                    ts_sem, tr_sem, zs_sem, zr_sem, us_sem, ur_sem):
+    shards, narrow = fetched_ref.shape[:2]
+    wide = first_ref.shape[1]
+    high = table_ref.shape[0] // narrow
+    y, z, x, c = place()
+    g = lax.axis_index("graph")
+    chip = z * 4 + x
+    barrier = pltpu.get_barrier_semaphore()
+
+    def signal(device):
+        pl.semaphore_signal(barrier, inc=1, device_id=device, device_id_type=MESH)
+
+    @pl.loop(1, shards)
+    def _(j):
+        signal((y, (g + j) % shards))
+
+    @pl.loop(8, 32)
+    def _(j):
+        signal(((y + j // 8) % 4, z * 8 + (x + j // 2 % 4) % 4 * 2 + (c + j % 2) % 2))
+
+    mine8 = y * 2 + c
+
+    def member8(j):
+        py, pc = (y + j // 2) % 4, (c + j % 2) % 2
+        return (py, chip * 2 + pc), py * 2 + pc
+
+    def copy_a(j):
+        device, index = member8(j)
+        return pltpu.make_async_remote_copy(
+            src_ref=send_a.at[index], dst_ref=got_a.at[j], send_sem=as_sem.at[j],
+            recv_sem=ar_sem.at[j], device_id=device, device_id_type=MESH)
+
+    def to_chip(src, dst, send_sem, recv_sem, j, block):
+        q = (chip + j) % 32
+        return pltpu.make_async_remote_copy(
+            src_ref=src.at[q if block is None else block], dst_ref=dst.at[chip],
+            send_sem=send_sem.at[q], recv_sem=recv_sem.at[chip], device_id=(y, 2 * q + c),
+            device_id_type=MESH)
+
+    def from_chip(src, dst, send_sem, recv_sem, j):
+        q = (chip + j) % 32
+        return pltpu.make_async_remote_copy(
+            src_ref=src.at[0], dst_ref=dst.at[q], send_sem=send_sem.at[q],
+            recv_sem=recv_sem.at[q], device_id=(y, 2 * q + c), device_id_type=MESH)
+
+    def copy_d(j):
+        device, _ = member8(j)
+        return pltpu.make_async_remote_copy(
+            src_ref=full_b, dst_ref=held.at[mine8], send_sem=ds_sem.at[j],
+            recv_sem=dr_sem.at[j], device_id=device, device_id_type=MESH)
+
+    mine32 = y * 8 + x * 2 + c
+
+    def member32(j):
+        py, px, pc = (y + j // 8) % 4, (x + j // 2 % 4) % 4, (c + j % 2) % 2
+        return (py, z * 8 + px * 2 + pc), py * 8 + px * 2 + pc
+
+    def copy_t(j):
+        device, index = member32(j)
+        return pltpu.make_async_remote_copy(
+            src_ref=send_t.at[index], dst_ref=got_t.at[j], send_sem=ts_sem.at[j],
+            recv_sem=tr_sem.at[j], device_id=device, device_id_type=MESH)
+
+    def copy_z(j):
+        return pltpu.make_async_remote_copy(
+            src_ref=part_z, dst_ref=got_z.at[z], send_sem=zs_sem.at[j],
+            recv_sem=zr_sem.at[j], device_id=(y, (z + j) % 8 * 8 + x * 2 + c), device_id_type=MESH)
+
+    def copy_u(j):
+        device, _ = member32(j)
+        return pltpu.make_async_remote_copy(
+            src_ref=part_z, dst_ref=held_t.at[mine32], send_sem=us_sem.at[j],
+            recv_sem=ur_sem.at[j], device_id=device, device_id_type=MESH)
+
+    def each(count, fn):
+        @pl.loop(1, count)
+        def _(j):
+            fn(j)
+
+    rows8 = wide // 8
+    for m in range(8):
+        at = slice(m * rows8, (m + 1) * rows8)
+        send_a[m, :, :wide] = first_ref[at, :].astype(BF16)
+        send_a[m, :, wide:] = second_ref[at, :].astype(BF16)
+    acc[...] = jnp.zeros_like(acc)
+    grad[...] = jnp.zeros_like(grad)
+    send_t[...] = jnp.zeros_like(send_t)
+    pl.semaphore_wait(barrier, shards - 1 + 24)
+    each(8, lambda j: copy_a(j).start())
+    give, given = exchange(outbox, returned, rs_sem, rr_sem)
+
+    @pl.loop(0, 8)
+    def _(k):
+        basis = columns_of(basis_ref, k, 1)
+        got = pick(table_ref[...], row_of(index_ref, k, 1), narrow)
+        back_coef = (got * pairs_of(fetched_ref, k, 1).astype(F32)).astype(BF16)
+        grad[...] += contract(basis, back_coef, 1, 1)
+        put_pairs(outbox, k, 1, (got * coef_of(weight_ref[...], basis)).astype(BF16))
+        for a in range(4):
+            for_peers(k, a, 1, lambda p: give(p).start())
+
+    returned[g] = outbox[g]
+
+    def collect(k):
+        for a in range(4):
+            for_peers(k, a, -1, lambda p: given(p).wait_recv())
+        value = pairs_of(returned, k, -1).astype(F32)
+        acc[...] += spread(value, pairs_of(wanted_ref, k, -1), high)
+
+    pl.loop(0, 4)(collect)
+
+    got_a[0] = send_a[mine8]
+    each(8, lambda j: copy_a(j).wait_recv())
+
+    for r in range(4):
+        at = slice(r * 16, (r + 1) * 16)
+        total = got_a[0, at, :].astype(F32)
+        for j in range(1, 8):
+            total = total + got_a[j, at, :].astype(F32)
+        total = total.astype(BF16)
+        for s in range(8):
+            part_b[r * 8 + s] = total[:, s * 128 : (s + 1) * 128]
+    each(32, lambda j: to_chip(part_b, got_b, bs_sem, br_sem, j, None).start())
+
+    pl.loop(4, 8)(collect)
 
     for h in range(high):
         columns = slice(h * LOW, (h + 1) * LOW)
-        back = acc_ref[h * narrow : (h + 1) * narrow]
-        out_ref[:, columns] = (back * silu_slope(pre_ref[:, columns])).astype(BF16)
-
-
-def local_call(kernel, out_shape, *args, scratch=()):
+        back = acc[h * narrow : (h + 1) * narrow]
+        back_pre[:, columns] = (back * silu_slope(pre_ref[:, columns])).astype(BF16)
+    down = jnp.dot(back_pre[...], edge_ref[...], preferred_element_type=F32).astype(BF16)
+    ups = up_ref[...].astype(BF16)
+    for m in range(16):
+        at, columns = slice(m // 4 * 16, m // 4 * 16 + 16), slice(m % 4 * 128, m % 4 * 128 + 128)
+        send_t[m, :16] = down[at, columns]
+        send_t[16 + m, :16] = ups[at, columns]
+    for m in range(narrow // 16):
+        send_t[m, 16:, :narrow] = bil_ref[m * 16 : (m + 1) * 16, :].astype(BF16)
+    send_t[narrow // 16, 16:, :narrow] = grad[...].astype(BF16)
+    each(32, lambda j: copy_t(j).start())
+
+    got_b[chip] = part_b[chip]
+    each(32, lambda j: from_chip(part_b, got_b, bs_sem, br_sem, j).wait_recv())
+    total = got_b[0].astype(F32)
+    for j in range(1, 32):
+        total = total + got_b[j].astype(F32)
+    full_b[chip] = (total * scale).astype(BF16)
+    each(32, lambda j: to_chip(full_b, full_b, cs_sem, cr_sem, j, chip).start())
+
+    down_t = down_ref[...].T
+    steps = edge_ref.shape[0] // LOW
+
+    def finish(i):
+        at = pl.ds(pl.multiple_of(i * LOW, LOW), LOW)
+        add = contract(back_pre[:, at], down_t, 0, 0)
+        edge_out[at, :] = (summed_ref[at, :] + add).astype(BF16)
+
+    pl.loop(0, steps // 2)(finish)
+
+    got_t[0] = send_t[mine32]
+    each(32, lambda j: copy_t(j).wait_recv())
+    total = got_t[0].astype(F32)
+    for j in range(1, 32):
+        total = total + got_t[j].astype(F32)
+    part_z[...] = total.astype(BF16)
+    got_z[z] = total.astype(BF16)
+    each(8, lambda j: copy_z(j).start())
+
+    pl.loop(steps // 2, steps)(finish)
+
+    each(32, lambda j: from_chip(full_b, full_b, cs_sem, cr_sem, j).wait_recv())
+    each(8, lambda j: copy_d(j).start())
+    held[mine8] = full_b[...]
+
+    each(8, lambda j: copy_z(j).wait())
+    total = got_z[0].astype(F32)
+    for j in range(1, 8):
+        total = total + got_z[j].astype(F32)
+    total = (total * scale).astype(BF16)
+    part_z[...] = total
+    held_t[mine32] = total
+    each(32, lambda j: copy_u(j).start())
+
+    each(8, lambda j: copy_d(j).wait())
+
+    @pl.loop(0, 8)
+    def _(m):
+        for r in range(4):
+            at = pl.ds(pl.multiple_of(m * rows8 + r * 16, 16), 16)
+            for s in range(4):
+                columns = slice(s * 128, (s + 1) * 128)
+                first_out[at, columns] = held[m, r * 8 + s].astype(F32)
+                second_out[at, columns] = held[m, r * 8 + 4 + s].astype(F32)
+
+    each(32, lambda j: copy_u(j).wait())
+    for m in range(32):
+        at, columns = slice(m // 4 * 16, m // 4 * 16 + 16), slice(m % 4 * 128, m % 4 * 128 + 128)
+        tail_out[at, columns] = held_t[m, :16].astype(F32)
+    for m in range(5):
+        corner_out[m * 16 : (m + 1) * 16, :] = held_t[m, 16:].astype(F32)
+
+    each(shards, lambda j: give((g + j) % shards).wait_send())
+    each(8, lambda j: copy_a(j).wait_send())
+    each(32, lambda j: copy_t(j).wait_send())
+    each(32, lambda j: from_chip(part_b, got_b, bs_sem, br_sem, j).wait_send())
+    each(32, lambda j: from_chip(full_b, full_b, cs_sem, cr_sem, j).wait_send())
+
+
+def backward(scale, table, fetched, basis, out_index, basis_weight, wanted, pre_down, edge_rows,
+             back_summed, down_weight, first, second, up, bilinear):
+    shards, narrow, slots = fetched.shape
+    rows, wide = edge_rows.shape
+    dma = pltpu.SemaphoreType.DMA
+    shape = jax.ShapeDtypeStruct
+    vmem = pltpu.VMEM
     return pl.pallas_call(
-        kernel,
-        out_shape=out_shape,
-        in_specs=[VM] * len(args),
-        out_specs=jax.tree.map(lambda _: VM, out_shape),
-        scratch_shapes=list(scratch),
-        compiler_params=pltpu.CompilerParams(vmem_limit_bytes=VMEM_LIMIT),
-    )(*args)
-
-
-def reduce_kernel(scale, first_ref, second_ref, small_ref, first_out, second_out, small_out,
-                  send, got_a, part, got_b, held, sem_a, sem_ar, sem_b, sem_br, sem_c, sem_cr):
-    wide = first_ref.shape[1]
-    rows = send.shape[1]
-    group = send.shape[0]
-    depth = got_b.shape[0]
-    y = lax.axis_index("dp")
-    g = lax.axis_index("graph")
-    z, x, c = g // 8, (g // 2) % 4, g % 2
-    mine = y * 8 + x * 2 + c
-
-    def member(j):
-        py = (y + j // 8) % 4
-        px = (x + (j // 2) % 4) % 4
-        pc = (c + j % 2) % 2
-        return (py, z * 8 + px * 2 + pc), py * 8 + px * 2 + pc
-
-    def along(j):
-        pz = (z + j) % depth
-        return (y, pz * 8 + x * 2 + c)
-
-    barrier = pltpu.get_barrier_semaphore()
-
-    @pl.loop(1, group)
-    def _(j):
-        pl.semaphore_signal(barrier, inc=1, device_id=member(j)[0], device_id_type=MESH)
-
-    @pl.loop(1, depth)
-    def _(j):
-        pl.semaphore_signal(barrier, inc=1, device_id=along(j), device_id_type=MESH)
-
-    @pl.loop(0, group)
-    def _(m):
-        at = pl.ds(pl.multiple_of(m * rows, rows), rows)
-        send[m, :, :wide] = first_ref[at, :].astype(BF16)
-        send[m, :, wide : 2 * wide] = second_ref[at, :].astype(BF16)
-        send[m, :, 2 * wide :] = small_ref[at, :].astype(BF16)
-
-    pl.semaphore_wait(barrier, group - 1 + depth - 1)
-
-    def copy_a(j):
-        device, index = member(j)
-        return pltpu.make_async_remote_copy(
-            src_ref=send.at[index], dst_ref=got_a.at[j], send_sem=sem_a.at[j],
-            recv_sem=sem_ar.at[j], device_id=device, device_id_type=MESH)
-
-    def copy_b(j):
-        return pltpu.make_async_remote_copy(
-            src_ref=part, dst_ref=got_b.at[z], send_sem=sem_b.at[j],
-            recv_sem=sem_br.at[j], device_id=along(j), device_id_type=MESH)
-
-    def copy_c(j):
-        device, _ = member(j)
-        return pltpu.make_async_remote_copy(
-            src_ref=held.at[mine], dst_ref=held.at[mine], send_sem=sem_c.at[j],
-            recv_sem=sem_cr.at[j], device_id=device, device_id_type=MESH)
-
-    @pl.loop(1, group)
-    def _(j):
-        copy_a(j).start()
-
-    got_a[0] = send[mine]
-
-    @pl.loop(1, group)
-    def _(j):
-        copy_a(j).wait()
-
-    total = got_a[0].astype(F32)
-    for j in range(1, group):
-        total = total + got_a[j].astype(F32)
-    part[...] = total.astype(BF16)
-    got_b[z] = total.astype(BF16)
-
-    @pl.loop(1, depth)
-    def _(j):
-        copy_b(j).start()
-
-    @pl.loop(1, depth)
-    def _(j):
-        copy_b(j).wait()
-
-    total = got_b[0].astype(F32)
-    for j in range(1, depth):
-        total = total + got_b[j].astype(F32)
-    held[mine] = (total * scale).astype(BF16)
-
-    @pl.loop(1, group)
-    def _(j):
-        copy_c(j).start()
-
-    @pl.loop(1, group)
-    def _(j):
-        copy_c(j).wait()
-
-    @pl.loop(0, group)
-    def _(m):
-        at = pl.ds(pl.multiple_of(m * rows, rows), rows)
-        first_out[at, :] = held[m, :, :wide].astype(F32)
-        second_out[at, :] = held[m, :, wide : 2 * wide].astype(F32)
-        small_out[at, :] = held[m, :, 2 * wide :].astype(F32)
-
-
-def reduce_all(scale, first, second, small):
-    group, depth = 32, 8
-    rows = first.shape[0] // group
-    width = 2 * first.shape[1] + small.shape[1]
-    vmem = pl.BlockSpec(memory_space=pltpu.VMEM)
-    dma = pltpu.SemaphoreType.DMA
-    return pl.pallas_call(
-        functools.partial(reduce_kernel, scale),
+        functools.partial(backward_kernel, scale),
         out_shape=(
-            jax.ShapeDtypeStruct(first.shape, F32),
-            jax.ShapeDtypeStruct(second.shape, F32),
-            jax.ShapeDtypeStruct(small.shape, F32),
+            shape((rows, wide), BF16),
+            shape(first.shape, F32),
+            shape(second.shape, F32),
+            shape((2 * narrow, wide), F32),
+            shape((narrow + basis.shape[0], 128), F32),
         ),
-        in_specs=[vmem] * 3,
-        out_specs=(vmem,) * 3,
+        in_specs=[VM] * 14,
+        out_specs=(VM,) * 5,
         scratch_shapes=[
-            pltpu.VMEM((group, rows, width), BF16),
-            pltpu.VMEM((group, rows, width), BF16),
-            pltpu.VMEM((rows, width), BF16),
-            pltpu.VMEM((depth, rows, width), BF16),
-            pltpu.VMEM((group, rows, width), BF16),
-            dma((group,)), dma((group,)), dma((depth,)), dma((depth,)), dma((group,)), dma((group,)),
+            vmem((shards, narrow, slots), BF16),
+            vmem((shards, narrow, slots), BF16),
+            vmem((rows // LOW * narrow, LOW), F32),
+            vmem(basis_weight.shape, F32),
+            vmem((narrow, rows), BF16),
+            vmem((8, wide // 8, 2 * wide), BF16),
+            vmem((8, wide // 8, 2 * wide), BF16),
+            vmem((32, 16, 128), BF16),
+            vmem((32, 16, 128), BF16),
+            vmem((32, 16, 128), BF16),
+            vmem((8, 32, 16, 128), BF16),
+            vmem((32, 32, 128), BF16),
+            vmem((32, 32, 128), BF16),
+            vmem((32, 128), BF16),
+            vmem((8, 32, 128), BF16),
+            vmem((32, 32, 128), BF16),
+            dma((shards,)), dma((shards,)), dma((8,)), dma((8,)), dma((32,)), dma((32,)),
+            dma((32,)), dma((32,)), dma((8,)), dma((8,)), dma((32,)), dma((32,)),
+            dma((8,)), dma((8,)), dma((32,)), dma((32,)),
         ],
         compiler_params=pltpu.CompilerParams(
-            collective_id=0, has_side_effects=True, vmem_limit_bytes=VMEM_LIMIT),
-    )(first, second, small)
+            collective_id=2, has_side_effects=True, vmem_limit_bytes=VMEM_LIMIT),
+        name="backward_exchange",
+    )(table, fetched, basis, out_index, basis_weight, wanted, pre_down, edge_rows, back_summed,
+      down_weight, first, second, up, bilinear)
 
 
 def local(
@@ -477,7 +560,6 @@
     row_count, wide = edge_rows.shape
     shards = lax.axis_size("graph")
     narrow = down_weight.shape[1]
-    high = row_count // LOW
     tri_rows = triplet_in.shape[1]
     slot_count = tri_rows // shards
     basis = triplet_basis[0]
@@ -488,28 +570,16 @@
     back_summed, table, first_grad, second_grad, up_grad, bilinear_grad = dense(
         edge_rows, cotangent[0], edge_count, gathered, bilinear_weight, up_weight,
         first_weight, second_weight)
-    block = jax.ShapeDtypeStruct((shards, narrow, slot_count), BF16)
-    back_fetched, basis_grad = local_call(
-        back_kernel, (block, jax.ShapeDtypeStruct(basis_weight.shape, F32)),
-        table, fetched, basis, out_index.reshape(8, 1, 1024), basis_weight)
-    returned = lax.all_to_all(back_fetched, "graph", split_axis=0, concat_axis=0, tiled=True)
-    back_pre = local_call(
-        return_kernel, jax.ShapeDtypeStruct((narrow, row_count), BF16),
-        returned, wanted.reshape(8, 1, 1024), pre_down,
-        scratch=(pltpu.VMEM((high * narrow, LOW), F32),))
-    down_grad = contract(edge_rows, back_pre, 0, 1)
-    edge_grad = (back_summed + contract(back_pre, down_weight, 0, 1)).astype(jnp.bfloat16)
-    corner = jnp.concatenate([bilinear_grad, basis_grad], axis=0)
-    corner = jnp.pad(corner, ((0, wide - corner.shape[0]), (0, 128 - narrow)))
-    small = jnp.concatenate([down_grad, up_grad.T, corner], axis=1)
     grad_scale = 1.0 / math.sqrt(lax.axis_size("dp") * shards * row_count)
-    first_grad, second_grad, small = reduce_all(grad_scale, first_grad, second_grad, small)
+    edge_grad, first_grad, second_grad, tail, corner = backward(
+        grad_scale, table, fetched, basis, out_index, basis_weight, wanted, pre_down, edge_rows,
+        back_summed, down_weight, first_grad, second_grad, up_grad, bilinear_grad)
     return (
         edge_grad[None],
-        small[:, :narrow],
-        small[narrow : narrow + basis_weight.shape[0], 2 * narrow : 3 * narrow],
-        small[:narrow, 2 * narrow : 3 * narrow],
-        small[:, narrow : 2 * narrow].T,
+        tail[:narrow].T,
+        corner[narrow:, :narrow],
+        corner[:narrow, :narrow],
+        tail[narrow:],
         first_grad,
         second_grad,
     )

time: 198 us -> 158 us (0.80)
  waiting for transfers between devices: 26.5 us -> 0 us
  matrix products: 6.2 us -> 0 us
  starting transfers between devices: 5.36 us -> 0 us
  other arithmetic: 2.48 us -> 0 us
    all_to_all x1 -> x0, waiting for transfers between devices: 26.5 us -> none  [local(): lax.all_to_all(back_fetched, 'graph', split_axis=0, concat_axis=0, tiled=...]
    dot_general x2 -> x0, matrix products: 6.2 us -> none  [contract(): lax.dot_general(left, right, (((left_dim,), (right_dim,)), ((), ())), pre...]
    all_to_all x1 -> x0, starting transfers between devices: 5.36 us -> none  [local(): lax.all_to_all(back_fetched, 'graph', split_axis=0, concat_axis=0, tiled=...]
    concatenate x2 -> x0, other arithmetic: 2.48 us -> none  [the longest x1 1.48 us: local(): corner = jnp.concatenate([bilinear_grad, basis_grad], axis=0)]
    slice x2 -> x3, local copies, waits for them, and re-layouts: 2.67 us -> 4.35 us  [the longest x1 1.68 us: local(): tail[narrow:]]
    unnamed x23 -> x8, local copies, waits for them, and re-layouts: 6.08 us -> 7.31 us
    pallas_call x3 -> x1, Pallas kernels: 72.9 us -> 71.9 us  [backward(): pl.pallas_call(functools.partial(backward_kernel, scale), out_shape=(shap...]
  transfers between devices with their start and end apart: 1 -> 0, of which waited for: 1 -> 0; matrix products, arithmetic and copies ran while one was open for 1% -> 0% of each run, Pallas kernels for 0% -> 0%
where the time goes in v3:
time: 158 us; the launch traced here: 157 us
  Pallas kernels  144 us (91%)
  local copies, waits for them, and re-layouts  11.7 us (7%)
    pallas_call x1, Pallas kernels, backward(): pl.pallas_call(functools.partial(backward_kernel, scale), out_shape=(shap...  71.9 us
    pallas_call x1, Pallas kernels, forward(): pl.pallas_call(forward_kernel, out_shape=(jax.ShapeDtypeStruct((shards, n...  50.4 us
    pallas_call x1, Pallas kernels, dense(): pl.pallas_call(dense_kernel, out_shape=(shape((rows, wide), F32), shape((...  22.1 us
    unnamed x8, local copies, waits for them, and re-layouts  7.31 us

profile of v3, /device:TPU:1, one launch (start us, length us, event | category | flops | bytes accessed | tf_op | source)
XLA Modules:
  0.0 157.3 jit_solution(4922912279304026982)
XLA Ops:
  1.3 1.6 %copy.19.down_ref = bf16[512,64]{1,0:T(8,128)(2,1)} copy(bf16[512,64]{0,1:T(8,128)(2,1)} %param.18) | data formatting | bytes 131072 | tf_op args[6]
  2.9 50.4 %forward_exchange.1 = (bf16[64,64,128]{2,1,0:T(8,128)(2,1)}, s32[64,1,128]{2,1,0:T(1,128)}, f32[64,2048]{1,0:T(8,128)}, bf16[64,2048]{1,0:T(8,128)(2,1)}) custom-call(bf16[2048,512]{1,0:T(8,128)(2,1)} %bitcast.8, s32[64,1,128]{2,1,0:T(1,128)} %bitcast.17, s32[32,1,256]{2,1,0:T(1,128)} %bitcast.15, bf16[16,8192]{1,0:T(8,128)(2,1)} %bitcast.13, ...), custom_call_target="tpu_custom_call" | custom-call | tf_op jit(solution)/shard_map/forward_exchange/pallas_call | solution.py:196
  53.3 22.1 %dense.1 = (f32[2048,512]{1,0:T(8,128)}, bf16[512,256]{1,0:T(8,128)(2,1)}, f32[512,512]{1,0:T(8,128)}, f32[512,512]{1,0:T(8,128)}, f32[64,512]{1,0:T(8,128)}, /*index=5*/f32[64,64]{1,0:T(8,128)}) custom-call(bf16[2048,512]{1,0:T(8,128)(2,1)} %bitcast.9, bf16[2048,512]{1,0:T(8,128)(2,1)} %bitcast.11, s32[1,1]{1,0:T(1,128)S(6)} %copy.24.count_ref, ...), custom_call_target="tpu_custom_call" | custom-call | tf_op jit(solution)/shard_map/dense/pallas_call | solution.py:267
  75.4 71.9 %backward_exchange.1 = (bf16[2048,512]{1,0:T(8,128)(2,1)}, f32[512,512]{1,0:T(8,128)}, f32[512,512]{1,0:T(8,128)}, f32[128,512]{1,0:T(8,128)}, f32[80,128]{1,0:T(8,128)}) custom-call(bf16[512,256]{1,0:T(8,128)(2,1)} %get-tuple-element.23.table_ref, bf16[64,64,128]{2,1,0:T(8,128)(2,1)} %get-tuple-element.24.fetched_ref, bf16[16,8192]{1,0:T(8,128)(2,1)} %bitcast.14, ...), custom_call_target="tpu_custom_call" | custom-call | tf_op jit(solution)/shard_map/backward_exchange/pallas_call | solution.py:506
  147.2 1.3 slice.13
  148.5 1.4 slice.14
  149.9 1.7 %fusion = (f32[64,512]{1,0:T(8,128)}, f32[512,64]{0,1:T(8,128)}) fusion(f32[128,512]{1,0:T(8,128)} %get-tuple-element.33), kind=kLoop, calls=%fused_computation.1 | loop fusion | bytes 524288 | tf_op jit(solution)/shard_map/slice | solution.py:582
  151.6 0.0 copy-start.1
  151.6 3.1 %copy.25 = bf16[1,2048,512]{2,1,0:T(8,128)(2,1)} copy(bf16[1,2048,512]{2,1,0:T(8,128)(2,1)} %bitcast.12) | data formatting | bytes 4194304
  154.7 0.0 copy-done.1
  154.7 0.0 copy-start
  154.7 1.0 copy.26
  155.7 0.6 copy-done
  156.3 1.0 copy.27
Async XLA Ops:
  151.6 3.1 %copy-start.1 = (f32[512,512]{1,0:T(8,128)S(1)}, f32[512,512]{1,0:T(8,128)}, u32[]{:S(2)}) copy-start(f32[512,512]{1,0:T(8,128)} %get-tuple-element.51) | copy-start | bytes 3145732
  154.7 1.6 %copy-start = (f32[512,512]{1,0:T(8,128)S(1)}, f32[512,512]{1,0:T(8,128)}, u32[]{:S(2)}) copy-start(f32[512,512]{1,0:T(8,128)} %get-tuple-element.52) | copy-start | bytes 3145732

commit v4 on v0

v4 whole, which is shorter than its diff:
```python
import functools
import math

import jax
import jax.numpy as jnp
from jax import lax
from jax.experimental import pallas as pl
from jax.experimental.pallas import tpu as pltpu
from jax.sharding import PartitionSpec as P

HALF = 0.7071067811865476
LOW = 256
MESH = pl.DeviceIdType.MESH
F32 = jnp.float32
BF16 = jnp.bfloat16
VMEM_LIMIT = 60 * 1024 * 1024


def sigmoid(value):
    return 0.5 * jnp.tanh(0.5 * value) + 0.5


def slope_from(value, logistic):
    return logistic * (1.0 + value * (1.0 - logistic))


def contract(left, right, left_dim, right_dim):
    return lax.dot_general(
        left, right, (((left_dim,), (right_dim,)), ((), ())), preferred_element_type=jnp.float32
    )


def low_hot(low, width):
    rows = lax.broadcasted_iota(jnp.int32, (LOW, width), 0)
    return jnp.where(rows == low, 1.0, 0.0).astype(BF16)


def pick(table, index, narrow):
    width = index.shape[1]
    high = table.shape[0] // narrow
    hot = low_hot(index & (LOW - 1), width)
    upper = index >> 8
    wide = jnp.dot(table, hot, preferred_element_type=F32)
    out = wide[:narrow]
    for h in range(1, high):
        out = jnp.where(upper == h, wide[h * narrow : (h + 1) * narrow], out)
    return out


def spread(value, index, high):
    hot = low_hot(index & (LOW - 1), index.shape[1])
    upper = index >> 8
    parts = [jnp.where(upper == h, value, 0.0).astype(BF16) for h in range(high)]
    return contract(jnp.concatenate(parts, axis=0), hot, 1, 1)


def coef_of(weight, basis):
    return contract(weight, basis, 0, 0)


def place():
    g = lax.axis_index("graph")
    return lax.axis_index("dp"), g // 8, (g // 2) % 4, g % 2


def chip_at(k, a, sign):
    _, z, x, _ = place()
    dz, dx = (k + 2 * a) % 8, a
    if sign < 0:
        dz, dx = 8 - dz, 4 - dx
    return (z + dz) % 8 * 4 + (x + dx) % 4


def for_peers(k, a, sign, fn):
    q = chip_at(k, a, sign)
    if a:
        fn(2 * q)
        fn(2 * q + 1)
        return

    @pl.when(k > 0)
    def _():
        fn(2 * q)
        fn(2 * q + 1)

    @pl.when(k == 0)
    def _():
        g = lax.axis_index("graph")
        fn(g + 1 - 2 * (g % 2))


def row_of(ref, k, sign):
    return jnp.concatenate([ref[chip_at(k, a, sign)] for a in range(4)], axis=1)


def pairs_of(ref, k, sign):
    chips = [chip_at(k, a, sign) for a in range(4)]
    return jnp.concatenate([ref[2 * q + c] for q in chips for c in range(2)], axis=1)


def columns_of(ref, k, sign):
    chips = [chip_at(k, a, sign) for a in range(4)]
    return jnp.concatenate(
        [ref[:, pl.ds(pl.multiple_of(q * LOW, LOW), LOW)] for q in chips], axis=1)


def put_pairs(ref, k, sign, value):
    for a in range(4):
        q = chip_at(k, a, sign)
        for c in range(2):
            at = (2 * a + c) * 128
            ref[2 * q + c] = value[:, at : at + 128]


def exchange(src, dst, send_sem, recv_sem):
    y = lax.axis_index("dp")
    g = lax.axis_index("graph")

    def out(p):
        return pltpu.make_async_remote_copy(
            src_ref=src.at[p], dst_ref=dst.at[g], send_sem=send_sem.at[p],
            recv_sem=recv_sem.at[g], device_id=(y, p), device_id_type=MESH)

    def back(p):
        return pltpu.make_async_remote_copy(
            src_ref=src.at[p], dst_ref=dst.at[p], send_sem=send_sem.at[p],
            recv_sem=recv_sem.at[p], device_id=(y, p), device_id_type=MESH)

    return out, back


VM = pl.BlockSpec(memory_space=pltpu.VMEM)
HB = pl.BlockSpec(memory_space=pl.ANY)
DENSE = 512
TILE = 16


def each(count, fn):
    @pl.loop(1, count)
    def _(j):
        fn(j)


def total_of(ref, count):
    total = ref[0].astype(F32)
    for j in range(1, count):
        total = total + ref[j].astype(F32)
    return total


def plane_sum(send, got, part, got_z, held, sems, scale):
    y, z, x, c = place()
    mine = y * 8 + x * 2 + c
    ts_sem, tr_sem, zs_sem, zr_sem, us_sem, ur_sem = sems

    def member(j):
        py, px, pc = (y + j // 8) % 4, (x + j // 2 % 4) % 4, (c + j % 2) % 2
        return (py, z * 8 + px * 2 + pc), py * 8 + px * 2 + pc

    def copy_t(j):
        device, index = member(j)
        return pltpu.make_async_remote_copy(
            src_ref=send.at[index], dst_ref=got.at[j], send_sem=ts_sem.at[j],
            recv_sem=tr_sem.at[j], device_id=device, device_id_type=MESH)

    def copy_z(j):
        return pltpu.make_async_remote_copy(
            src_ref=part.at[0], dst_ref=got_z.at[z], send_sem=zs_sem.at[j],
            recv_sem=zr_sem.at[j], device_id=(y, (z + j) % 8 * 8 + x * 2 + c), device_id_type=MESH)

    def copy_u(j):
        device, _ = member(j)
        return pltpu.make_async_remote_copy(
            src_ref=part.at[1], dst_ref=held.at[mine], send_sem=us_sem.at[j],
            recv_sem=ur_sem.at[j], device_id=device, device_id_type=MESH)

    def start():
        each(32, lambda j: copy_t(j).start())

    def along():
        got[0] = send[mine]
        each(32, lambda j: copy_t(j).wait_recv())
        total = total_of(got, 32).astype(part.dtype)
        part[0] = total
        got_z[z] = total
        each(8, lambda j: copy_z(j).start())

    def share():
        each(8, lambda j: copy_z(j).wait_recv())
        total = (total_of(got_z, 8) * scale).astype(part.dtype)
        part[1] = total
        held[mine] = total
        each(32, lambda j: copy_u(j).start())

    def end():
        each(32, lambda j: copy_u(j).wait())
        each(32, lambda j: copy_t(j).wait_send())
        each(8, lambda j: copy_z(j).wait_send())

    return start, along, share, end


def main_kernel(scale, edge_ref, in_ref, down_ref, count_ref, weight_ref, bil_ref,
                cot_hbm, basis_hbm, index_hbm, up_hbm, w1_hbm, w2_hbm,
                edge_hbm, big_ref, early_ref, late_ref,
                cot_ref, basis_ref, index_ref, up_ref, w1_ref, w2_ref,
                fetched, wanted, pre_ref, table, outbox, acc, gathered,
                summed, half_s, back1_s, rows1_s, back2_s, backup_s, mixed_s, bil_grad, grad,
                outbox2, returned, back_pre, edge_out,
                send_a, got_p, pair_s, got_a, part_b, got_b, full_b,
                send_e, got_e, part_e, gotz_e, send_t, got_t, part_t, gotz_t,
                load_sem, save_sem, is_sem, ir_sem, rs_sem, rr_sem, qs_sem, qr_sem,
                ps_sem, as_sem, ar_sem, bs_sem, br_sem, cs_sem, cr_sem, ds_sem, dr_sem,
                *plane_sems):
    shards, narrow = fetched.shape[:2]
    rows, wide = edge_ref.shape
    high = rows // LOW
    y, z, x, c = place()
    g = lax.axis_index("graph")
    chip = z * 4 + x
    barrier = pltpu.get_barrier_semaphore()

    def signal(device):
        pl.semaphore_signal(barrier, inc=1, device_id=device, device_id_type=MESH)

    @pl.loop(1, shards)
    def _(j):
        signal((y, (g + j) % shards))

    @pl.loop(8, 32)
    def _(j):
        signal(((y + j // 8) % 4, z * 8 + (x + j // 2 % 4) % 4 * 2 + (c + j % 2) % 2))

    loads = [
        pltpu.make_async_copy(src, dst, load_sem.at[i])
        for i, (src, dst) in enumerate((
            (basis_hbm, basis_ref), (index_hbm, index_ref), (up_hbm, up_ref), (w1_hbm, w1_ref),
            (w2_hbm, w2_ref), (cot_hbm, cot_ref)))
    ]
    for load in loads:
        load.start()

    wanted[g] = in_ref[g]
    for h in range(high):
        pre = jnp.dot(edge_ref[h * LOW : (h + 1) * LOW], down_ref[...], preferred_element_type=F32)
        pre = pre.T
        pre_ref[:, h * LOW : (h + 1) * LOW] = pre
        table[h * narrow : (h + 1) * narrow] = (pre * sigmoid(pre)).astype(BF16)
    acc[...] = jnp.zeros_like(acc)
    grad[...] = jnp.zeros_like(grad)
    bil_grad[...] = jnp.zeros_like(bil_grad)
    send_e[...] = jnp.zeros_like(send_e)
    pl.semaphore_wait(barrier, shards - 1 + 24)
    ask, asked = exchange(in_ref, wanted, is_sem, ir_sem)
    give, given = exchange(outbox, fetched, rs_sem, rr_sem)

    @pl.loop(0, 8)
    def _(k):
        for a in range(4):
            for_peers(k, a, -1, lambda p: ask(p).start())

    @pl.loop(0, 8)
    def _(k):
        for a in range(4):
            for_peers(k, a, 1, lambda p: asked(p).wait_recv())
        index = pairs_of(wanted, k, 1)
        put_pairs(outbox, k, 1, pick(table[...], index, narrow).astype(BF16))
        for a in range(4):
            for_peers(k, a, 1, lambda p: give(p).start())

    fetched[g] = outbox[g]
    for load in loads:
        load.wait()

    @pl.loop(0, 8)
    def _(k):
        for a in range(4):
            for_peers(k, a, -1, lambda p: given(p).wait_recv())
        coef = coef_of(weight_ref[...], columns_of(basis_ref, k, -1))
        message = coef * pairs_of(fetched, k, -1).astype(F32)
        acc[...] += spread(message, row_of(index_ref, k, -1), high)

    for h in range(high):
        gathered[:, h * LOW : (h + 1) * LOW] = acc[h * narrow : (h + 1) * narrow].astype(BF16)
    acc[...] = jnp.zeros_like(acc)

    count = count_ref[0, 0]

    @pl.loop(0, rows // DENSE)
    def _(i):
        at = pl.ds(pl.multiple_of(i * DENSE, DENSE), DENSE)
        gat = gathered[:, at]
        mixed = contract(bil_ref[...], gat, 0, 0).astype(BF16)
        mixed_s[:, at] = mixed
        pre_up = contract(mixed, up_ref[...], 0, 0)
        s_up = sigmoid(pre_up)
        half = (edge_ref[at, :].astype(F32) + pre_up * s_up).astype(BF16)
        half_s[at, :] = half
        pre_first = jnp.dot(half, w1_ref[...], preferred_element_type=F32)
        s_first = sigmoid(pre_first)
        rows1 = (pre_first * s_first).astype(BF16)
        rows1_s[at, :] = rows1
        pre_second = jnp.dot(rows1, w2_ref[...], preferred_element_type=F32)
        live = lax.broadcasted_iota(jnp.int32, (DENSE, 1), 0) + i * DENSE < count
        top = cot_ref[at, :].astype(F32) * jnp.where(live, HALF, 0.0)
        back2 = (top * slope_from(pre_second, sigmoid(pre_second))).astype(BF16)
        back2_s[at, :] = back2
        back1 = contract(back2, w2_ref[...], 1, 1) * slope_from(pre_first, s_first)
        back1 = back1.astype(BF16)
        back1_s[at, :] = back1
        total = top + contract(back1, w1_ref[...], 1, 1)
        summed[at, :] = total
        back_up = (total * slope_from(pre_up, s_up)).astype(BF16)
        backup_s[at, :] = back_up
        back_mixed = contract(up_ref[...], back_up, 1, 1).astype(BF16)
        bil_grad[...] += contract(gat, back_mixed, 1, 1)
        turned = jnp.dot(bil_ref[...], back_mixed, preferred_element_type=F32).astype(BF16)
        for q in range(DENSE // LOW):
            where = pl.multiple_of((i * (DENSE // LOW) + q) * narrow, narrow)
            table[pl.ds(where, narrow), :] = turned[:, q * LOW : (q + 1) * LOW]

    bring, brought = exchange(outbox2, returned, qs_sem, qr_sem)

    @pl.loop(0, 8)
    def _(k):
        basis = columns_of(basis_ref, k, 1)
        got = pick(table[...], row_of(index_ref, k, 1), narrow)
        put_pairs(outbox2, k, 1, (got * coef_of(weight_ref[...], basis)).astype(BF16))
        for a in range(4):
            for_peers(k, a, 1, lambda p: bring(p).start())
        back_coef = (got * pairs_of(fetched, k, 1).astype(F32)).astype(BF16)
        grad[...] += contract(basis, back_coef, 1, 1)

    returned[g] = outbox2[g]

    def collect(k):
        for a in range(4):
            for_peers(k, a, -1, lambda p: brought(p).wait_recv())
        value = pairs_of(returned, k, -1).astype(F32)
        acc[...] += spread(value, pairs_of(wanted, k, -1), high)

    eighth = wide // 8

    def pair_copy(src, dst, at):
        return pltpu.make_async_remote_copy(
            src_ref=src, dst_ref=dst, send_sem=ps_sem.at[at], recv_sem=ps_sem.at[at + 1],
            device_id=(y, g + 1 - 2 * c), device_id_type=MESH)

    def copy_a(j):
        py = (y + j) % 4
        return pltpu.make_async_remote_copy(
            src_ref=pair_s.at[py], dst_ref=got_a.at[j], send_sem=as_sem.at[j],
            recv_sem=ar_sem.at[j], device_id=(py, g), device_id_type=MESH)

    def to_chip(src, dst, send_sem, recv_sem, j, block):
        q = (chip + j) % 32
        return pltpu.make_async_remote_copy(
            src_ref=src.at[q if block is None else block], dst_ref=dst.at[chip],
            send_sem=send_sem.at[q], recv_sem=recv_sem.at[chip], device_id=(y, 2 * q + c),
            device_id_type=MESH)

    def from_chip(src, dst, send_sem, recv_sem, j):
        q = (chip + j) % 32
        return pltpu.make_async_remote_copy(
            src_ref=src.at[0], dst_ref=dst.at[q], send_sem=send_sem.at[q],
            recv_sem=recv_sem.at[q], device_id=(y, 2 * q + c), device_id_type=MESH)

    def copy_d(j):
        return pltpu.make_async_remote_copy(
            src_ref=full_b, dst_ref=big_ref.at[c * 4 + y], send_sem=ds_sem.at[j],
            recv_sem=dr_sem.at[j], device_id=((y + j) % 4, g), device_id_type=MESH)

    second = contract(rows1_s[...], back2_s[...], 0, 0).astype(BF16)
    for m in range(8):
        send_a[m % 2, m // 2, :, wide:] = second[m * eighth : (m + 1) * eighth]
    first = contract(half_s[...], back1_s[...], 0, 0).astype(BF16)
    for m in range(8):
        send_a[m % 2, m // 2, :, :wide] = first[m * eighth : (m + 1) * eighth]
    pair_a = pair_copy(send_a.at[1 - c], got_p, 0)
    pair_a.start()

    early = plane_sum(send_e, got_e, part_e, gotz_e, early_ref, plane_sems[:6], scale)
    late = plane_sum(send_t, got_t, part_t, gotz_t, late_ref, plane_sems[6:], scale)
    ups = jnp.dot(mixed_s[...], backup_s[...], preferred_element_type=F32).astype(BF16)
    for m in range(16):
        send_e[m] = ups[m // 4 * 16 : m // 4 * 16 + 16, m % 4 * 128 : m % 4 * 128 + 128]
    for m in range(narrow // 16):
        send_e[16 + m, :, :narrow] = bil_grad[m * 16 : (m + 1) * 16, :].astype(BF16)
    send_e[16 + narrow // 16, :, :narrow] = grad[...].astype(BF16)
    early[0]()

    collect(0)
    pair_a.wait()
    for j in range(4):
        for r in range(4):
            at = slice(r * TILE, (r + 1) * TILE)
            pair_s[j, at] = (send_a[c, j, at].astype(F32) + got_p[j, at].astype(F32)).astype(BF16)
    each(4, lambda j: copy_a(j).start())
    pl.loop(1, 4)(collect)
    early[1]()
    pl.loop(4, 6)(collect)
    got_a[0] = pair_s[y]
    each(4, lambda j: copy_a(j).wait_recv())
    for r in range(4):
        at = slice(r * TILE, (r + 1) * TILE)
        total = got_a[0, at].astype(F32)
        for j in range(1, 4):
            total = total + got_a[j, at].astype(F32)
        total = total.astype(BF16)
        for s in range(8):
            part_b[r * 8 + s] = total[:, s * 128 : (s + 1) * 128]
    each(32, lambda j: to_chip(part_b, got_b, bs_sem, br_sem, j, None).start())
    early[2]()
    pl.loop(6, 8)(collect)

    for h in range(high):
        columns = slice(h * LOW, (h + 1) * LOW)
        pre = pre_ref[:, columns]
        back = acc[h * narrow : (h + 1) * narrow]
        back_pre[:, columns] = (back * slope_from(pre, sigmoid(pre))).astype(BF16)
    down = jnp.dot(back_pre[...], edge_ref[...], preferred_element_type=F32)
    for m in range(32):
        send_t[m] = down[m // 4 * 8 : m // 4 * 8 + 8, m % 4 * 128 : m % 4 * 128 + 128]
    late[0]()

    got_b[chip] = part_b[chip]
    each(32, lambda j: from_chip(part_b, got_b, bs_sem, br_sem, j).wait_recv())
    full_b[chip] = (total_of(got_b, 32) * scale).astype(BF16)
    each(32, lambda j: to_chip(full_b, full_b, cs_sem, cr_sem, j, chip).start())

    down_t = down_ref[...].T
    blocks = rows // DENSE

    def save(i):
        at = pl.ds(pl.multiple_of(i * DENSE, DENSE), DENSE)
        return pltpu.make_async_copy(edge_out.at[at], edge_hbm.at[at], save_sem.at[i])

    def finish(i):
        at = pl.ds(pl.multiple_of(i * DENSE, DENSE), DENSE)
        add = contract(back_pre[:, at], down_t, 0, 0)
        edge_out[at, :] = (summed[at, :] + add).astype(BF16)

    pl.loop(0, blocks // 2)(finish)
    late[1]()
    each(32, lambda j: from_chip(full_b, full_b, cs_sem, cr_sem, j).wait_recv())
    each(4, lambda j: copy_d(j).start())
    big_ref[c * 4 + y] = full_b[...]
    pl.loop(blocks // 2, blocks)(finish)
    pl.loop(0, blocks)(lambda i: save(i).start())
    late[2]()
    each(4, lambda j: copy_d(j).wait_recv())
    mine = pl.ds(c * 4, 4)
    pair_d = pair_copy(big_ref.at[mine], big_ref.at[mine], 2)
    pair_d.start()
    pl.loop(0, blocks)(lambda i: save(i).wait())

    @pl.loop(1, shards)
    def _(j):
        p = (g + j) % shards
        ask(p).wait_send()
        give(p).wait_send()
        bring(p).wait_send()

    each(4, lambda j: copy_a(j).wait_send())
    each(4, lambda j: copy_d(j).wait_send())
    each(32, lambda j: from_chip(part_b, got_b, bs_sem, br_sem, j).wait_send())
    each(32, lambda j: from_chip(full_b, full_b, cs_sem, cr_sem, j).wait_send())
    early[3]()
    late[3]()
    pair_d.wait()


def main(scale, edge_rows, in_index, down_weight, count, basis_weight, bilinear, cotangent, basis,
         out_index, up, first, second):
    shards, _, slots = in_index.shape
    rows, wide = edge_rows.shape
    narrow = down_weight.shape[1]
    high = rows // LOW
    d = pltpu.SemaphoreType.DMA
    shape = jax.ShapeDtypeStruct
    v = pltpu.VMEM
    block = (shards, narrow, slots)
    tiles = (32, TILE, 128)
    halves = (32, TILE // 2, 128)
    plane = [d((32,)), d((32,)), d((8,)), d((8,)), d((32,)), d((32,))]
    return pl.pallas_call(
        functools.partial(main_kernel, scale),
        out_shape=(
            shape((rows, wide), BF16),
            shape((8,) + tiles, BF16),
            shape(tiles, BF16),
            shape(halves, F32),
        ),
        in_specs=[VM, VM, VM, pl.BlockSpec(memory_space=pltpu.SMEM), VM, VM] + [HB] * 6,
        out_specs=(HB, VM, VM, VM),
        scratch_shapes=[
            v(cotangent.shape, BF16), v(basis.shape, BF16), v(out_index.shape, jnp.int32),
            v(up.shape, BF16), v(first.shape, BF16), v(second.shape, BF16),
            v(block, BF16), v(in_index.shape, jnp.int32), v((narrow, rows), F32),
            v((high * narrow, LOW), BF16), v(block, BF16), v((high * narrow, LOW), F32),
            v((narrow, rows), BF16),
            v((rows, wide), F32), v((rows, wide), BF16), v((rows, wide), BF16),
            v((rows, wide), BF16), v((rows, wide), BF16), v((rows, wide), BF16),
            v((narrow, rows), BF16), v((narrow, narrow), F32), v(basis_weight.shape, F32),
            v(block, BF16), v(block, BF16), v((narrow, rows), BF16), v((rows, wide), BF16),
            v((2, 4, wide // 8, 2 * wide), BF16), v((4, wide // 8, 2 * wide), BF16),
            v((4, wide // 8, 2 * wide), BF16), v((4, wide // 8, 2 * wide), BF16),
            v(tiles, BF16), v(tiles, BF16), v(tiles, BF16),
            v(tiles, BF16), v(tiles, BF16), v((2,) + tiles[1:], BF16), v((8,) + tiles[1:], BF16),
            v(halves, F32), v(halves, F32), v((2,) + halves[1:], F32), v((8,) + halves[1:], F32),
            d((6,)), d((rows // DENSE,)),
            d((shards,)), d((shards,)), d((shards,)), d((shards,)), d((shards,)), d((shards,)),
            d((4,)), d((4,)), d((4,)), d((32,)), d((32,)), d((32,)), d((32,)), d((4,)), d((4,)),
        ] + plane + plane,
        compiler_params=pltpu.CompilerParams(
            collective_id=1, has_side_effects=True, vmem_limit_bytes=VMEM_LIMIT),
        name="main",
    )(edge_rows, in_index, down_weight, count, basis_weight, bilinear, cotangent, basis, out_index,
      up, first, second)


def final_kernel(edge_ref, big_ref, early_ref, late_ref,
                 edge_out, first_out, second_out, down_out, basis_out, bil_out, up_out):
    edge_out[...] = edge_ref[...]
    for r in range(4):
        for s in range(4):
            at, columns = slice(r * 16, r * 16 + 16), slice(s * 128, s * 128 + 128)
            first_out[at, columns] = big_ref[0, r * 8 + s].astype(F32)
            second_out[at, columns] = big_ref[0, r * 8 + 4 + s].astype(F32)

    @pl.when(pl.program_id(0) == 0)
    def _():
        narrow = bil_out.shape[0]
        for s in range(4):
            column = jnp.concatenate([late_ref[r * 4 + s] for r in range(8)], axis=0)
            down_out[s * 128 : (s + 1) * 128, :] = column.T
        for m in range(16):
            up_out[m // 4 * 16 : m // 4 * 16 + 16, m % 4 * 128 : m % 4 * 128 + 128] = (
                early_ref[m].astype(F32))
        for m in range(narrow // 16):
            bil_out[m * 16 : (m + 1) * 16, :] = early_ref[16 + m].astype(F32)[:, :narrow]
        basis_out[...] = early_ref[16 + narrow // 16].astype(F32)[:, :narrow]


def final(edge, big, early, late, narrow, bases):
    rows, wide = edge.shape
    shape = jax.ShapeDtypeStruct

    def whole(s):
        return pl.BlockSpec(s, lambda i: (0,) * len(s))

    edge_spec = pl.BlockSpec((rows // 8, wide), lambda i: (i, 0))
    grad_spec = pl.BlockSpec((wide // 8, wide), lambda i: (i, 0))
    smalls = [(wide, narrow), (bases, narrow), (narrow, narrow), (narrow, wide)]
    return pl.pallas_call(
        final_kernel,
        grid=(8,),
        out_shape=(shape((rows, wide), BF16), shape((wide, wide), F32), shape((wide, wide), F32))
        + tuple(shape(s, F32) for s in smalls),
        in_specs=[
            edge_spec,
            pl.BlockSpec((1,) + big.shape[1:], lambda i: (i % 2 * 4 + i // 2, 0, 0, 0)),
            whole(early.shape), whole(late.shape)],
        out_specs=(edge_spec, grad_spec, grad_spec) + tuple(whole(s) for s in smalls),
        compiler_params=pltpu.CompilerParams(dimension_semantics=("arbitrary",)),
        name="final",
    )(edge, big, early, late)


def local(
    edge_state,
    cotangent,
    edge_count,
    triplet_basis,
    triplet_in,
    triplet_out,
    down_weight,
    basis_weight,
    bilinear_weight,
    up_weight,
    first_weight,
    second_weight,
):
    edge_rows = edge_state[0]
    row_count = edge_rows.shape[0]
    shards = lax.axis_size("graph")
    bases, narrow = basis_weight.shape
    tri_rows = triplet_in.shape[1]
    out_index = triplet_out[0].reshape(tri_rows // LOW, 1, LOW)
    in_index = triplet_in[0].reshape(shards, 1, tri_rows // shards)
    grad_scale = 1.0 / math.sqrt(lax.axis_size("dp") * shards * row_count)
    edge_grad, big, early, late = main(
        grad_scale, edge_rows, in_index, down_weight, edge_count, basis_weight, bilinear_weight,
        cotangent[0], triplet_basis[0], out_index, up_weight, first_weight, second_weight)
    edge_grad, first_grad, second_grad, down_grad, basis_grad, bilinear_grad, up_grad = final(
        edge_grad, big, early, late, narrow, bases)
    return edge_grad[None], down_grad, basis_grad, bilinear_grad, up_grad, first_grad, second_grad


def solution(mesh):
    in_specs = (
        P("dp", "graph", None),
        P("dp", "graph", None),
        P("dp", "graph"),
        P("dp", None, "graph"),
        P("dp", "graph"),
        P("dp", "graph"),
        P(),
        P(),
        P(),
        P(),
        P(),
        P(),
    )
    out_specs = (P("dp", "graph", None), P(), P(), P(), P(), P(), P())
    return jax.shard_map(local, mesh=mesh, in_specs=in_specs, out_specs=out_specs, check_vma=False)
```

time: 560 us -> 125 us (0.22)
  waiting for transfers between devices: 226 us -> 0 us
  Pallas kernels: 0 us -> 120 us
  other arithmetic: 107 us -> 0 us
  blocking collectives: 77.2 us -> 0 us
  local copies, waits for them, and re-layouts: 68.5 us -> 3.32 us
  matrix products: 38.2 us -> 0 us
  starting transfers between devices: 25.9 us -> 0 us
  between operations: 15 us -> 1.29 us
    psum x1 -> x0, waiting for transfers between devices: 175 us -> none  [local(): lax.psum((down_grad, basis_grad, bilinear_grad, up_grad, first_grad, seco...]
    pallas_call x0 -> x2, Pallas kernels: none -> 120 us  [the longest x1 113 us: main(): pl.pallas_call(functools.partial(main_kernel, scale), out_shape=(shape((r...]
    scatter-add x2 -> x0, other arithmetic: 89.9 us -> none  [the longest x1 45.3 us: local(): gathered = jnp.zeros((narrow, row_count), jnp.float32).at[:, out_local].a...]
    psum x1 -> x0, blocking collectives: 77.2 us -> none  [local(): lax.psum((down_grad, basis_grad, bilinear_grad, up_grad, first_grad, seco...]
    gather x4 -> x0, local copies, waits for them, and re-layouts: 57.3 us -> none  [the longest x2 31.7 us: local(): back_message = jnp.take(back_gathered, out_local, axis=1)]
    all_to_all x3 -> x0, waiting for transfers between devices: 51.9 us -> none  [the longest x1 27.5 us: local(): lax.all_to_all(served, 'graph', split_axis=1, concat_axis=1, tiled=True)]
    dot_general x17 -> x0, matrix products: 38.2 us -> none  [the longest x15 33.7 us: contract(): lax.dot_general(left, right, (((left_dim,), (right_dim,)), ((), ())), pre...]
    all_to_all x3 -> x0, starting transfers between devices: 25.6 us -> none  [the longest x1 13.1 us: local(): lax.all_to_all(in_local.reshape(shards, slot_count), 'graph', split_axis=...]
  transfers between devices with their start and end apart: 4 -> 0, of which waited for: 4 -> 0; matrix products, arithmetic and copies ran while one was open for 4% -> 0% of each run, Pallas kernels for 0% -> 0%
where the time goes in v4:
time: 125 us
  Pallas kernels  120 us (96%)
  local copies, waits for them, and re-layouts  3.32 us (3%)
  between operations  1.29 us (1%)
    pallas_call x1, Pallas kernels, main(): pl.pallas_call(functools.partial(main_kernel, scale), out_shape=(shape((r...  113 us
    pallas_call x1, Pallas kernels, final(): pl.pallas_call(final_kernel, grid=(8,), out_shape=(shape((rows, wide), BF...  6.71 us
    unnamed x2, local copies, waits for them, and re-layouts  3.32 us

profile of v4, /device:TPU:1, one launch (start us, length us, event | category | flops | bytes accessed | tf_op | source)
XLA Modules:
  0.0 124.5 jit_solution(12240248078086574437)
XLA Ops:
  1.3 1.6 %copy.19.down_ref = bf16[512,64]{1,0:T(8,128)(2,1)} copy(bf16[512,64]{0,1:T(8,128)(2,1)} %param.18) | data formatting | bytes 131072 | tf_op args[6]
  2.9 113.2 %main.1 = (bf16[2048,512]{1,0:T(8,128)(2,1)}, bf16[8,32,16,128]{3,2,1,0:T(8,128)(2,1)}, bf16[32,16,128]{2,1,0:T(8,128)(2,1)}, f32[32,8,128]{2,1,0:T(8,128)}) custom-call(bf16[2048,512]{1,0:T(8,128)(2,1)} %bitcast.6, s32[64,1,128]{2,1,0:T(1,128)} %bitcast.9, bf16[512,64]{1,0:T(8,128)(2,1)} %copy.19.down_ref, s32[1,1]{1,0:T(1,128)S(6)} %copy.21.count_ref, ...), custom_call_target="tpu_custom_call" | custom-call | tf_op jit(solution)/shard_map/main/pallas_call | solution.py:486
  116.1 6.7 %final.1 = (bf16[2048,512]{1,0:T(8,128)(2,1)}, f32[512,512]{1,0:T(8,128)}, f32[512,512]{1,0:T(8,128)}, f32[512,64]{1,0:T(8,128)}, f32[16,64]{1,0:T(8,128)}, /*index=5*/f32[64,64]{1,0:T(8,128)}, f32[64,512]{1,0:T(8,128)}) custom-call(bf16[2048,512]{1,0:T(8,128)(2,1)} %get-tuple-element.18.edge_ref, bf16[8,32,16,128]{3,2,1,0:T(8,128)(2,1)} %get-tuple-element.19.big_ref, ...), custom_call_target="tpu_custom_call" | custom-call | tf_op jit(solution)/shard_map/final/pallas_call | solution.py:555
  122.8 1.7 %copy.20 = f32[512,64]{0,1:T(8,128)} copy(f32[512,64]{1,0:T(8,128)} %get-tuple-element.30) | data formatting | bytes 262144

commit v5 on v4

--- a/solution.py
+++ b/solution.py
@@ -60,53 +60,58 @@
 
 def place():
     g = lax.axis_index("graph")
-    return lax.axis_index("dp"), g // 8, (g // 2) % 4, g % 2
-
-
-def chip_at(k, a, sign):
+    return lax.axis_index("dp"), lax.div(g, 8), lax.rem(lax.div(g, 2), 4), lax.rem(g, 2)
+
+
+def turns():
+    y, z, x, c = place()
+    return (
+        [y] + [lax.rem(y + d, 4) for d in range(1, 4)],
+        [z] + [lax.rem(z + d, 8) for d in range(1, 8)],
+        [x] + [lax.rem(x + d, 4) for d in range(1, 4)],
+        [c, 1 - c],
+    )
+
+
+def far(k):
+    odd = lax.rem(k, 2)
+    return 4 + lax.div(k, 2) * (1 - odd) - lax.div(k + 1, 2) * odd
+
+
+def chips_of(dz, sign):
     _, z, x, _ = place()
-    dz, dx = (k + 2 * a) % 8, a
-    if sign < 0:
-        dz, dx = 8 - dz, 4 - dx
-    return (z + dz) % 8 * 4 + (x + dx) % 4
-
-
-def for_peers(k, a, sign, fn):
-    q = chip_at(k, a, sign)
-    if a:
-        fn(2 * q)
-        fn(2 * q + 1)
-        return
-
-    @pl.when(k > 0)
-    def _():
-        fn(2 * q)
-        fn(2 * q + 1)
-
-    @pl.when(k == 0)
-    def _():
-        g = lax.axis_index("graph")
-        fn(g + 1 - 2 * (g % 2))
-
-
-def row_of(ref, k, sign):
-    return jnp.concatenate([ref[chip_at(k, a, sign)] for a in range(4)], axis=1)
-
-
-def pairs_of(ref, k, sign):
-    chips = [chip_at(k, a, sign) for a in range(4)]
-    return jnp.concatenate([ref[2 * q + c] for q in chips for c in range(2)], axis=1)
-
-
-def columns_of(ref, k, sign):
-    chips = [chip_at(k, a, sign) for a in range(4)]
+    own = isinstance(dz, int) and dz == 0
+    row = z if own else lax.rem(z + (dz if sign > 0 else 8 - dz), 8)
+    return [row * 4 + (lax.rem(x + (a if sign > 0 else 4 - a), 4) if a else x) for a in range(4)]
+
+
+def for_peers(dz, sign, fn):
+    own = isinstance(dz, int) and dz == 0
+    for a, q in enumerate(chips_of(dz, sign)):
+        if own and a == 0:
+            g = lax.axis_index("graph")
+            fn(g + 1 - 2 * lax.rem(g, 2))
+        else:
+            fn(2 * q)
+            fn(2 * q + 1)
+
+
+def row_of(ref, dz, sign):
+    return jnp.concatenate([ref[q] for q in chips_of(dz, sign)], axis=1)
+
+
+def pairs_of(ref, dz, sign):
     return jnp.concatenate(
-        [ref[:, pl.ds(pl.multiple_of(q * LOW, LOW), LOW)] for q in chips], axis=1)
-
-
-def put_pairs(ref, k, sign, value):
-    for a in range(4):
-        q = chip_at(k, a, sign)
+        [ref[2 * q + c] for q in chips_of(dz, sign) for c in range(2)], axis=1)
+
+
+def columns_of(ref, dz, sign):
+    return jnp.concatenate(
+        [ref[:, pl.ds(pl.multiple_of(q * LOW, LOW), LOW)] for q in chips_of(dz, sign)], axis=1)
+
+
+def put_pairs(ref, dz, sign, value):
+    for a, q in enumerate(chips_of(dz, sign)):
         for c in range(2):
             at = (2 * a + c) * 128
             ref[2 * q + c] = value[:, at : at + 128]
@@ -133,6 +138,11 @@
 HB = pl.BlockSpec(memory_space=pl.ANY)
 DENSE = 512
 TILE = 16
+
+
+FAR32 = sorted(range(1, 32), key=lambda j: -(2 - abs(j // 8 - 2)) - (2 - abs(j // 2 % 4 - 2)))
+
+FARCHIPS = sorted(range(1, 32), key=lambda j: -(4 - abs(j // 4 - 4)) - (2 - abs(j % 4 - 2)))
 
 
 def each(count, fn):
@@ -153,29 +163,33 @@
     mine = y * 8 + x * 2 + c
     ts_sem, tr_sem, zs_sem, zr_sem, us_sem, ur_sem = sems
 
+    ys, zs, xs, cs = turns()
+
     def member(j):
-        py, px, pc = (y + j // 8) % 4, (x + j // 2 % 4) % 4, (c + j % 2) % 2
+        py, px, pc = ys[j // 8], xs[j // 2 % 4], cs[j % 2]
         return (py, z * 8 + px * 2 + pc), py * 8 + px * 2 + pc
 
     def copy_t(j):
-        device, index = member(j)
+        device, index = member(j) if isinstance(j, int) else ((y, z * 8 + x * 2 + 1 - c), mine)
         return pltpu.make_async_remote_copy(
             src_ref=send.at[index], dst_ref=got.at[j], send_sem=ts_sem.at[j],
             recv_sem=tr_sem.at[j], device_id=device, device_id_type=MESH)
 
     def copy_z(j):
+        device = (y, zs[j] * 8 + x * 2 + c) if isinstance(j, int) else (y, z * 8 + x * 2 + 1 - c)
         return pltpu.make_async_remote_copy(
             src_ref=part.at[0], dst_ref=got_z.at[z], send_sem=zs_sem.at[j],
-            recv_sem=zr_sem.at[j], device_id=(y, (z + j) % 8 * 8 + x * 2 + c), device_id_type=MESH)
+            recv_sem=zr_sem.at[j], device_id=device, device_id_type=MESH)
 
     def copy_u(j):
-        device, _ = member(j)
+        device = member(j)[0] if isinstance(j, int) else (y, z * 8 + x * 2 + 1 - c)
         return pltpu.make_async_remote_copy(
             src_ref=part.at[1], dst_ref=held.at[mine], send_sem=us_sem.at[j],
             recv_sem=ur_sem.at[j], device_id=device, device_id_type=MESH)
 
     def start():
-        each(32, lambda j: copy_t(j).start())
+        for j in FAR32:
+            copy_t(j).start()
 
     def along():
         got[0] = send[mine]
@@ -183,14 +197,16 @@
         total = total_of(got, 32).astype(part.dtype)
         part[0] = total
         got_z[z] = total
-        each(8, lambda j: copy_z(j).start())
+        for j in (4, 3, 5, 2, 6, 1, 7):
+            copy_z(j).start()
 
     def share():
         each(8, lambda j: copy_z(j).wait_recv())
         total = (total_of(got_z, 8) * scale).astype(part.dtype)
         part[1] = total
         held[mine] = total
-        each(32, lambda j: copy_u(j).start())
+        for j in FAR32:
+            copy_u(j).start()
 
     def end():
         each(32, lambda j: copy_u(j).wait())
@@ -200,10 +216,10 @@
     return start, along, share, end
 
 
-def main_kernel(scale, edge_ref, in_ref, down_ref, count_ref, weight_ref, bil_ref,
-                cot_hbm, basis_hbm, index_hbm, up_hbm, w1_hbm, w2_hbm,
+def main_kernel(scale, in_ref, down_ref, count_ref, weight_ref, bil_ref,
+                edge_in, cot_hbm, basis_hbm, index_hbm, up_hbm, w1_hbm, w2_hbm,
                 edge_hbm, big_ref, early_ref, late_ref,
-                cot_ref, basis_ref, index_ref, up_ref, w1_ref, w2_ref,
+                edge_ref, cot_ref, basis_ref, index_ref, up_ref, w1_ref, w2_ref,
                 fetched, wanted, pre_ref, table, outbox, acc, gathered,
                 summed, half_s, back1_s, rows1_s, back2_s, backup_s, mixed_s, bil_grad, grad,
                 outbox2, returned, back_pre, edge_out,
@@ -223,27 +239,36 @@
     def signal(device):
         pl.semaphore_signal(barrier, inc=1, device_id=device, device_id_type=MESH)
 
-    @pl.loop(1, shards)
-    def _(j):
-        signal((y, (g + j) % shards))
-
-    @pl.loop(8, 32)
-    def _(j):
-        signal(((y + j // 8) % 4, z * 8 + (x + j // 2 % 4) % 4 * 2 + (c + j % 2) % 2))
-
+    ys, zs, xs, cs = turns()
+    for dz in (4, 3, 5, 2, 6, 1, 7, 0):
+        for j in range(8):
+            if dz or j:
+                signal((y, zs[dz] * 8 + xs[j // 2] * 2 + cs[j % 2]))
+    for j in range(8, 32):
+        signal((ys[j // 8], z * 8 + xs[j // 2 % 4] * 2 + cs[j % 2]))
+
+    parts = 4
+    span = rows // parts
+    edges = [
+        pltpu.make_async_copy(
+            edge_in.at[pl.ds(i * span, span)], edge_ref.at[pl.ds(i * span, span)],
+            load_sem.at[6 + i])
+        for i in range(parts)
+    ]
     loads = [
         pltpu.make_async_copy(src, dst, load_sem.at[i])
         for i, (src, dst) in enumerate((
             (basis_hbm, basis_ref), (index_hbm, index_ref), (up_hbm, up_ref), (w1_hbm, w1_ref),
             (w2_hbm, w2_ref), (cot_hbm, cot_ref)))
     ]
-    for load in loads:
+    for load in edges + loads:
         load.start()
 
     wanted[g] = in_ref[g]
     for h in range(high):
-        pre = jnp.dot(edge_ref[h * LOW : (h + 1) * LOW], down_ref[...], preferred_element_type=F32)
-        pre = pre.T
+        if h * LOW % span == 0:
+            edges[h * LOW // span].wait()
+        pre = contract(down_ref[...], edge_ref[h * LOW : (h + 1) * LOW], 1, 1)
         pre_ref[:, h * LOW : (h + 1) * LOW] = pre
         table[h * narrow : (h + 1) * narrow] = (pre * sigmoid(pre)).astype(BF16)
     acc[...] = jnp.zeros_like(acc)
@@ -254,31 +279,33 @@
     ask, asked = exchange(in_ref, wanted, is_sem, ir_sem)
     give, given = exchange(outbox, fetched, rs_sem, rr_sem)
 
-    @pl.loop(0, 8)
-    def _(k):
-        for a in range(4):
-            for_peers(k, a, -1, lambda p: ask(p).start())
-
-    @pl.loop(0, 8)
-    def _(k):
-        for a in range(4):
-            for_peers(k, a, 1, lambda p: asked(p).wait_recv())
-        index = pairs_of(wanted, k, 1)
-        put_pairs(outbox, k, 1, pick(table[...], index, narrow).astype(BF16))
-        for a in range(4):
-            for_peers(k, a, 1, lambda p: give(p).start())
-
+    for dz in (4, 3, 5, 2, 6, 1, 7, 0):
+        for j in range(8):
+            if dz or j:
+                ask(zs[dz] * 8 + xs[j // 2] * 2 + cs[j % 2]).start()
+
+    def serve(dz):
+        for_peers(dz, 1, lambda p: asked(p).wait_recv())
+        index = pairs_of(wanted, dz, 1)
+        put_pairs(outbox, dz, 1, pick(table[...], index, narrow).astype(BF16))
+        for_peers(dz, 1, lambda p: give(p).start())
+
+    pl.loop(0, 2)(lambda k: serve(1 + 6 * k))
+    pl.loop(0, 5)(lambda k: serve(far(k)))
+    serve(0)
     fetched[g] = outbox[g]
     for load in loads:
         load.wait()
 
-    @pl.loop(0, 8)
-    def _(k):
-        for a in range(4):
-            for_peers(k, a, -1, lambda p: given(p).wait_recv())
-        coef = coef_of(weight_ref[...], columns_of(basis_ref, k, -1))
-        message = coef * pairs_of(fetched, k, -1).astype(F32)
-        acc[...] += spread(message, row_of(index_ref, k, -1), high)
+    def gather(dz):
+        for_peers(dz, -1, lambda p: given(p).wait_recv())
+        coef = coef_of(weight_ref[...], columns_of(basis_ref, dz, -1))
+        message = coef * pairs_of(fetched, dz, -1).astype(F32)
+        acc[...] += spread(message, row_of(index_ref, dz, -1), high)
+
+    pl.loop(0, 2)(lambda k: gather(1 + 6 * k))
+    pl.loop(0, 5)(lambda k: gather(far(k)))
+    gather(0)
 
     for h in range(high):
         gathered[:, h * LOW : (h + 1) * LOW] = acc[h * narrow : (h + 1) * narrow].astype(BF16)
@@ -321,23 +348,18 @@
 
     bring, brought = exchange(outbox2, returned, qs_sem, qr_sem)
 
-    @pl.loop(0, 8)
-    def _(k):
-        basis = columns_of(basis_ref, k, 1)
-        got = pick(table[...], row_of(index_ref, k, 1), narrow)
-        put_pairs(outbox2, k, 1, (got * coef_of(weight_ref[...], basis)).astype(BF16))
-        for a in range(4):
-            for_peers(k, a, 1, lambda p: bring(p).start())
-        back_coef = (got * pairs_of(fetched, k, 1).astype(F32)).astype(BF16)
+    def answer(dz):
+        basis = columns_of(basis_ref, dz, 1)
+        got = pick(table[...], row_of(index_ref, dz, 1), narrow)
+        put_pairs(outbox2, dz, 1, (got * coef_of(weight_ref[...], basis)).astype(BF16))
+        for_peers(dz, 1, lambda p: bring(p).start())
+        back_coef = (got * pairs_of(fetched, dz, 1).astype(F32)).astype(BF16)
         grad[...] += contract(basis, back_coef, 1, 1)
 
-    returned[g] = outbox2[g]
-
-    def collect(k):
-        for a in range(4):
-            for_peers(k, a, -1, lambda p: brought(p).wait_recv())
-        value = pairs_of(returned, k, -1).astype(F32)
-        acc[...] += spread(value, pairs_of(wanted, k, -1), high)
+    def collect(dz):
+        for_peers(dz, -1, lambda p: brought(p).wait_recv())
+        value = pairs_of(returned, dz, -1).astype(F32)
+        acc[...] += spread(value, pairs_of(wanted, dz, -1), high)
 
     eighth = wide // 8
 
@@ -347,20 +369,20 @@
             device_id=(y, g + 1 - 2 * c), device_id_type=MESH)
 
     def copy_a(j):
-        py = (y + j) % 4
+        py = lax.rem(y + j, 4)
         return pltpu.make_async_remote_copy(
             src_ref=pair_s.at[py], dst_ref=got_a.at[j], send_sem=as_sem.at[j],
             recv_sem=ar_sem.at[j], device_id=(py, g), device_id_type=MESH)
 
     def to_chip(src, dst, send_sem, recv_sem, j, block):
-        q = (chip + j) % 32
+        q = zs[j // 4] * 4 + xs[j % 4]
         return pltpu.make_async_remote_copy(
             src_ref=src.at[q if block is None else block], dst_ref=dst.at[chip],
             send_sem=send_sem.at[q], recv_sem=recv_sem.at[chip], device_id=(y, 2 * q + c),
             device_id_type=MESH)
 
     def from_chip(src, dst, send_sem, recv_sem, j):
-        q = (chip + j) % 32
+        q = lax.rem(chip + j, 32)
         return pltpu.make_async_remote_copy(
             src_ref=src.at[0], dst_ref=dst.at[q], send_sem=send_sem.at[q],
             recv_sem=recv_sem.at[q], device_id=(y, 2 * q + c), device_id_type=MESH)
@@ -368,16 +390,22 @@
     def copy_d(j):
         return pltpu.make_async_remote_copy(
             src_ref=full_b, dst_ref=big_ref.at[c * 4 + y], send_sem=ds_sem.at[j],
-            recv_sem=dr_sem.at[j], device_id=((y + j) % 4, g), device_id_type=MESH)
-
-    second = contract(rows1_s[...], back2_s[...], 0, 0).astype(BF16)
-    for m in range(8):
-        send_a[m % 2, m // 2, :, wide:] = second[m * eighth : (m + 1) * eighth]
-    first = contract(half_s[...], back1_s[...], 0, 0).astype(BF16)
-    for m in range(8):
-        send_a[m % 2, m // 2, :, :wide] = first[m * eighth : (m + 1) * eighth]
+            recv_sem=dr_sem.at[j], device_id=(lax.rem(y + j, 4), g), device_id_type=MESH)
+
+    def store_grad(value, columns):
+        value = value.astype(BF16)
+        for m in range(8):
+            send_a[m % 2, m // 2, :, columns] = value[m * eighth : (m + 1) * eighth]
+
+    pl.loop(0, 2)(lambda k: answer(far(k)))
+    store_grad(contract(rows1_s[...], back2_s[...], 0, 0), slice(wide, 2 * wide))
+    pl.loop(2, 4)(lambda k: answer(far(k)))
+    store_grad(contract(half_s[...], back1_s[...], 0, 0), slice(0, wide))
     pair_a = pair_copy(send_a.at[1 - c], got_p, 0)
     pair_a.start()
+    pl.loop(4, 7)(lambda k: answer(far(k)))
+    answer(0)
+    returned[g] = outbox2[g]
 
     early = plane_sum(send_e, got_e, part_e, gotz_e, early_ref, plane_sems[:6], scale)
     late = plane_sum(send_t, got_t, part_t, gotz_t, late_ref, plane_sems[6:], scale)
@@ -389,16 +417,15 @@
     send_e[16 + narrow // 16, :, :narrow] = grad[...].astype(BF16)
     early[0]()
 
-    collect(0)
     pair_a.wait()
     for j in range(4):
         for r in range(4):
             at = slice(r * TILE, (r + 1) * TILE)
             pair_s[j, at] = (send_a[c, j, at].astype(F32) + got_p[j, at].astype(F32)).astype(BF16)
     each(4, lambda j: copy_a(j).start())
-    pl.loop(1, 4)(collect)
+    pl.loop(0, 4)(lambda k: collect(far(k)))
     early[1]()
-    pl.loop(4, 6)(collect)
+    collect(far(jnp.int32(4)))
     got_a[0] = pair_s[y]
     each(4, lambda j: copy_a(j).wait_recv())
     for r in range(4):
@@ -409,9 +436,11 @@
         total = total.astype(BF16)
         for s in range(8):
             part_b[r * 8 + s] = total[:, s * 128 : (s + 1) * 128]
-    each(32, lambda j: to_chip(part_b, got_b, bs_sem, br_sem, j, None).start())
+    for j in FARCHIPS:
+        to_chip(part_b, got_b, bs_sem, br_sem, j, None).start()
+    pl.loop(5, 7)(lambda k: collect(far(k)))
     early[2]()
-    pl.loop(6, 8)(collect)
+    collect(0)
 
     for h in range(high):
         columns = slice(h * LOW, (h + 1) * LOW)
@@ -426,9 +455,9 @@
     got_b[chip] = part_b[chip]
     each(32, lambda j: from_chip(part_b, got_b, bs_sem, br_sem, j).wait_recv())
     full_b[chip] = (total_of(got_b, 32) * scale).astype(BF16)
-    each(32, lambda j: to_chip(full_b, full_b, cs_sem, cr_sem, j, chip).start())
-
-    down_t = down_ref[...].T
+    for j in FARCHIPS:
+        to_chip(full_b, full_b, cs_sem, cr_sem, j, chip).start()
+
     blocks = rows // DENSE
 
     def save(i):
@@ -437,7 +466,7 @@
 
     def finish(i):
         at = pl.ds(pl.multiple_of(i * DENSE, DENSE), DENSE)
-        add = contract(back_pre[:, at], down_t, 0, 0)
+        add = contract(back_pre[:, at], down_ref[...], 0, 0)
         edge_out[at, :] = (summed[at, :] + add).astype(BF16)
 
     pl.loop(0, blocks // 2)(finish)
@@ -456,7 +485,7 @@
 
     @pl.loop(1, shards)
     def _(j):
-        p = (g + j) % shards
+        p = lax.rem(g + j, shards)
         ask(p).wait_send()
         give(p).wait_send()
         bring(p).wait_send()
@@ -474,7 +503,7 @@
          out_index, up, first, second):
     shards, _, slots = in_index.shape
     rows, wide = edge_rows.shape
-    narrow = down_weight.shape[1]
+    narrow = down_weight.shape[0]
     high = rows // LOW
     d = pltpu.SemaphoreType.DMA
     shape = jax.ShapeDtypeStruct
@@ -491,10 +520,10 @@
             shape(tiles, BF16),
             shape(halves, F32),
         ),
-        in_specs=[VM, VM, VM, pl.BlockSpec(memory_space=pltpu.SMEM), VM, VM] + [HB] * 6,
+        in_specs=[VM, VM, pl.BlockSpec(memory_space=pltpu.SMEM), VM, VM] + [HB] * 7,
         out_specs=(HB, VM, VM, VM),
         scratch_shapes=[
-            v(cotangent.shape, BF16), v(basis.shape, BF16), v(out_index.shape, jnp.int32),
+            v(edge_rows.shape, BF16), v(cotangent.shape, BF16), v(basis.shape, BF16), v(out_index.shape, jnp.int32),
             v(up.shape, BF16), v(first.shape, BF16), v(second.shape, BF16),
             v(block, BF16), v(in_index.shape, jnp.int32), v((narrow, rows), F32),
             v((high * narrow, LOW), BF16), v(block, BF16), v((high * narrow, LOW), F32),
@@ -508,61 +537,94 @@
             v(tiles, BF16), v(tiles, BF16), v(tiles, BF16),
             v(tiles, BF16), v(tiles, BF16), v((2,) + tiles[1:], BF16), v((8,) + tiles[1:], BF16),
             v(halves, F32), v(halves, F32), v((2,) + halves[1:], F32), v((8,) + halves[1:], F32),
-            d((6,)), d((rows // DENSE,)),
+            d((10,)), d((rows // DENSE,)),
             d((shards,)), d((shards,)), d((shards,)), d((shards,)), d((shards,)), d((shards,)),
             d((4,)), d((4,)), d((4,)), d((32,)), d((32,)), d((32,)), d((32,)), d((4,)), d((4,)),
         ] + plane + plane,
         compiler_params=pltpu.CompilerParams(
             collective_id=1, has_side_effects=True, vmem_limit_bytes=VMEM_LIMIT),
         name="main",
-    )(edge_rows, in_index, down_weight, count, basis_weight, bilinear, cotangent, basis, out_index,
+    )(in_index, down_weight, count, basis_weight, bilinear, edge_rows, cotangent, basis, out_index,
       up, first, second)
 
 
-def final_kernel(edge_ref, big_ref, early_ref, late_ref,
-                 edge_out, first_out, second_out, down_out, basis_out, bil_out, up_out):
-    edge_out[...] = edge_ref[...]
-    for r in range(4):
-        for s in range(4):
-            at, columns = slice(r * 16, r * 16 + 16), slice(s * 128, s * 128 + 128)
-            first_out[at, columns] = big_ref[0, r * 8 + s].astype(F32)
-            second_out[at, columns] = big_ref[0, r * 8 + 4 + s].astype(F32)
-
-    @pl.when(pl.program_id(0) == 0)
-    def _():
-        narrow = bil_out.shape[0]
-        for s in range(4):
-            column = jnp.concatenate([late_ref[r * 4 + s] for r in range(8)], axis=0)
-            down_out[s * 128 : (s + 1) * 128, :] = column.T
-        for m in range(16):
-            up_out[m // 4 * 16 : m // 4 * 16 + 16, m % 4 * 128 : m % 4 * 128 + 128] = (
-                early_ref[m].astype(F32))
-        for m in range(narrow // 16):
-            bil_out[m * 16 : (m + 1) * 16, :] = early_ref[16 + m].astype(F32)[:, :narrow]
-        basis_out[...] = early_ref[16 + narrow // 16].astype(F32)[:, :narrow]
+def final_kernel(edge_in, big_in, early_ref, late_ref,
+                 edge_out, first_out, second_out, down_out, basis_out, bil_out, up_out,
+                 edge_buf, big_buf, first_buf, second_buf, in_sem, out_sem, big_sem, grad_sem):
+    rows, wide = edge_buf.shape
+    parts = in_sem.shape[0]
+    span = rows // parts
+    narrow = bil_out.shape[0]
+
+    def big(m):
+        return pltpu.make_async_copy(big_in.at[m], big_buf.at[m], big_sem.at[m])
+
+    def piece(i):
+        at = pl.ds(i * span, span)
+        return (
+            pltpu.make_async_copy(edge_in.at[at], edge_buf.at[at], in_sem.at[i]),
+            pltpu.make_async_copy(edge_buf.at[at], edge_out.at[at], out_sem.at[i]),
+        )
+
+    def grads(i):
+        at = pl.ds(i * (wide // 2), wide // 2)
+        return (
+            pltpu.make_async_copy(first_buf.at[at], first_out.at[at], grad_sem.at[i]),
+            pltpu.make_async_copy(second_buf.at[at], second_out.at[at], grad_sem.at[2 + i]),
+        )
+
+    for m in range(8):
+        big(m % 2 * 4 + m // 2).start()
+    for i in range(parts):
+        piece(i)[0].start()
+    for s in range(4):
+        for r in range(8):
+            down_out[r * 8 : r * 8 + 8, s * 128 : s * 128 + 128] = late_ref[r * 4 + s]
+    for m in range(16):
+        up_out[m // 4 * 16 : m // 4 * 16 + 16, m % 4 * 128 : m % 4 * 128 + 128] = (
+            early_ref[m].astype(F32))
+    for m in range(narrow // 16):
+        bil_out[m * 16 : (m + 1) * 16, :] = early_ref[16 + m].astype(F32)[:, :narrow]
+    basis_out[...] = early_ref[16 + narrow // 16].astype(F32)[:, :narrow]
+    for m in range(8):
+        block = m % 2 * 4 + m // 2
+        big(block).wait()
+        for r in range(4):
+            at = slice(m * 64 + r * 16, m * 64 + r * 16 + 16)
+            for s in range(4):
+                columns = slice(s * 128, s * 128 + 128)
+                first_buf[at, columns] = big_buf[block, r * 8 + s].astype(F32)
+                second_buf[at, columns] = big_buf[block, r * 8 + 4 + s].astype(F32)
+        if m % 4 == 3:
+            for copy in grads(m // 4):
+                copy.start()
+    for i in range(parts):
+        piece(i)[0].wait()
+        piece(i)[1].start()
+    for i in range(parts):
+        piece(i)[1].wait()
+    for i in range(2):
+        for copy in grads(i):
+            copy.wait()
 
 
 def final(edge, big, early, late, narrow, bases):
     rows, wide = edge.shape
     shape = jax.ShapeDtypeStruct
-
-    def whole(s):
-        return pl.BlockSpec(s, lambda i: (0,) * len(s))
-
-    edge_spec = pl.BlockSpec((rows // 8, wide), lambda i: (i, 0))
-    grad_spec = pl.BlockSpec((wide // 8, wide), lambda i: (i, 0))
-    smalls = [(wide, narrow), (bases, narrow), (narrow, narrow), (narrow, wide)]
+    d = pltpu.SemaphoreType.DMA
+    smalls = [(narrow, wide), (bases, narrow), (narrow, narrow), (narrow, wide)]
     return pl.pallas_call(
         final_kernel,
-        grid=(8,),
         out_shape=(shape((rows, wide), BF16), shape((wide, wide), F32), shape((wide, wide), F32))
         + tuple(shape(s, F32) for s in smalls),
-        in_specs=[
-            edge_spec,
-            pl.BlockSpec((1,) + big.shape[1:], lambda i: (i % 2 * 4 + i // 2, 0, 0, 0)),
-            whole(early.shape), whole(late.shape)],
-        out_specs=(edge_spec, grad_spec, grad_spec) + tuple(whole(s) for s in smalls),
-        compiler_params=pltpu.CompilerParams(dimension_semantics=("arbitrary",)),
+        in_specs=[HB, HB, VM, VM],
+        out_specs=(HB, HB, HB) + (VM,) * 4,
+        scratch_shapes=[
+            pltpu.VMEM((rows, wide), BF16), pltpu.VMEM(big.shape, BF16),
+            pltpu.VMEM((wide, wide), F32), pltpu.VMEM((wide, wide), F32),
+            d((8,)), d((8,)), d((8,)), d((4,)),
+        ],
+        compiler_params=pltpu.CompilerParams(vmem_limit_bytes=VMEM_LIMIT),
         name="final",
     )(edge, big, early, late)
 
@@ -590,11 +652,11 @@
     in_index = triplet_in[0].reshape(shards, 1, tri_rows // shards)
     grad_scale = 1.0 / math.sqrt(lax.axis_size("dp") * shards * row_count)
     edge_grad, big, early, late = main(
-        grad_scale, edge_rows, in_index, down_weight, edge_count, basis_weight, bilinear_weight,
+        grad_scale, edge_rows, in_index, down_weight.T, edge_count, basis_weight, bilinear_weight,
         cotangent[0], triplet_basis[0], out_index, up_weight, first_weight, second_weight)
     edge_grad, first_grad, second_grad, down_grad, basis_grad, bilinear_grad, up_grad = final(
         edge_grad, big, early, late, narrow, bases)
-    return edge_grad[None], down_grad, basis_grad, bilinear_grad, up_grad, first_grad, second_grad
+    return edge_grad[None], down_grad.T, basis_grad, bilinear_grad, up_grad, first_grad, second_grad
 
 
 def solution(mesh):

time: 125 us -> 118 us (0.944)
  Pallas kernels: 120 us -> 116 us
  local copies, waits for them, and re-layouts: 3.32 us -> 0 us
    unnamed x2 -> x0, local copies, waits for them, and re-layouts: 3.32 us -> none
    pallas_call x1, Pallas kernels: 113 us -> 111 us  [main(): pl.pallas_call(functools.partial(main_kernel, scale), out_shape=(shape((r...]
    pallas_call x1, Pallas kernels: 6.71 us -> 5.38 us  [final(): pl.pallas_call(final_kernel, out_shape=(shape((rows, wide), BF16), shape(...]
where the time goes in v5:
time: 118 us
  Pallas kernels  116 us (98%)
  between operations  1.45 us (1%)
    pallas_call x1, Pallas kernels, main(): pl.pallas_call(functools.partial(main_kernel, scale), out_shape=(shape((r...  111 us
    pallas_call x1, Pallas kernels, final(): pl.pallas_call(final_kernel, out_shape=(shape((rows, wide), BF16), shape(...  5.38 us

profile of v5, /device:TPU:1, one launch (start us, length us, event | category | flops | bytes accessed | tf_op | source)
XLA Modules:
  0.0 117.9 jit_solution(1675109540930051318)
XLA Ops:
  1.3 111.1 %main.1 = (bf16[2048,512]{1,0:T(8,128)(2,1)}, bf16[8,32,16,128]{3,2,1,0:T(8,128)(2,1)}, bf16[32,16,128]{2,1,0:T(8,128)(2,1)}, f32[32,8,128]{2,1,0:T(8,128)}) custom-call(s32[64,1,128]{2,1,0:T(1,128)} %bitcast.12, bf16[64,512]{1,0:T(8,128)(2,1)} %bitcast.11, s32[1,1]{1,0:T(1,128)S(6)} %copy.19.count_ref, bf16[16,64]{1,0:T(8,128)(2,1)} %weight_ref.1, ...), custom_call_target="tpu_custom_call" | custom-call | tf_op jit(solution)/shard_map/main/pallas_call | solution.py:515
  112.4 5.4 %final.1 = (bf16[2048,512]{1,0:T(8,128)(2,1)}, f32[512,512]{1,0:T(8,128)}, f32[512,512]{1,0:T(8,128)}, f32[64,512]{1,0:T(8,128)}, f32[16,64]{1,0:T(8,128)}, /*index=5*/f32[64,64]{1,0:T(8,128)}, f32[64,512]{1,0:T(8,128)}) custom-call(bf16[2048,512]{1,0:T(8,128)(2,1)} %get-tuple-element.18.edge_in, bf16[8,32,16,128]{3,2,1,0:T(8,128)(2,1)} %get-tuple-element.19.big_in, ...), custom_call_target="tpu_custom_call" | custom-call | tf_op jit(solution)/shard_map/final/pallas_call | solution.py:616

commit v6 on v5

--- a/solution.py
+++ b/solution.py
@@ -74,21 +74,26 @@
 
 
 def far(k):
-    odd = lax.rem(k, 2)
-    return 4 + lax.div(k, 2) * (1 - odd) - lax.div(k + 1, 2) * odd
-
-
-def chips_of(dz, sign):
+    return 4 - lax.div(k + 1, 2), lax.rem(k + 1, 2)
+
+
+def chips_of(group, sign):
     _, z, x, _ = place()
-    own = isinstance(dz, int) and dz == 0
-    row = z if own else lax.rem(z + (dz if sign > 0 else 8 - dz), 8)
-    return [row * 4 + (lax.rem(x + (a if sign > 0 else 4 - a), 4) if a else x) for a in range(4)]
-
-
-def for_peers(dz, sign, fn):
-    own = isinstance(dz, int) and dz == 0
-    for a, q in enumerate(chips_of(dz, sign)):
-        if own and a == 0:
+    columns = [x] + [lax.rem(x + (a if sign > 0 else 4 - a), 4) for a in range(1, 4)]
+    if group is None:
+        return [z * 4 + q for q in columns]
+    distance, turn = group
+    ahead = distance + turn * (8 - 2 * distance)
+    back = 8 - ahead
+    rows = [lax.rem(z + (d if sign > 0 else 8 - d), 8) for d in (ahead, back)]
+    return [rows[a // 2] * 4 + columns[a] for a in range(4)]
+
+
+def for_peers(group, sign, fn):
+    chips = chips_of(group, sign)
+    for a in (0, 2, 1, 3):
+        q = chips[a]
+        if group is None and a == 0:
             g = lax.axis_index("graph")
             fn(g + 1 - 2 * lax.rem(g, 2))
         else:
@@ -96,22 +101,22 @@
             fn(2 * q + 1)
 
 
-def row_of(ref, dz, sign):
-    return jnp.concatenate([ref[q] for q in chips_of(dz, sign)], axis=1)
-
-
-def pairs_of(ref, dz, sign):
+def row_of(ref, group, sign):
+    return jnp.concatenate([ref[q] for q in chips_of(group, sign)], axis=1)
+
+
+def pairs_of(ref, group, sign):
     return jnp.concatenate(
-        [ref[2 * q + c] for q in chips_of(dz, sign) for c in range(2)], axis=1)
-
-
-def columns_of(ref, dz, sign):
+        [ref[2 * q + c] for q in chips_of(group, sign) for c in range(2)], axis=1)
+
+
+def columns_of(ref, group, sign):
     return jnp.concatenate(
-        [ref[:, pl.ds(pl.multiple_of(q * LOW, LOW), LOW)] for q in chips_of(dz, sign)], axis=1)
-
-
-def put_pairs(ref, dz, sign, value):
-    for a, q in enumerate(chips_of(dz, sign)):
+        [ref[:, pl.ds(pl.multiple_of(q * LOW, LOW), LOW)] for q in chips_of(group, sign)], axis=1)
+
+
+def put_pairs(ref, group, sign, value):
+    for a, q in enumerate(chips_of(group, sign)):
         for c in range(2):
             at = (2 * a + c) * 128
             ref[2 * q + c] = value[:, at : at + 128]
@@ -135,7 +140,7 @@
 
 
 VM = pl.BlockSpec(memory_space=pltpu.VMEM)
-HB = pl.BlockSpec(memory_space=pl.ANY)
+HB = pl.BlockSpec(memory_space=pltpu.HBM)
 DENSE = 512
 TILE = 16
 
@@ -218,14 +223,14 @@
 
 def main_kernel(scale, in_ref, down_ref, count_ref, weight_ref, bil_ref,
                 edge_in, cot_hbm, basis_hbm, index_hbm, up_hbm, w1_hbm, w2_hbm,
-                edge_hbm, big_ref, early_ref, late_ref,
+                edge_out, big_ref, early_ref, late_ref,
                 edge_ref, cot_ref, basis_ref, index_ref, up_ref, w1_ref, w2_ref,
                 fetched, wanted, pre_ref, table, outbox, acc, gathered,
                 summed, half_s, back1_s, rows1_s, back2_s, backup_s, mixed_s, bil_grad, grad,
-                outbox2, returned, back_pre, edge_out,
+                outbox2, returned, back_pre,
                 send_a, got_p, pair_s, got_a, part_b, got_b, full_b,
                 send_e, got_e, part_e, gotz_e, send_t, got_t, part_t, gotz_t,
-                load_sem, save_sem, is_sem, ir_sem, rs_sem, rr_sem, qs_sem, qr_sem,
+                load_sem, is_sem, ir_sem, rs_sem, rr_sem, qs_sem, qr_sem,
                 ps_sem, as_sem, ar_sem, bs_sem, br_sem, cs_sem, cr_sem, ds_sem, dr_sem,
                 *plane_sems):
     shards, narrow = fetched.shape[:2]
@@ -284,28 +289,28 @@
             if dz or j:
                 ask(zs[dz] * 8 + xs[j // 2] * 2 + cs[j % 2]).start()
 
-    def serve(dz):
-        for_peers(dz, 1, lambda p: asked(p).wait_recv())
-        index = pairs_of(wanted, dz, 1)
-        put_pairs(outbox, dz, 1, pick(table[...], index, narrow).astype(BF16))
-        for_peers(dz, 1, lambda p: give(p).start())
-
-    pl.loop(0, 2)(lambda k: serve(1 + 6 * k))
+    def serve(group):
+        for_peers(group, 1, lambda p: asked(p).wait_recv())
+        index = pairs_of(wanted, group, 1)
+        put_pairs(outbox, group, 1, pick(table[...], index, narrow).astype(BF16))
+        for_peers(group, 1, lambda p: give(p).start())
+
+    pl.loop(5, 7)(lambda k: serve(far(k)))
     pl.loop(0, 5)(lambda k: serve(far(k)))
-    serve(0)
+    serve(None)
     fetched[g] = outbox[g]
     for load in loads:
         load.wait()
 
-    def gather(dz):
-        for_peers(dz, -1, lambda p: given(p).wait_recv())
-        coef = coef_of(weight_ref[...], columns_of(basis_ref, dz, -1))
-        message = coef * pairs_of(fetched, dz, -1).astype(F32)
-        acc[...] += spread(message, row_of(index_ref, dz, -1), high)
-
-    pl.loop(0, 2)(lambda k: gather(1 + 6 * k))
+    def gather(group):
+        for_peers(group, -1, lambda p: given(p).wait_recv())
+        coef = coef_of(weight_ref[...], columns_of(basis_ref, group, -1))
+        message = coef * pairs_of(fetched, group, -1).astype(F32)
+        acc[...] += spread(message, row_of(index_ref, group, -1), high)
+
+    pl.loop(5, 7)(lambda k: gather(far(k)))
     pl.loop(0, 5)(lambda k: gather(far(k)))
-    gather(0)
+    gather(None)
 
     for h in range(high):
         gathered[:, h * LOW : (h + 1) * LOW] = acc[h * narrow : (h + 1) * narrow].astype(BF16)
@@ -348,18 +353,18 @@
 
     bring, brought = exchange(outbox2, returned, qs_sem, qr_sem)
 
-    def answer(dz):
-        basis = columns_of(basis_ref, dz, 1)
-        got = pick(table[...], row_of(index_ref, dz, 1), narrow)
-        put_pairs(outbox2, dz, 1, (got * coef_of(weight_ref[...], basis)).astype(BF16))
-        for_peers(dz, 1, lambda p: bring(p).start())
-        back_coef = (got * pairs_of(fetched, dz, 1).astype(F32)).astype(BF16)
+    def answer(group):
+        basis = columns_of(basis_ref, group, 1)
+        got = pick(table[...], row_of(index_ref, group, 1), narrow)
+        put_pairs(outbox2, group, 1, (got * coef_of(weight_ref[...], basis)).astype(BF16))
+        for_peers(group, 1, lambda p: bring(p).start())
+        back_coef = (got * pairs_of(fetched, group, 1).astype(F32)).astype(BF16)
         grad[...] += contract(basis, back_coef, 1, 1)
 
-    def collect(dz):
-        for_peers(dz, -1, lambda p: brought(p).wait_recv())
-        value = pairs_of(returned, dz, -1).astype(F32)
-        acc[...] += spread(value, pairs_of(wanted, dz, -1), high)
+    def collect(group):
+        for_peers(group, -1, lambda p: brought(p).wait_recv())
+        value = pairs_of(returned, group, -1).astype(F32)
+        acc[...] += spread(value, pairs_of(wanted, group, -1), high)
 
     eighth = wide // 8
 
@@ -404,7 +409,7 @@
     pair_a = pair_copy(send_a.at[1 - c], got_p, 0)
     pair_a.start()
     pl.loop(4, 7)(lambda k: answer(far(k)))
-    answer(0)
+    answer(None)
     returned[g] = outbox2[g]
 
     early = plane_sum(send_e, got_e, part_e, gotz_e, early_ref, plane_sems[:6], scale)
@@ -440,7 +445,7 @@
         to_chip(part_b, got_b, bs_sem, br_sem, j, None).start()
     pl.loop(5, 7)(lambda k: collect(far(k)))
     early[2]()
-    collect(0)
+    collect(None)
 
     for h in range(high):
         columns = slice(h * LOW, (h + 1) * LOW)
@@ -460,10 +465,6 @@
 
     blocks = rows // DENSE
 
-    def save(i):
-        at = pl.ds(pl.multiple_of(i * DENSE, DENSE), DENSE)
-        return pltpu.make_async_copy(edge_out.at[at], edge_hbm.at[at], save_sem.at[i])
-
     def finish(i):
         at = pl.ds(pl.multiple_of(i * DENSE, DENSE), DENSE)
         add = contract(back_pre[:, at], down_ref[...], 0, 0)
@@ -475,13 +476,11 @@
     each(4, lambda j: copy_d(j).start())
     big_ref[c * 4 + y] = full_b[...]
     pl.loop(blocks // 2, blocks)(finish)
-    pl.loop(0, blocks)(lambda i: save(i).start())
     late[2]()
     each(4, lambda j: copy_d(j).wait_recv())
     mine = pl.ds(c * 4, 4)
     pair_d = pair_copy(big_ref.at[mine], big_ref.at[mine], 2)
     pair_d.start()
-    pl.loop(0, blocks)(lambda i: save(i).wait())
 
     @pl.loop(1, shards)
     def _(j):
@@ -521,7 +520,7 @@
             shape(halves, F32),
         ),
         in_specs=[VM, VM, pl.BlockSpec(memory_space=pltpu.SMEM), VM, VM] + [HB] * 7,
-        out_specs=(HB, VM, VM, VM),
+        out_specs=(VM,) * 4,
         scratch_shapes=[
             v(edge_rows.shape, BF16), v(cotangent.shape, BF16), v(basis.shape, BF16), v(out_index.shape, jnp.int32),
             v(up.shape, BF16), v(first.shape, BF16), v(second.shape, BF16),
@@ -531,52 +530,52 @@
             v((rows, wide), F32), v((rows, wide), BF16), v((rows, wide), BF16),
             v((rows, wide), BF16), v((rows, wide), BF16), v((rows, wide), BF16),
             v((narrow, rows), BF16), v((narrow, narrow), F32), v(basis_weight.shape, F32),
-            v(block, BF16), v(block, BF16), v((narrow, rows), BF16), v((rows, wide), BF16),
+            v(block, BF16), v(block, BF16), v((narrow, rows), BF16),
             v((2, 4, wide // 8, 2 * wide), BF16), v((4, wide // 8, 2 * wide), BF16),
             v((4, wide // 8, 2 * wide), BF16), v((4, wide // 8, 2 * wide), BF16),
             v(tiles, BF16), v(tiles, BF16), v(tiles, BF16),
             v(tiles, BF16), v(tiles, BF16), v((2,) + tiles[1:], BF16), v((8,) + tiles[1:], BF16),
             v(halves, F32), v(halves, F32), v((2,) + halves[1:], F32), v((8,) + halves[1:], F32),
-            d((10,)), d((rows // DENSE,)),
+            d((10,)),
             d((shards,)), d((shards,)), d((shards,)), d((shards,)), d((shards,)), d((shards,)),
             d((4,)), d((4,)), d((4,)), d((32,)), d((32,)), d((32,)), d((32,)), d((4,)), d((4,)),
         ] + plane + plane,
         compiler_params=pltpu.CompilerParams(
-            collective_id=1, has_side_effects=True, vmem_limit_bytes=VMEM_LIMIT),
+            collective_id=1, has_side_effects=True, vmem_limit_bytes=48 * 1024 * 1024),
         name="main",
     )(in_index, down_weight, count, basis_weight, bilinear, edge_rows, cotangent, basis, out_index,
       up, first, second)
 
 
-def final_kernel(edge_in, big_in, early_ref, late_ref,
+def final_kernel(edge_ref, big_ref, early_ref, late_ref,
                  edge_out, first_out, second_out, down_out, basis_out, bil_out, up_out,
-                 edge_buf, big_buf, first_buf, second_buf, in_sem, out_sem, big_sem, grad_sem):
-    rows, wide = edge_buf.shape
-    parts = in_sem.shape[0]
+                 first_buf, second_buf, edge_sem, grad_sem):
+    rows, wide = edge_ref.shape
+    parts = edge_sem.shape[0]
     span = rows // parts
     narrow = bil_out.shape[0]
 
-    def big(m):
-        return pltpu.make_async_copy(big_in.at[m], big_buf.at[m], big_sem.at[m])
-
     def piece(i):
         at = pl.ds(i * span, span)
-        return (
-            pltpu.make_async_copy(edge_in.at[at], edge_buf.at[at], in_sem.at[i]),
-            pltpu.make_async_copy(edge_buf.at[at], edge_out.at[at], out_sem.at[i]),
-        )
-
-    def grads(i):
+        return pltpu.make_async_copy(edge_ref.at[at], edge_out.at[at], edge_sem.at[i])
+
+    def grads(i, buf, out, sem):
         at = pl.ds(i * (wide // 2), wide // 2)
-        return (
-            pltpu.make_async_copy(first_buf.at[at], first_out.at[at], grad_sem.at[i]),
-            pltpu.make_async_copy(second_buf.at[at], second_out.at[at], grad_sem.at[2 + i]),
-        )
-
+        return pltpu.make_async_copy(buf.at[at], out.at[at], grad_sem.at[sem])
+
+    for i in range(parts):
+        piece(i).start()
     for m in range(8):
-        big(m % 2 * 4 + m // 2).start()
-    for i in range(parts):
-        piece(i)[0].start()
+        block = m % 2 * 4 + m // 2
+        for r in range(4):
+            at = slice(m * 64 + r * 16, m * 64 + r * 16 + 16)
+            for s in range(4):
+                columns = slice(s * 128, s * 128 + 128)
+                first_buf[at, columns] = big_ref[block, r * 8 + s].astype(F32)
+                second_buf[at, columns] = big_ref[block, r * 8 + 4 + s].astype(F32)
+        if m % 4 == 3:
+            grads(m // 4, first_buf, first_out, m // 4).start()
+            grads(m // 4, second_buf, second_out, 2 + m // 4).start()
     for s in range(4):
         for r in range(8):
             down_out[r * 8 : r * 8 + 8, s * 128 : s * 128 + 128] = late_ref[r * 4 + s]
@@ -586,26 +585,11 @@
     for m in range(narrow // 16):
         bil_out[m * 16 : (m + 1) * 16, :] = early_ref[16 + m].astype(F32)[:, :narrow]
     basis_out[...] = early_ref[16 + narrow // 16].astype(F32)[:, :narrow]
-    for m in range(8):
-        block = m % 2 * 4 + m // 2
-        big(block).wait()
-        for r in range(4):
-            at = slice(m * 64 + r * 16, m * 64 + r * 16 + 16)
-            for s in range(4):
-                columns = slice(s * 128, s * 128 + 128)
-                first_buf[at, columns] = big_buf[block, r * 8 + s].astype(F32)
-                second_buf[at, columns] = big_buf[block, r * 8 + 4 + s].astype(F32)
-        if m % 4 == 3:
-            for copy in grads(m // 4):
-                copy.start()
+    for i in range(2):
+        grads(i, first_buf, first_out, i).wait()
+        grads(i, second_buf, second_out, 2 + i).wait()
     for i in range(parts):
-        piece(i)[0].wait()
-        piece(i)[1].start()
-    for i in range(parts):
-        piece(i)[1].wait()
-    for i in range(2):
-        for copy in grads(i):
-            copy.wait()
+        piece(i).wait()
 
 
 def final(edge, big, early, late, narrow, bases):
@@ -617,14 +601,12 @@
         final_kernel,
         out_shape=(shape((rows, wide), BF16), shape((wide, wide), F32), shape((wide, wide), F32))
         + tuple(shape(s, F32) for s in smalls),
-        in_specs=[HB, HB, VM, VM],
+        in_specs=[VM] * 4,
         out_specs=(HB, HB, HB) + (VM,) * 4,
         scratch_shapes=[
-            pltpu.VMEM((rows, wide), BF16), pltpu.VMEM(big.shape, BF16),
-            pltpu.VMEM((wide, wide), F32), pltpu.VMEM((wide, wide), F32),
-            d((8,)), d((8,)), d((8,)), d((4,)),
+            pltpu.VMEM((wide, wide), F32), pltpu.VMEM((wide, wide), F32), d((4,)), d((4,)),
         ],
-        compiler_params=pltpu.CompilerParams(vmem_limit_bytes=VMEM_LIMIT),
+        compiler_params=pltpu.CompilerParams(vmem_limit_bytes=12 * 1024 * 1024),
         name="final",
     )(edge, big, early, late)
 

time: 118 us -> 120 us (1.017)
  local copies, waits for them, and re-layouts: 0 us -> 7.62 us
  Pallas kernels: 116 us -> 111 us
    unnamed x0 -> x18, local copies, waits for them, and re-layouts: none -> 7.62 us
    pallas_call x1, Pallas kernels: 111 us -> 108 us  [main(): pl.pallas_call(functools.partial(main_kernel, scale), out_shape=(shape((r...]
    pallas_call x1, Pallas kernels: 5.38 us -> 2.79 us  [final(): pl.pallas_call(final_kernel, out_shape=(shape((rows, wide), BF16), shape(...]
where the time goes in v6:
time: 120 us
  Pallas kernels  111 us (92%)
  local copies, waits for them, and re-layouts  7.62 us (6%)
  between operations  1.47 us (1%)
    pallas_call x1, Pallas kernels, main(): pl.pallas_call(functools.partial(main_kernel, scale), out_shape=(shape((r...  108 us
    unnamed x18, local copies, waits for them, and re-layouts  7.62 us
    pallas_call x1, Pallas kernels, final(): pl.pallas_call(final_kernel, out_shape=(shape((rows, wide), BF16), shape(...  2.79 us

profile of v6, /device:TPU:1, one launch (start us, length us, event | category | flops | bytes accessed | tf_op | source)
XLA Modules:
  0.0 119.9 jit_solution(3561833476242625267)
XLA Ops:
  1.3 0.0 copy-start
  1.3 1.0 copy-done
  2.3 0.0 copy-start.1
  2.3 1.0 copy-done.1
  3.4 0.0 copy-start.2
  3.4 0.9 copy-done.2
  4.3 0.0 copy-start.3
  4.3 0.8 copy-done.3
  5.2 0.0 copy-start.4
  5.2 0.8 copy-done.4
  6.0 0.0 copy-start.5
  6.0 0.8 copy-done.5
  6.8 0.0 copy-start.6
  6.8 0.8 copy-done.6
  7.5 0.0 copy-start.7
  7.5 0.7 copy-done.7
  8.2 0.0 copy-start.8
  8.2 0.7 copy-done.8
  8.9 108.0 %main.1 = (bf16[2048,512]{1,0:T(8,128)(2,1)S(1)}, bf16[8,32,16,128]{3,2,1,0:T(8,128)(2,1)S(1)}, bf16[32,16,128]{2,1,0:T(8,128)(2,1)S(1)}, f32[32,8,128]{2,1,0:T(8,128)S(1)}) custom-call(s32[64,1,128]{2,1,0:T(1,128)S(1)} %bitcast.10, bf16[64,512]{1,0:T(8,128)(2,1)S(1)} %bitcast.9, s32[1,1]{1,0:T(1,128)S(6)} %copy.19.count_ref, bf16[16,64]{1,0:T(8,128)(2,1)S(1)} %copy-done.8, ...), custom_call_target="tpu_custom_call" | custom-call | tf_op jit(solution)/shard_map/main/pallas_call | solution.py:514
  117.0 2.8 %final.1 = (bf16[2048,512]{1,0:T(8,128)(2,1)}, f32[512,512]{1,0:T(8,128)}, f32[512,512]{1,0:T(8,128)}, f32[64,512]{1,0:T(8,128)}, f32[16,64]{1,0:T(8,128)}, /*index=5*/f32[64,64]{1,0:T(8,128)}, f32[64,512]{1,0:T(8,128)}) custom-call(bf16[2048,512]{1,0:T(8,128)(2,1)S(1)} %get-tuple-element.18.edge_ref, ...), custom_call_target="tpu_custom_call" | custom-call | tf_op jit(solution)/shard_map/final/pallas_call | solution.py:600
Async XLA Ops:
  1.3 1.0 copy-start
  2.3 1.0 copy-start.1
  3.4 0.9 copy-start.2
  4.3 0.8 copy-start.3
  5.2 0.8 copy-start.4
  6.0 0.8 copy-start.5
  6.8 0.8 copy-start.6
  7.5 0.7 copy-start.7
  8.2 0.7 copy-start.8

commit v7 on v6

--- a/solution.py
+++ b/solution.py
@@ -221,10 +221,9 @@
     return start, along, share, end
 
 
-def main_kernel(scale, in_ref, down_ref, count_ref, weight_ref, bil_ref,
-                edge_in, cot_hbm, basis_hbm, index_hbm, up_hbm, w1_hbm, w2_hbm,
+def main_kernel(scale, count_ref, in_hbm, down_hbm, weight_hbm, bil_hbm, edge_in, cot_hbm, basis_hbm, index_hbm, up_hbm, w1_hbm, w2_hbm,
                 edge_out, big_ref, early_ref, late_ref,
-                edge_ref, cot_ref, basis_ref, index_ref, up_ref, w1_ref, w2_ref,
+                in_ref, down_ref, weight_ref, bil_ref, edge_ref, cot_ref, basis_ref, index_ref, up_ref, w1_ref, w2_ref,
                 fetched, wanted, pre_ref, table, outbox, acc, gathered,
                 summed, half_s, back1_s, rows1_s, back2_s, backup_s, mixed_s, bil_grad, grad,
                 outbox2, returned, back_pre,
@@ -257,18 +256,24 @@
     edges = [
         pltpu.make_async_copy(
             edge_in.at[pl.ds(i * span, span)], edge_ref.at[pl.ds(i * span, span)],
-            load_sem.at[6 + i])
+            load_sem.at[8 + i])
         for i in range(parts)
     ]
     loads = [
         pltpu.make_async_copy(src, dst, load_sem.at[i])
         for i, (src, dst) in enumerate((
             (basis_hbm, basis_ref), (index_hbm, index_ref), (up_hbm, up_ref), (w1_hbm, w1_ref),
-            (w2_hbm, w2_ref), (cot_hbm, cot_ref)))
+            (w2_hbm, w2_ref), (cot_hbm, cot_ref), (weight_hbm, weight_ref), (bil_hbm, bil_ref)))
     ]
-    for load in edges + loads:
+    heads = [
+        pltpu.make_async_copy(in_hbm, in_ref, load_sem.at[12]),
+        pltpu.make_async_copy(down_hbm, down_ref, load_sem.at[13]),
+    ]
+    for load in heads + edges + loads:
         load.start()
 
+    for load in heads:
+        load.wait()
     wanted[g] = in_ref[g]
     for h in range(high):
         if h * LOW % span == 0:
@@ -519,10 +524,11 @@
             shape(tiles, BF16),
             shape(halves, F32),
         ),
-        in_specs=[VM, VM, pl.BlockSpec(memory_space=pltpu.SMEM), VM, VM] + [HB] * 7,
+        in_specs=[pl.BlockSpec(memory_space=pltpu.SMEM)] + [HB] * 11,
         out_specs=(VM,) * 4,
         scratch_shapes=[
-            v(edge_rows.shape, BF16), v(cotangent.shape, BF16), v(basis.shape, BF16), v(out_index.shape, jnp.int32),
+            v(in_index.shape, jnp.int32), v(down_weight.shape, BF16), v(basis_weight.shape, BF16),
+            v(bilinear.shape, BF16), v(edge_rows.shape, BF16), v(cotangent.shape, BF16), v(basis.shape, BF16), v(out_index.shape, jnp.int32),
             v(up.shape, BF16), v(first.shape, BF16), v(second.shape, BF16),
             v(block, BF16), v(in_index.shape, jnp.int32), v((narrow, rows), F32),
             v((high * narrow, LOW), BF16), v(block, BF16), v((high * narrow, LOW), F32),
@@ -536,15 +542,17 @@
             v(tiles, BF16), v(tiles, BF16), v(tiles, BF16),
             v(tiles, BF16), v(tiles, BF16), v((2,) + tiles[1:], BF16), v((8,) + tiles[1:], BF16),
             v(halves, F32), v(halves, F32), v((2,) + halves[1:], F32), v((8,) + halves[1:], F32),
-            d((10,)),
+            d((14,)),
             d((shards,)), d((shards,)), d((shards,)), d((shards,)), d((shards,)), d((shards,)),
             d((4,)), d((4,)), d((4,)), d((32,)), d((32,)), d((32,)), d((32,)), d((4,)), d((4,)),
         ] + plane + plane,
         compiler_params=pltpu.CompilerParams(
             collective_id=1, has_side_effects=True, vmem_limit_bytes=48 * 1024 * 1024),
         name="main",
-    )(in_index, down_weight, count, basis_weight, bilinear, edge_rows, cotangent, basis, out_index,
-      up, first, second)
+    )(count, *(
+        pltpu.with_memory_space_constraint(a, memory_space=pltpu.HBM)
+        for a in (in_index, down_weight, basis_weight, bilinear, edge_rows, cotangent, basis,
+                  out_index, up, first, second)))
 
 
 def final_kernel(edge_ref, big_ref, early_ref, late_ref,

time: 120 us -> 113 us (0.942)
  local copies, waits for them, and re-layouts: 7.62 us -> 0 us
    unnamed x18 -> x0, local copies, waits for them, and re-layouts: 7.62 us -> none
where the time goes in v7:
time: 113 us; the launch traced here: 112 us
  Pallas kernels  111 us (98%)
  between operations  1.45 us (1%)
    pallas_call x1, Pallas kernels, main(): pl.pallas_call(functools.partial(main_kernel, scale), out_shape=(shape((r...  108 us
    pallas_call x1, Pallas kernels, final(): pl.pallas_call(final_kernel, out_shape=(shape((rows, wide), BF16), shape(...  2.79 us

profile of v7, /device:TPU:1, one launch (start us, length us, event | category | flops | bytes accessed | tf_op | source)
XLA Modules:
  0.0 112.5 jit_solution(8706749214641216717)
XLA Ops:
  1.3 108.3 %main.1 = (bf16[2048,512]{1,0:T(8,128)(2,1)S(1)}, bf16[8,32,16,128]{3,2,1,0:T(8,128)(2,1)S(1)}, bf16[32,16,128]{2,1,0:T(8,128)(2,1)S(1)}, f32[32,8,128]{2,1,0:T(8,128)S(1)}) custom-call(s32[1,1]{1,0:T(1,128)S(6)} %copy.19.count_ref, s32[64,1,128]{2,1,0:T(1,128)} %bitcast.12, bf16[64,512]{1,0:T(8,128)(2,1)} %bitcast.11, bf16[16,64]{1,0:T(8,128)(2,1)} %weight_hbm.1, ...), custom_call_target="tpu_custom_call" | custom-call | tf_op jit(solution)/shard_map/main/pallas_call | solution.py:519
  109.5 2.8 %final.1 = (bf16[2048,512]{1,0:T(8,128)(2,1)}, f32[512,512]{1,0:T(8,128)}, f32[512,512]{1,0:T(8,128)}, f32[64,512]{1,0:T(8,128)}, f32[16,64]{1,0:T(8,128)}, /*index=5*/f32[64,64]{1,0:T(8,128)}, f32[64,512]{1,0:T(8,128)}) custom-call(bf16[2048,512]{1,0:T(8,128)(2,1)S(1)} %get-tuple-element.18.edge_ref, ...), custom_call_target="tpu_custom_call" | custom-call | tf_op jit(solution)/shard_map/final/pallas_call | solution.py:608

commit v8 on v7

--- a/solution.py
+++ b/solution.py
@@ -141,7 +141,7 @@
 
 VM = pl.BlockSpec(memory_space=pltpu.VMEM)
 HB = pl.BlockSpec(memory_space=pltpu.HBM)
-DENSE = 512
+DENSE = 1024
 TILE = 16
 
 
@@ -450,6 +450,11 @@
         to_chip(part_b, got_b, bs_sem, br_sem, j, None).start()
     pl.loop(5, 7)(lambda k: collect(far(k)))
     early[2]()
+    got_b[chip] = part_b[chip]
+    each(32, lambda j: from_chip(part_b, got_b, bs_sem, br_sem, j).wait_recv())
+    full_b[chip] = (total_of(got_b, 32) * scale).astype(BF16)
+    for j in FARCHIPS:
+        to_chip(full_b, full_b, cs_sem, cr_sem, j, chip).start()
     collect(None)
 
     for h in range(high):
@@ -461,12 +466,6 @@
     for m in range(32):
         send_t[m] = down[m // 4 * 8 : m // 4 * 8 + 8, m % 4 * 128 : m % 4 * 128 + 128]
     late[0]()
-
-    got_b[chip] = part_b[chip]
-    each(32, lambda j: from_chip(part_b, got_b, bs_sem, br_sem, j).wait_recv())
-    full_b[chip] = (total_of(got_b, 32) * scale).astype(BF16)
-    for j in FARCHIPS:
-        to_chip(full_b, full_b, cs_sem, cr_sem, j, chip).start()
 
     blocks = rows // DENSE
 

time: 113 us -> 114 us (level)
    pallas_call x1, Pallas kernels: 108 us -> 110 us  [main(): pl.pallas_call(functools.partial(main_kernel, scale), out_shape=(shape((r...]
where the time goes in v8:
time: 114 us
  Pallas kernels  112 us (98%)
  between operations  1.45 us (1%)
    pallas_call x1, Pallas kernels, main(): pl.pallas_call(functools.partial(main_kernel, scale), out_shape=(shape((r...  110 us
    pallas_call x1, Pallas kernels, final(): pl.pallas_call(final_kernel, out_shape=(shape((rows, wide), BF16), shape(...  2.79 us

profile of v8, /device:TPU:1, one launch (start us, length us, event | category | flops | bytes accessed | tf_op | source)
XLA Modules:
  0.0 113.9 jit_solution(669034708374768012)
XLA Ops:
  1.3 109.7 %main.1 = (bf16[2048,512]{1,0:T(8,128)(2,1)S(1)}, bf16[8,32,16,128]{3,2,1,0:T(8,128)(2,1)S(1)}, bf16[32,16,128]{2,1,0:T(8,128)(2,1)S(1)}, f32[32,8,128]{2,1,0:T(8,128)S(1)}) custom-call(s32[1,1]{1,0:T(1,128)S(6)} %copy.19.count_ref, s32[64,1,128]{2,1,0:T(1,128)} %bitcast.12, bf16[64,512]{1,0:T(8,128)(2,1)} %bitcast.11, bf16[16,64]{1,0:T(8,128)(2,1)} %weight_hbm.1, ...), custom_call_target="tpu_custom_call" | custom-call | tf_op jit(solution)/shard_map/main/pallas_call | solution.py:518
  111.0 2.8 %final.1 = (bf16[2048,512]{1,0:T(8,128)(2,1)}, f32[512,512]{1,0:T(8,128)}, f32[512,512]{1,0:T(8,128)}, f32[64,512]{1,0:T(8,128)}, f32[16,64]{1,0:T(8,128)}, /*index=5*/f32[64,64]{1,0:T(8,128)}, f32[64,512]{1,0:T(8,128)}) custom-call(bf16[2048,512]{1,0:T(8,128)(2,1)S(1)} %get-tuple-element.18.edge_ref, ...), custom_call_target="tpu_custom_call" | custom-call | tf_op jit(solution)/shard_map/final/pallas_call | solution.py:607
